TPU v7x, 256 devices: a whole 4x4x8 slice. The times are simulated.
256 devices in a mesh: group: 8 (over z_hi, core), tensor: 8 (over y, z_lo), seq: 4 (over x).
Axes of the slice: x: 4, y: 4, z: 8 (z_hi: 4, z_lo: 2; z = z_hi * 2 + z_lo), core: 2. Of those that a mesh axis runs over, the one named last changes fastest.
Arguments:
- patches: bfloat16 [8192, 1280], P(('group', 'tensor', 'seq')), may hold values from -6 to 6
- enc_gain: float32 [1280], replicated, may hold values from 0.1 to 1.9
- enc_qkv: bfloat16 [3, 1280, 1280], P(None, None, 'tensor')
- enc_out: bfloat16 [1280, 1280], P('tensor'), may hold values from -0.15625 to 0.15625
- cross_kv: bfloat16 [1280, 2048], P(None, 'tensor'), may hold values from -0.15625 to 0.15625
- key_gain: float32 [128], replicated, may hold values from 0.1 to 1.9
- dec_hidden: bfloat16 [4096, 8192], P(('group', 'seq')), may hold values from -6 to 6
- dec_gain: float32 [8192], replicated, may hold values from 0.1 to 1.9
- query_weight: bfloat16 [8192, 4096], P(None, 'tensor'), may hold values from -0.0625 to 0.0625
- query_gain: float32 [128], replicated, may hold values from 1.5 to 3
- image_of_row: int32 [4096], P(('group', 'seq')), may hold values from 0 to 3
- valid_count: int32 [4096], P(('group', 'seq')), may hold values from 1 to 2048, as said below
Outputs:
- decoded: bfloat16 [4096, 4096], P(('group', 'seq'), 'tensor')
Inputs may be any that keep to these rules, and one draw needn't show every extreme that they name: `valid_count`: every draw has a row reading a whole image and a row reading one patch.
All inputs are finite; a program needn't handle non-finite values.
Results may differ from a plain program's by a relative error of at most 0.028.
The roundings to bfloat16 on the way count: a program that leaves them out, or rounds other values in their place, can miss the bound.
Values may be sent and summed in bfloat16 or wider, within the bound.
No kernel may reach another device: no remote copies, remote signals or barrier semaphores. Data moves between devices by JAX's collectives and lax.ppermute only.
A program may use at most 128 MiB of HBM per device.

v0:
```python
import math

import jax
import jax.numpy as jnp
from jax import lax
from jax.experimental import pallas as pl
from jax.experimental.pallas import tpu as pltpu
from jax.sharding import Mesh
from jax.sharding import PartitionSpec as P

EHD = 80
HD = 128
EPSILON = 1e-05
F32 = jnp.float32
BF16 = jnp.bfloat16
ZH, CORES, YS, ZL, XS = 4, 2, 4, 2, 4
TENSOR = YS * ZL
NT = (((1,), (1,)), ((), ()))


def rms_norm(values, gain_vector):
    square_mean = jnp.mean(values * values, axis=-1, keepdims=True)
    return values * lax.rsqrt(square_mean + EPSILON) * gain_vector


def vmem(count):
    return [pl.BlockSpec(memory_space=pltpu.VMEM)] * count


def smem():
    return pl.BlockSpec(memory_space=pltpu.SMEM)


def xor_permute(values, axes, size, step):
    return lax.ppermute(values, axes, [(i, i ^ step) for i in range(size)])


def image_permute(values):
    pairs = []
    for zh in range(ZH):
        for y in range(YS):
            for zl in range(ZL):
                image, slot = (y % 2) * 2 + zl, zh * 2 + y // 2
                pairs.append(((zh * YS + y) * ZL + zl, image * TENSOR + slot))
    return lax.ppermute(values, ("zh", "y", "zl"), pairs)


def qkv_kernel(me_ref, *refs):
    pieces, (gain_ref, weight_ref, q_ref, kv_ref, normed) = refs[:TENSOR], refs[TENSOR:]
    me = me_ref[0]
    for step in range(TENSOR):
        values = pieces[step][...].astype(F32)
        mean_value = jnp.mean(values, axis=-1, keepdims=True)
        centered = values - mean_value
        variance = jnp.mean(centered * centered, axis=-1, keepdims=True)
        result = centered * lax.rsqrt(variance + EPSILON) * gain_ref[...]
        rows = values.shape[0]
        slot = jnp.bitwise_xor(me, step)
        normed[pl.ds(pl.multiple_of(slot * rows, rows), rows), :] = result.astype(BF16)
    x = normed[...]
    q = lax.dot_general(x, weight_ref[0], NT, preferred_element_type=F32)
    for head in range(2):
        q_ref[head] = q[:, head * EHD : (head + 1) * EHD].astype(BF16)
    width = 2 * EHD
    for part in range(2):
        out = lax.dot_general(weight_ref[1 + part], x, NT, preferred_element_type=F32)
        kv_ref[part * width : (part + 1) * width, :] = out.astype(BF16)


def encoder_kernel(q_ref, *refs):
    count = 8
    pieces, (weight_ref, out_ref, scores) = refs[:count], refs[count:]
    rows = q_ref.shape[1]
    scale = 1.0 / math.sqrt(EHD)
    heads = []
    for head in range(2):
        q = q_ref[head]
        top = None
        for j in range(count):
            s = jnp.dot(q, pieces[j][head * EHD : (head + 1) * EHD, :], preferred_element_type=F32)
            scores[head, :, j * rows : (j + 1) * rows] = s
            part = jnp.maximum(s[:, :128], s[:, 128:])
            top = part if top is None else jnp.maximum(top, part)
        top = jnp.max(top, axis=-1, keepdims=True)
        mix = jnp.zeros((rows, EHD), F32)
        total = jnp.zeros((rows, 128), F32)
        low = 2 * EHD + head * EHD
        for j in range(count):
            p = jnp.exp((scores[head, :, j * rows : (j + 1) * rows] - top) * scale)
            total = total + (p[:, :128] + p[:, 128:])
            mix = mix + lax.dot_general(
                p.astype(BF16), pieces[j][low : low + EHD, :], NT, preferred_element_type=F32
            )
        heads.append((mix / jnp.sum(total, axis=-1, keepdims=True)).astype(BF16))
    partial = jnp.dot(heads[0], weight_ref[:EHD, :], preferred_element_type=F32)
    partial = partial + jnp.dot(heads[1], weight_ref[EHD:, :], preferred_element_type=F32)
    size = rows // TENSOR
    for slot in range(TENSOR):
        out_ref[slot] = partial[slot * size : (slot + 1) * size].astype(BF16)


def cross_kernel(me_ref, *refs):
    pieces, (weight_ref, gain_ref, out_ref, encoded) = refs[:TENSOR], refs[TENSOR:]
    me = me_ref[0]
    for step in range(TENSOR):
        rows = pieces[step].shape[0]
        slot = jnp.bitwise_xor(me, step)
        encoded[pl.ds(pl.multiple_of(slot * rows, rows), rows), :] = pieces[step][...]
    proj = jnp.dot(encoded[...], weight_ref[...], preferred_element_type=F32)
    keys = proj[:, :HD]
    square_mean = jnp.mean(keys * keys, axis=-1, keepdims=True)
    keys = keys * lax.rsqrt(square_mean + EPSILON) * gain_ref[...]
    out_ref[:, :HD] = keys.astype(BF16)
    out_ref[:, HD:] = proj[:, HD:].astype(BF16)


def decode_kernel(place_ref, query_ref, *refs):
    slabs, out_ref = refs[:8], refs[8]
    rows = query_ref.shape[0]
    keys = slabs[0].shape[0]
    zh, x, c = place_ref[0], place_ref[1], place_ref[2]
    lane = lax.broadcasted_iota(jnp.int32, (1, keys), 1)
    base = (lane >> 6) * 512 + ((lane >> 5) & 1) * 128 + (lane & 31)
    extra = query_ref[:, 4 * HD :].astype(F32)
    limit = extra[:, 1:2] * 16.0 + extra[:, 2:3]
    limit = jnp.where(extra[:, 0:1] == zh.astype(F32), limit, 0.0)
    for head in range(4):
        q = query_ref[:, head * HD : (head + 1) * HD]
        mix = jnp.zeros((rows, HD), F32)
        total = jnp.zeros((rows, 128), F32)
        for j in range(8):
            px = jnp.bitwise_xor(x, j % 4)
            pc = jnp.bitwise_xor(c, j // 4)
            pos = (base + (pc * 256 + px * 32)).astype(F32)
            s = lax.dot_general(q, slabs[j][:, :HD], NT, preferred_element_type=F32)
            w = jnp.where(pos < limit, jnp.exp(s), 0.0)
            total = total + (w[:, :128] + w[:, 128:])
            mix = mix + jnp.dot(w.astype(BF16), slabs[j][:, HD:], preferred_element_type=F32)
        total = jnp.sum(total, axis=-1, keepdims=True)
        total = jnp.where(total > 0.0, total, 1.0)
        out_ref[:, head * HD : (head + 1) * HD] = (mix / total).astype(BF16)


def limits(mib):
    return pltpu.CompilerParams(vmem_limit_bytes=mib << 20)


def gather_xc(piece):
    along_x = [piece] + [xor_permute(piece, "x", XS, k) for k in range(1, XS)]
    return along_x + [xor_permute(value, "c", CORES, 1) for value in along_x]


def gather_tensor(piece):
    return [piece] + [xor_permute(piece, ("y", "zl"), TENSOR, k) for k in range(1, TENSOR)]


def on_device(
    patches,
    enc_gain,
    enc_qkv,
    enc_out,
    cross_kv,
    key_gain,
    dec_hidden,
    dec_gain,
    query_weight,
    query_gain,
    image_of_row,
    valid_count,
):
    tensor_index = (lax.axis_index("y") * ZL + lax.axis_index("zl")).astype(jnp.int32)
    me = tensor_index.reshape(1)
    place = jnp.stack([lax.axis_index("zh"), lax.axis_index("x"), lax.axis_index("c")]).astype(
        jnp.int32
    )
    patch_rows, width = patches.shape
    rows = patch_rows * TENSOR
    own = image_permute(patches)

    dec_rows = dec_hidden.shape[0]
    dec_normed = rms_norm(dec_hidden.astype(F32), dec_gain).astype(BF16)
    queries = jnp.dot(dec_normed, query_weight, preferred_element_type=F32)
    queries = queries.reshape(dec_rows, -1, HD)
    queries = (rms_norm(queries, query_gain) / math.sqrt(HD)).astype(BF16)
    columns = jnp.stack([image_of_row, valid_count // 16, valid_count % 16], axis=1)
    message = jnp.concatenate(
        [
            queries.reshape(dec_rows, -1),
            jnp.pad(columns.astype(BF16), ((0, 0), (0, HD - 3))),
        ],
        axis=1,
    )

    pieces = gather_tensor(own)
    q, kv = pl.pallas_call(
        qkv_kernel,
        out_shape=(
            jax.ShapeDtypeStruct((2, rows, EHD), BF16),
            jax.ShapeDtypeStruct((4 * EHD, rows), BF16),
        ),
        in_specs=[smem()] + vmem(TENSOR + 2),
        out_specs=tuple(vmem(2)),
        scratch_shapes=[pltpu.VMEM((rows, width), BF16)],
        compiler_params=limits(12),
    )(me, *pieces, enc_gain.reshape(1, -1), enc_qkv.transpose(0, 2, 1))
    kv_pieces = gather_xc(kv)

    partial = pl.pallas_call(
        encoder_kernel,
        out_shape=jax.ShapeDtypeStruct((TENSOR, patch_rows, width), BF16),
        in_specs=vmem(10),
        out_specs=vmem(1)[0],
        scratch_shapes=[pltpu.VMEM((2, rows, 8 * rows), F32)],
        compiler_params=limits(20),
    )(q, *kv_pieces, enc_out)
    shares = lax.all_to_all(partial, ("y", "zl"), 0, 0)
    every_query = [message] + [xor_permute(message, "zh", ZH, k) for k in range(1, ZH)]
    encoded = (own.astype(F32) + jnp.sum(shares.astype(F32), axis=0)).astype(BF16)
    encoded_pieces = gather_tensor(encoded)
    slab = pl.pallas_call(
        cross_kernel,
        out_shape=jax.ShapeDtypeStruct((rows, 2 * HD), BF16),
        in_specs=[smem()] + vmem(TENSOR + 2),
        out_specs=vmem(1)[0],
        scratch_shapes=[pltpu.VMEM((rows, width), BF16)],
        compiler_params=limits(12),
    )(me, *encoded_pieces, cross_kv, key_gain.reshape(1, -1))
    slabs = gather_xc(slab)
    result = None
    for k in (2, 1, 3, 0):
        out = pl.pallas_call(
            decode_kernel,
            out_shape=jax.ShapeDtypeStruct((dec_rows, 4 * HD), BF16),
            in_specs=[smem()] + vmem(9),
            out_specs=vmem(1)[0],
            compiler_params=limits(12),
        )(place, every_query[k], *slabs)
        if k:
            out = xor_permute(out, "zh", ZH, k)
        result = out if result is None else result + out
    return result


def solution(mesh):
    parts = Mesh(mesh.devices.reshape(ZH, CORES, YS, ZL, XS), ("zh", "c", "y", "zl", "x"))
    group, tensor, seq = ("zh", "c"), ("y", "zl"), ("x",)
    in_specs = (
        P(group + tensor + seq, None),
        P(),
        P(None, None, tensor),
        P(tensor, None),
        P(None, tensor),
        P(),
        P(group + seq, None),
        P(),
        P(None, tensor),
        P(),
        P(group + seq),
        P(group + seq),
    )
    out_specs = P(group + seq, tensor)

    return jax.shard_map(
        on_device, mesh=parts, in_specs=in_specs, out_specs=out_specs, check_vma=False
    )
```

profile of v0, /device:TPU:1, one launch (start us, length us, event | category | flops | bytes accessed | tf_op | source)
XLA Modules:
  0.0 121.4 jit_solution(13460696271127414877)
XLA Ops:
  1.7 8.7 %collective-permute-start.2 = (bf16[32,1280]{1,0:T(8,128)(2,1)S(1)}, bf16[32,1280]{1,0:T(8,128)(2,1)S(1)}, u32[]{:S(2)}, u32[]{:S(2)}) collective-permute-start(bf16[32,1280]{1,0:T(8,128)(2,1)S(1)} %collective-permute-done.1.refs_0_), channel_id=1, source_target_pairs={{0,4},{4,0},{8,12},{12,8},{16,20},{20,16},{24,28},{28,24},{1,5},{5... | collective-permute-start | bytes 245768 | tf_op jit(solution)/shard_map/ppermute | solution.py:35
  10.4 2.6 %collective-permute-start.3 = (bf16[32,1280]{1,0:T(8,128)(2,1)S(1)}, bf16[32,1280]{1,0:T(8,128)(2,1)S(1)}, u32[]{:S(2)}, u32[]{:S(2)}) collective-permute-start(bf16[32,1280]{1,0:T(8,128)(2,1)S(1)} %collective-permute-done.1.refs_0_), channel_id=1, source_target_pairs={{0,8},{4,12},{8,0},{12,4},{16,24},{20,28},{24,16},{28,20},{1,9},{5... | collective-permute-start | bytes 245768 | tf_op jit(solution)/shard_map/ppermute | solution.py:35
  13.9 5.0 %collective-permute-start.5 = (bf16[32,1280]{1,0:T(8,128)(2,1)S(1)}, bf16[32,1280]{1,0:T(8,128)(2,1)S(1)}, u32[]{:S(2)}, u32[]{:S(2)}) collective-permute-start(bf16[32,1280]{1,0:T(8,128)(2,1)S(1)} %collective-permute-done.1.refs_0_), channel_id=1, source_target_pairs={{0,16},{4,20},{8,24},{12,28},{16,0},{20,4},{24,8},{28,12},{1,17},{... | collective-permute-start | bytes 245768 | tf_op jit(solution)/shard_map/ppermute | solution.py:35
  18.9 3.0 %collective-permute-start.7 = (bf16[32,1280]{1,0:T(8,128)(2,1)S(1)}, bf16[32,1280]{1,0:T(8,128)(2,1)S(1)}, u32[]{:S(2)}, u32[]{:S(2)}) collective-permute-start(bf16[32,1280]{1,0:T(8,128)(2,1)S(1)} %collective-permute-done.1.refs_0_), channel_id=1, source_target_pairs={{0,24},{4,28},{8,16},{12,20},{16,8},{20,12},{24,0},{28,4},{1,25},{... | collective-permute-start | bytes 245768 | tf_op jit(solution)/shard_map/ppermute | solution.py:35
  25.2 2.4 %collective-permute-done.8.refs_7_ = bf16[32,1280]{1,0:T(8,128)(2,1)S(1)} collective-permute-done((bf16[32,1280]{1,0:T(8,128)(2,1)S(1)}, bf16[32,1280]{1,0:T(8,128)(2,1)S(1)}, u32[]{:S(2)}, u32[]{:S(2)}) %collective-permute-start.8) | collective-permute-done | bytes 81952 | tf_op jit(solution)/shard_map/ppermute | solution.py:35
  31.3 2.5 %collective-permute-start.10 = (bf16[320,256]{1,0:T(8,128)(2,1)S(1)}, bf16[320,256]{1,0:T(8,128)(2,1)S(1)}, u32[]{:S(2)}, u32[]{:S(2)}) collective-permute-start(bf16[320,256]{1,0:T(8,128)(2,1)S(1)} %get-tuple-element.8.refs_0_), channel_id=1, source_target_pairs={{0,2},{1,3},{2,0},{3,1},{4,6},{5,7},{6,4},{7,5},{8,10},{9,11},{10,... | collective-permute-start | bytes 491528 | tf_op jit(solution)/shard_map/ppermute | solution.py:35
  34.0 2.1 %fusion = f32[128]{0:T(128)S(1)} fusion(bf16[128,8192]{1,0:T(8,128)(2,1)} %param.18), kind=kLoop, calls=%fused_computation.2 | loop fusion | flops 3145600 | bytes 2097664 | tf_op jit(solution)/shard_map/reduce_sum | solution.py:22
  36.1 5.0 %collective-permute-start.12 = (bf16[320,256]{1,0:T(8,128)(2,1)S(1)}, bf16[320,256]{1,0:T(8,128)(2,1)S(1)}, u32[]{:S(2)}, u32[]{:S(2)}) collective-permute-start(bf16[320,256]{1,0:T(8,128)(2,1)S(1)} %get-tuple-element.8.refs_0_), channel_id=1, source_target_pairs={{0,32},{32,0},{1,33},{33,1},{2,34},{34,2},{3,35},{35,3},{4,36},{36... | collective-permute-start | bytes 491528 | tf_op jit(solution)/shard_map/ppermute | solution.py:35
  41.2 2.3 %collective-permute-start.14 = (bf16[320,256]{1,0:T(8,128)(2,1)S(1)}, bf16[320,256]{1,0:T(8,128)(2,1)S(1)}, u32[]{:S(2)}, u32[]{:S(2)}) collective-permute-start(bf16[320,256]{1,0:T(8,128)(2,1)S(1)} %collective-permute-done.10.refs_2_), channel_id=1, source_target_pairs={{0,32},{32,0},{1,33},{33,1},{2,34},{34,2},{3,35},{35,3},{4,36},{36... | collective-permute-start | bytes 491528 | tf_op jit(solution)/shard_map/ppermute | solution.py:35
  46.3 3.6 %shard_map.119 = bf16[8,32,1280]{2,1,0:T(8,128)(2,1)} custom-call(bf16[2,256,80]{2,1,0:T(8,128)(2,1)S(1)} %get-tuple-element.7.q_ref, bf16[320,256]{1,0:T(8,128)(2,1)S(1)} %get-tuple-element.8.refs_0_, bf16[320,256]{1,0:T(8,128)(2,1)S(1)} %collective-permute-done.9.refs_1_, bf16[320,256]{1,0:T(8,128)(2,1)S(1)} %collective-permute-done.10.refs_2_, ...), custom_call_target="tpu_custom_call" | custom-call | tf_op jit(solution)/shard_map/pallas_call | solution.py:208
  49.9 3.7 %all-to-all-start = ((bf16[8,32,1280]{2,1,0:T(8,128)(2,1)}), bf16[8,32,1280]{2,1,0:T(8,128)(2,1)S(1)}, u32[]{:S(2)}, u32[]{:S(2)}) async-start(bf16[8,32,1280]{2,1,0:T(8,128)(2,1)} %shard_map.119), calls=%async_computation | async-start | bytes 1310720 | tf_op jit(solution)/shard_map/all_to_all | solution.py:216
  53.7 5.4 %fusion.14 = (f32[128,512]{1,0:T(8,128)S(1)}, f32[128,512]{1,0:T(8,128)S(1)}) fusion(bf16[8192,512]{1,0:T(8,128)(2,1)} %param.20, bf16[128,8192]{1,0:T(8,128)(2,1)} %param.18, f32[8192]{0:T(1024)S(1)} %copy-done.7, f32[128]{0:T(128)S(1)} %add_rsqrt_fusion.1), kind=kOutput, calls=%fused_computation.32 | convolution fusion | flops 1078001664 | bytes 11043328 | tf_op jit(solution)/shard_map/dot_general | solution.py:182
  59.8 4.9 %all-to-all-done = bf16[8,32,1280]{2,1,0:T(8,128)(2,1)S(1)} async-done(((bf16[8,32,1280]{2,1,0:T(8,128)(2,1)}), bf16[8,32,1280]{2,1,0:T(8,128)(2,1)S(1)}, u32[]{:S(2)}, u32[]{:S(2)}) %all-to-all-start) | async-done | bytes 655392 | tf_op jit(solution)/shard_map/all_to_all | solution.py:216
  68.5 2.4 %collective-permute-start.20 = (bf16[32,1280]{1,0:T(8,128)(2,1)S(1)}, bf16[32,1280]{1,0:T(8,128)(2,1)S(1)}, u32[]{:S(2)}, u32[]{:S(2)}) collective-permute-start(bf16[32,1280]{1,0:T(8,128)(2,1)S(1)} %add_convert_fusion.refs_0_), channel_id=1, source_target_pairs={{0,20},{4,16},{8,28},{12,24},{16,4},{20,0},{24,12},{28,8},{1,21},{... | collective-permute-start | bytes 245768 | tf_op jit(solution)/shard_map/ppermute | solution.py:35
  74.3 3.2 %collective-permute-start.31 = (bf16[128,640]{1,0:T(8,128)(2,1)S(1)}, bf16[128,640]{1,0:T(8,128)(2,1)S(1)}, u32[]{:S(2)}, u32[]{:S(2)}) collective-permute-start(bf16[128,640]{1,0:T(8,128)(2,1)S(1)} %fusion.11.query_ref), channel_id=1, source_target_pairs={{0,64},{64,0},{128,192},{192,128},{1,65},{65,1},{129,193},{193,129... | collective-permute-start | bytes 491528 | tf_op jit(solution)/shard_map/ppermute | solution.py:35
  82.7 5.4 %collective-permute-start.26 = (bf16[256,256]{1,0:T(8,128)(2,1)S(1)}, bf16[256,256]{1,0:T(8,128)(2,1)S(1)}, u32[]{:S(2)}, u32[]{:S(2)}) collective-permute-start(bf16[256,256]{1,0:T(8,128)(2,1)S(1)} %shard_map.120.refs_0_), channel_id=1, source_target_pairs={{0,32},{32,0},{1,33},{33,1},{2,34},{34,2},{3,35},{35,3},{4,36},{36... | collective-permute-start | bytes 393224 | tf_op jit(solution)/shard_map/ppermute | solution.py:35
  88.0 6.0 %collective-permute-start = (bf16[128,640]{1,0:T(8,128)(2,1)S(1)}, bf16[128,640]{1,0:T(8,128)(2,1)S(1)}, u32[]{:S(2)}, u32[]{:S(2)}) collective-permute-start(bf16[128,640]{1,0:T(8,128)(2,1)S(1)} %fusion.11.query_ref), channel_id=1, source_target_pairs={{0,128},{64,192},{128,0},{192,64},{1,129},{65,193},{129,1},{193,65... | collective-permute-start | bytes 491528 | tf_op jit(solution)/shard_map/ppermute | solution.py:35
  96.1 2.9 %shard_map.122 = bf16[128,512]{1,0:T(8,128)(2,1)S(1)} custom-call(s32[3]{0:T(128)S(1)} %pad_add_fusion.place_ref, bf16[128,640]{1,0:T(8,128)(2,1)S(1)} %collective-permute-done.31.query_ref, bf16[256,256]{1,0:T(8,128)(2,1)S(1)} %shard_map.120.refs_0_, bf16[256,256]{1,0:T(8,128)(2,1)S(1)} %collective-permute-done.23.refs_1_, ...), custom_call_target="tpu_custom_call" | custom-call | tf_op jit(solution)/shard_map/pallas_call | solution.py:231
  101.5 2.9 %shard_map.121 = bf16[128,512]{1,0:T(8,128)(2,1)S(1)} custom-call(s32[3]{0:T(128)S(1)} %pad_add_fusion.place_ref, bf16[128,640]{1,0:T(8,128)(2,1)S(1)} %collective-permute-done.query_ref, bf16[256,256]{1,0:T(8,128)(2,1)S(1)} %shard_map.120.refs_0_, bf16[256,256]{1,0:T(8,128)(2,1)S(1)} %collective-permute-done.23.refs_1_, ...), custom_call_target="tpu_custom_call" | custom-call | tf_op jit(solution)/shard_map/pallas_call | solution.py:231
  104.3 5.1 %collective-permute-start.30 = (bf16[128,512]{1,0:T(8,128)(2,1)S(1)}, bf16[128,512]{1,0:T(8,128)(2,1)S(1)}, u32[]{:S(2)}, u32[]{:S(2)}) collective-permute-start(bf16[128,512]{1,0:T(8,128)(2,1)S(1)} %shard_map.121), channel_id=1, source_target_pairs={{0,128},{64,192},{128,0},{192,64},{1,129},{65,193},{129,1},{193,65... | collective-permute-start | bytes 393224 | tf_op jit(solution)/shard_map/ppermute | solution.py:35
  109.4 2.9 %shard_map.123 = bf16[128,512]{1,0:T(8,128)(2,1)S(1)} custom-call(s32[3]{0:T(128)S(1)} %pad_add_fusion.place_ref, bf16[128,640]{1,0:T(8,128)(2,1)S(1)} %collective-permute-done.33.query_ref, bf16[256,256]{1,0:T(8,128)(2,1)S(1)} %shard_map.120.refs_0_, bf16[256,256]{1,0:T(8,128)(2,1)S(1)} %collective-permute-done.23.refs_1_, ...), custom_call_target="tpu_custom_call" | custom-call | tf_op jit(solution)/shard_map/pallas_call | solution.py:231
  112.3 3.4 %collective-permute-start.34 = (bf16[128,512]{1,0:T(8,128)(2,1)S(1)}, bf16[128,512]{1,0:T(8,128)(2,1)S(1)}, u32[]{:S(2)}, u32[]{:S(2)}) collective-permute-start(bf16[128,512]{1,0:T(8,128)(2,1)S(1)} %shard_map.123), channel_id=1, source_target_pairs={{0,192},{64,128},{128,64},{192,0},{1,193},{65,129},{129,65},{193,1... | collective-permute-start | bytes 393224 | tf_op jit(solution)/shard_map/ppermute | solution.py:35
  115.7 2.8 %shard_map.124 = bf16[128,512]{1,0:T(8,128)(2,1)S(1)} custom-call(s32[3]{0:T(128)S(1)} %pad_add_fusion.place_ref, bf16[128,640]{1,0:T(8,128)(2,1)S(1)} %fusion.11.query_ref, bf16[256,256]{1,0:T(8,128)(2,1)S(1)} %shard_map.120.refs_0_, bf16[256,256]{1,0:T(8,128)(2,1)S(1)} %collective-permute-done.23.refs_1_, ...), custom_call_target="tpu_custom_call" | custom-call | tf_op jit(solution)/shard_map/pallas_call | solution.py:231
  118.6 2.1 %collective-permute-done.34 = bf16[128,512]{1,0:T(8,128)(2,1)S(1)} collective-permute-done((bf16[128,512]{1,0:T(8,128)(2,1)S(1)}, bf16[128,512]{1,0:T(8,128)(2,1)S(1)}, u32[]{:S(2)}, u32[]{:S(2)}) %collective-permute-start.34) | collective-permute-done | bytes 131104 | tf_op jit(solution)/shard_map/ppermute | solution.py:35
  (89 shorter events, 30.9 us)
Async XLA Ops:
  1.7 17.2 %collective-permute-start.2 = (bf16[32,1280]{1,0:T(8,128)(2,1)S(1)}, bf16[32,1280]{1,0:T(8,128)(2,1)S(1)}, u32[]{:S(2)}, u32[]{:S(2)}) collective-permute-start(bf16[32,1280]{1,0:T(8,128)(2,1)S(1)} %collective-permute-done.1.refs_0_), channel_id=1, source_target_pairs={{0,4},{4,0},{8,12},{12,8},{16,20},{20,16},{24,28},{28,24},{1,5},{5... | collective-permute-start | bytes 245768 | tf_op jit(solution)/shard_map/ppermute | solution.py:35
  10.4 11.5 %collective-permute-start.3 = (bf16[32,1280]{1,0:T(8,128)(2,1)S(1)}, bf16[32,1280]{1,0:T(8,128)(2,1)S(1)}, u32[]{:S(2)}, u32[]{:S(2)}) collective-permute-start(bf16[32,1280]{1,0:T(8,128)(2,1)S(1)} %collective-permute-done.1.refs_0_), channel_id=1, source_target_pairs={{0,8},{4,12},{8,0},{12,4},{16,24},{20,28},{24,16},{28,20},{1,9},{5... | collective-permute-start | bytes 245768 | tf_op jit(solution)/shard_map/ppermute | solution.py:35
  13.0 10.8 %collective-permute-start.4 = (bf16[32,1280]{1,0:T(8,128)(2,1)S(1)}, bf16[32,1280]{1,0:T(8,128)(2,1)S(1)}, u32[]{:S(2)}, u32[]{:S(2)}) collective-permute-start(bf16[32,1280]{1,0:T(8,128)(2,1)S(1)} %collective-permute-done.1.refs_0_), channel_id=1, source_target_pairs={{0,12},{4,8},{8,4},{12,0},{16,28},{20,24},{24,20},{28,16},{1,13},{... | collective-permute-start | bytes 245768 | tf_op jit(solution)/shard_map/ppermute | solution.py:35
  13.9 9.9 %collective-permute-start.5 = (bf16[32,1280]{1,0:T(8,128)(2,1)S(1)}, bf16[32,1280]{1,0:T(8,128)(2,1)S(1)}, u32[]{:S(2)}, u32[]{:S(2)}) collective-permute-start(bf16[32,1280]{1,0:T(8,128)(2,1)S(1)} %collective-permute-done.1.refs_0_), channel_id=1, source_target_pairs={{0,16},{4,20},{8,24},{12,28},{16,0},{20,4},{24,8},{28,12},{1,17},{... | collective-permute-start | bytes 245768 | tf_op jit(solution)/shard_map/ppermute | solution.py:35
  30.0 11.1 %collective-permute-start.9 = (bf16[320,256]{1,0:T(8,128)(2,1)S(1)}, bf16[320,256]{1,0:T(8,128)(2,1)S(1)}, u32[]{:S(2)}, u32[]{:S(2)}) collective-permute-start(bf16[320,256]{1,0:T(8,128)(2,1)S(1)} %get-tuple-element.8.refs_0_), channel_id=1, source_target_pairs={{0,1},{1,0},{2,3},{3,2},{4,5},{5,4},{6,7},{7,6},{8,9},{9,8},{10,11... | collective-permute-start | bytes 491528 | tf_op jit(solution)/shard_map/ppermute | solution.py:35
  31.3 9.9 %collective-permute-start.10 = (bf16[320,256]{1,0:T(8,128)(2,1)S(1)}, bf16[320,256]{1,0:T(8,128)(2,1)S(1)}, u32[]{:S(2)}, u32[]{:S(2)}) collective-permute-start(bf16[320,256]{1,0:T(8,128)(2,1)S(1)} %get-tuple-element.8.refs_0_), channel_id=1, source_target_pairs={{0,2},{1,3},{2,0},{3,1},{4,6},{5,7},{6,4},{7,5},{8,10},{9,11},{10,... | collective-permute-start | bytes 491528 | tf_op jit(solution)/shard_map/ppermute | solution.py:35
  33.8 9.7 %collective-permute-start.11 = (bf16[320,256]{1,0:T(8,128)(2,1)S(1)}, bf16[320,256]{1,0:T(8,128)(2,1)S(1)}, u32[]{:S(2)}, u32[]{:S(2)}) collective-permute-start(bf16[320,256]{1,0:T(8,128)(2,1)S(1)} %get-tuple-element.8.refs_0_), channel_id=1, source_target_pairs={{0,3},{1,2},{2,1},{3,0},{4,7},{5,6},{6,5},{7,4},{8,11},{9,10},{10,... | collective-permute-start | bytes 491528 | tf_op jit(solution)/shard_map/ppermute | solution.py:35
  36.1 9.2 %collective-permute-start.12 = (bf16[320,256]{1,0:T(8,128)(2,1)S(1)}, bf16[320,256]{1,0:T(8,128)(2,1)S(1)}, u32[]{:S(2)}, u32[]{:S(2)}) collective-permute-start(bf16[320,256]{1,0:T(8,128)(2,1)S(1)} %get-tuple-element.8.refs_0_), channel_id=1, source_target_pairs={{0,32},{32,0},{1,33},{33,1},{2,34},{34,2},{3,35},{35,3},{4,36},{36... | collective-permute-start | bytes 491528 | tf_op jit(solution)/shard_map/ppermute | solution.py:35
  49.9 14.7 %all-to-all-start = ((bf16[8,32,1280]{2,1,0:T(8,128)(2,1)}), bf16[8,32,1280]{2,1,0:T(8,128)(2,1)S(1)}, u32[]{:S(2)}, u32[]{:S(2)}) async-start(bf16[8,32,1280]{2,1,0:T(8,128)(2,1)} %shard_map.119), calls=%async_computation | async-start | bytes 1310720 | tf_op jit(solution)/shard_map/all_to_all | solution.py:216
  65.4 7.2 %collective-permute-start.17 = (bf16[32,1280]{1,0:T(8,128)(2,1)S(1)}, bf16[32,1280]{1,0:T(8,128)(2,1)S(1)}, u32[]{:S(2)}, u32[]{:S(2)}) collective-permute-start(bf16[32,1280]{1,0:T(8,128)(2,1)S(1)} %add_convert_fusion.refs_0_), channel_id=1, source_target_pairs={{0,8},{4,12},{8,0},{12,4},{16,24},{20,28},{24,16},{28,20},{1,9},{5... | collective-permute-start | bytes 245768 | tf_op jit(solution)/shard_map/ppermute | solution.py:35
  66.6 7.7 %collective-permute-start.18 = (bf16[32,1280]{1,0:T(8,128)(2,1)S(1)}, bf16[32,1280]{1,0:T(8,128)(2,1)S(1)}, u32[]{:S(2)}, u32[]{:S(2)}) collective-permute-start(bf16[32,1280]{1,0:T(8,128)(2,1)S(1)} %add_convert_fusion.refs_0_), channel_id=1, source_target_pairs={{0,12},{4,8},{8,4},{12,0},{16,28},{20,24},{24,20},{28,16},{1,13},{... | collective-permute-start | bytes 245768 | tf_op jit(solution)/shard_map/ppermute | solution.py:35
  67.7 9.8 %collective-permute-start.19 = (bf16[32,1280]{1,0:T(8,128)(2,1)S(1)}, bf16[32,1280]{1,0:T(8,128)(2,1)S(1)}, u32[]{:S(2)}, u32[]{:S(2)}) collective-permute-start(bf16[32,1280]{1,0:T(8,128)(2,1)S(1)} %add_convert_fusion.refs_0_), channel_id=1, source_target_pairs={{0,16},{4,20},{8,24},{12,28},{16,0},{20,4},{24,8},{28,12},{1,17},{... | collective-permute-start | bytes 245768 | tf_op jit(solution)/shard_map/ppermute | solution.py:35
  68.5 9.0 %collective-permute-start.20 = (bf16[32,1280]{1,0:T(8,128)(2,1)S(1)}, bf16[32,1280]{1,0:T(8,128)(2,1)S(1)}, u32[]{:S(2)}, u32[]{:S(2)}) collective-permute-start(bf16[32,1280]{1,0:T(8,128)(2,1)S(1)} %add_convert_fusion.refs_0_), channel_id=1, source_target_pairs={{0,20},{4,16},{8,28},{12,24},{16,4},{20,0},{24,12},{28,8},{1,21},{... | collective-permute-start | bytes 245768 | tf_op jit(solution)/shard_map/ppermute | solution.py:35
  71.0 6.6 %collective-permute-start.21 = (bf16[32,1280]{1,0:T(8,128)(2,1)S(1)}, bf16[32,1280]{1,0:T(8,128)(2,1)S(1)}, u32[]{:S(2)}, u32[]{:S(2)}) collective-permute-start(bf16[32,1280]{1,0:T(8,128)(2,1)S(1)} %add_convert_fusion.refs_0_), channel_id=1, source_target_pairs={{0,24},{4,28},{8,16},{12,20},{16,8},{20,12},{24,0},{28,4},{1,25},{... | collective-permute-start | bytes 245768 | tf_op jit(solution)/shard_map/ppermute | solution.py:35
  74.3 13.7 %collective-permute-start.31 = (bf16[128,640]{1,0:T(8,128)(2,1)S(1)}, bf16[128,640]{1,0:T(8,128)(2,1)S(1)}, u32[]{:S(2)}, u32[]{:S(2)}) collective-permute-start(bf16[128,640]{1,0:T(8,128)(2,1)S(1)} %fusion.11.query_ref), channel_id=1, source_target_pairs={{0,64},{64,0},{128,192},{192,128},{1,65},{65,1},{129,193},{193,129... | collective-permute-start | bytes 491528 | tf_op jit(solution)/shard_map/ppermute | solution.py:35
  78.7 15.3 %collective-permute-start.23 = (bf16[256,256]{1,0:T(8,128)(2,1)S(1)}, bf16[256,256]{1,0:T(8,128)(2,1)S(1)}, u32[]{:S(2)}, u32[]{:S(2)}) collective-permute-start(bf16[256,256]{1,0:T(8,128)(2,1)S(1)} %shard_map.120.refs_0_), channel_id=1, source_target_pairs={{0,1},{1,0},{2,3},{3,2},{4,5},{5,4},{6,7},{7,6},{8,9},{9,8},{10,11... | collective-permute-start | bytes 393224 | tf_op jit(solution)/shard_map/ppermute | solution.py:35
  78.8 15.2 %collective-permute-start.24 = (bf16[256,256]{1,0:T(8,128)(2,1)S(1)}, bf16[256,256]{1,0:T(8,128)(2,1)S(1)}, u32[]{:S(2)}, u32[]{:S(2)}) collective-permute-start(bf16[256,256]{1,0:T(8,128)(2,1)S(1)} %shard_map.120.refs_0_), channel_id=1, source_target_pairs={{0,2},{1,3},{2,0},{3,1},{4,6},{5,7},{6,4},{7,5},{8,10},{9,11},{10,... | collective-permute-start | bytes 393224 | tf_op jit(solution)/shard_map/ppermute | solution.py:35
  80.9 13.6 %collective-permute-start.25 = (bf16[256,256]{1,0:T(8,128)(2,1)S(1)}, bf16[256,256]{1,0:T(8,128)(2,1)S(1)}, u32[]{:S(2)}, u32[]{:S(2)}) collective-permute-start(bf16[256,256]{1,0:T(8,128)(2,1)S(1)} %shard_map.120.refs_0_), channel_id=1, source_target_pairs={{0,3},{1,2},{2,1},{3,0},{4,7},{5,6},{6,5},{7,4},{8,11},{9,10},{10,... | collective-permute-start | bytes 393224 | tf_op jit(solution)/shard_map/ppermute | solution.py:35
  82.7 12.0 %collective-permute-start.26 = (bf16[256,256]{1,0:T(8,128)(2,1)S(1)}, bf16[256,256]{1,0:T(8,128)(2,1)S(1)}, u32[]{:S(2)}, u32[]{:S(2)}) collective-permute-start(bf16[256,256]{1,0:T(8,128)(2,1)S(1)} %shard_map.120.refs_0_), channel_id=1, source_target_pairs={{0,32},{32,0},{1,33},{33,1},{2,34},{34,2},{3,35},{35,3},{4,36},{36... | collective-permute-start | bytes 393224 | tf_op jit(solution)/shard_map/ppermute | solution.py:35
  88.0 13.4 %collective-permute-start = (bf16[128,640]{1,0:T(8,128)(2,1)S(1)}, bf16[128,640]{1,0:T(8,128)(2,1)S(1)}, u32[]{:S(2)}, u32[]{:S(2)}) collective-permute-start(bf16[128,640]{1,0:T(8,128)(2,1)S(1)} %fusion.11.query_ref), channel_id=1, source_target_pairs={{0,128},{64,192},{128,0},{192,64},{1,129},{65,193},{129,1},{193,65... | collective-permute-start | bytes 491528 | tf_op jit(solution)/shard_map/ppermute | solution.py:35
  94.1 15.3 %collective-permute-start.33 = (bf16[128,640]{1,0:T(8,128)(2,1)S(1)}, bf16[128,640]{1,0:T(8,128)(2,1)S(1)}, u32[]{:S(2)}, u32[]{:S(2)}) collective-permute-start(bf16[128,640]{1,0:T(8,128)(2,1)S(1)} %fusion.11.query_ref), channel_id=1, source_target_pairs={{0,192},{64,128},{128,64},{192,0},{1,193},{65,129},{129,65},{193,1... | collective-permute-start | bytes 491528 | tf_op jit(solution)/shard_map/ppermute | solution.py:35
  99.0 19.6 %collective-permute-start.32 = (bf16[128,512]{1,0:T(8,128)(2,1)S(1)}, bf16[128,512]{1,0:T(8,128)(2,1)S(1)}, u32[]{:S(2)}, u32[]{:S(2)}) collective-permute-start(bf16[128,512]{1,0:T(8,128)(2,1)S(1)} %shard_map.122), channel_id=1, source_target_pairs={{0,64},{64,0},{128,192},{192,128},{1,65},{65,1},{129,193},{193,129... | collective-permute-start | bytes 393224 | tf_op jit(solution)/shard_map/ppermute | solution.py:35
  104.3 14.2 %collective-permute-start.30 = (bf16[128,512]{1,0:T(8,128)(2,1)S(1)}, bf16[128,512]{1,0:T(8,128)(2,1)S(1)}, u32[]{:S(2)}, u32[]{:S(2)}) collective-permute-start(bf16[128,512]{1,0:T(8,128)(2,1)S(1)} %shard_map.121), channel_id=1, source_target_pairs={{0,128},{64,192},{128,0},{192,64},{1,129},{65,193},{129,1},{193,65... | collective-permute-start | bytes 393224 | tf_op jit(solution)/shard_map/ppermute | solution.py:35
  112.3 8.4 %collective-permute-start.34 = (bf16[128,512]{1,0:T(8,128)(2,1)S(1)}, bf16[128,512]{1,0:T(8,128)(2,1)S(1)}, u32[]{:S(2)}, u32[]{:S(2)}) collective-permute-start(bf16[128,512]{1,0:T(8,128)(2,1)S(1)} %shard_map.123), channel_id=1, source_target_pairs={{0,192},{64,128},{128,64},{192,0},{1,193},{65,129},{129,65},{193,1... | collective-permute-start | bytes 393224 | tf_op jit(solution)/shard_map/ppermute | solution.py:35
  (20 other events, 239.6 us)
where the time goes:
time: 123 us; the launch traced here: 121 us
  starting transfers between devices  77.7 us (63%)
  Pallas kernels  16.6 us (13%)
  waiting for transfers between devices  15.6 us (13%)
  matrix products  5.39 us (4%)
  other arithmetic  3.27 us (3%)
  local copies, waits for them, and re-layouts  2.45 us (2%)
    ppermute x34, starting transfers between devices, xor_permute(): return lax.ppermute(values, axes, [(i, i ^ step) for i in range(size)])  72.4 us
    pallas_call x4, Pallas kernels, on_device(): pl.pallas_call(decode_kernel, out_shape=jax.ShapeDtypeStruct((dec_rows, 4...  11.4 us
    ppermute x34, waiting for transfers between devices, xor_permute(): return lax.ppermute(values, axes, [(i, i ^ step) for i in range(size)])  10.7 us
    dot_general x1, matrix products, on_device(): queries = jnp.dot(dec_normed, query_weight, preferred_element_type=F32)  5.39 us
    all_to_all x1, waiting for transfers between devices, on_device(): shares = lax.all_to_all(partial, ('y', 'zl'), 0, 0)  4.9 us
    all_to_all x1, starting transfers between devices, on_device(): shares = lax.all_to_all(partial, ('y', 'zl'), 0, 0)  3.72 us
    pallas_call x1, Pallas kernels, on_device(): pl.pallas_call(encoder_kernel, out_shape=jax.ShapeDtypeStruct((TENSOR, pa...  3.63 us
  transfers between devices with their start and end apart: 36, of which 10 were waited for; matrix products, arithmetic and copies ran while one was open for 7% of the time, Pallas kernels for 10%

commit v1 on v0

--- a/solution.py
+++ b/solution.py
@@ -14,13 +14,9 @@
 F32 = jnp.float32
 BF16 = jnp.bfloat16
 ZH, CORES, YS, ZL, XS = 4, 2, 4, 2, 4
+SHARE, SLOT = 20, 32
 TENSOR = YS * ZL
 NT = (((1,), (1,)), ((), ()))
-
-
-def rms_norm(values, gain_vector):
-    square_mean = jnp.mean(values * values, axis=-1, keepdims=True)
-    return values * lax.rsqrt(square_mean + EPSILON) * gain_vector
 
 
 def vmem(count):
@@ -46,33 +42,43 @@
 
 
 def qkv_kernel(me_ref, *refs):
-    pieces, (gain_ref, weight_ref, q_ref, kv_ref, normed) = refs[:TENSOR], refs[TENSOR:]
+    pieces, refs = refs[:TENSOR], refs[TENSOR:]
+    gain_ref, weight_ref, cross_ref, q_ref, kv_ref, fold_ref, base_ref, normed, raw, out_rows = refs
     me = me_ref[0]
+    rows = raw.shape[0] // TENSOR
     for step in range(TENSOR):
-        values = pieces[step][...].astype(F32)
+        piece = pieces[step][:rows, :]
+        values = piece.astype(F32)
         mean_value = jnp.mean(values, axis=-1, keepdims=True)
         centered = values - mean_value
         variance = jnp.mean(centered * centered, axis=-1, keepdims=True)
         result = centered * lax.rsqrt(variance + EPSILON) * gain_ref[...]
-        rows = values.shape[0]
-        slot = jnp.bitwise_xor(me, step)
-        normed[pl.ds(pl.multiple_of(slot * rows, rows), rows), :] = result.astype(BF16)
+        place = pl.ds(pl.multiple_of(jnp.bitwise_xor(me, step) * rows, rows), rows)
+        normed[place, :] = result.astype(BF16)
+        raw[place, :] = piece
+        share = pieces[step][rows:, :]
+        fill = jnp.zeros((SLOT - share.shape[0], share.shape[1]), BF16)
+        place = pl.ds(pl.multiple_of(jnp.bitwise_xor(me, step) * SLOT, SLOT), SLOT)
+        out_rows[place, :] = jnp.concatenate([share, fill], axis=0)
     x = normed[...]
-    q = lax.dot_general(x, weight_ref[0], NT, preferred_element_type=F32)
-    for head in range(2):
-        q_ref[head] = q[:, head * EHD : (head + 1) * EHD].astype(BF16)
     width = 2 * EHD
     for part in range(2):
         out = lax.dot_general(weight_ref[1 + part], x, NT, preferred_element_type=F32)
         kv_ref[part * width : (part + 1) * width, :] = out.astype(BF16)
+    q = lax.dot_general(x, weight_ref[0], NT, preferred_element_type=F32)
+    for head in range(2):
+        q_ref[head] = q[:, head * EHD : (head + 1) * EHD].astype(BF16)
+    cross = cross_ref[...]
+    fold_ref[...] = jnp.dot(out_rows[...], cross, preferred_element_type=F32).astype(BF16)
+    base_ref[...] = jnp.dot(raw[...], cross, preferred_element_type=F32)
 
 
 def encoder_kernel(q_ref, *refs):
     count = 8
-    pieces, (weight_ref, out_ref, scores) = refs[:count], refs[count:]
+    pieces, (out_ref, scores) = refs[:count], refs[count:]
     rows = q_ref.shape[1]
     scale = 1.0 / math.sqrt(EHD)
-    heads = []
+    spread = jnp.zeros(out_ref.shape, F32)
     for head in range(2):
         q = q_ref[head]
         top = None
@@ -91,22 +97,31 @@
             mix = mix + lax.dot_general(
                 p.astype(BF16), pieces[j][low : low + EHD, :], NT, preferred_element_type=F32
             )
-        heads.append((mix / jnp.sum(total, axis=-1, keepdims=True)).astype(BF16))
-    partial = jnp.dot(heads[0], weight_ref[:EHD, :], preferred_element_type=F32)
-    partial = partial + jnp.dot(heads[1], weight_ref[EHD:, :], preferred_element_type=F32)
-    size = rows // TENSOR
-    for slot in range(TENSOR):
-        out_ref[slot] = partial[slot * size : (slot + 1) * size].astype(BF16)
-
-
-def cross_kernel(me_ref, *refs):
-    pieces, (weight_ref, gain_ref, out_ref, encoded) = refs[:TENSOR], refs[TENSOR:]
-    me = me_ref[0]
+        attended = (mix / jnp.sum(total, axis=-1, keepdims=True)).astype(BF16)
+        feature = lax.broadcasted_iota(jnp.int32, (EHD, out_ref.shape[1]), 0) + head * EHD
+        column = lax.broadcasted_iota(jnp.int32, (EHD, out_ref.shape[1]), 1)
+        block = (feature * 3277) >> 16
+        chosen = (column == feature + block * (SLOT - SHARE)).astype(F32).astype(BF16)
+        spread = spread + jnp.dot(attended, chosen, preferred_element_type=F32)
+    out_ref[...] = spread.astype(BF16)
+
+
+def cross_kernel(me_ref, place_ref, *refs):
+    pieces, folds, refs = refs[:TENSOR], refs[TENSOR : TENSOR + 8], refs[TENSOR + 8 :]
+    base_ref, gain_ref, out_ref, weight = refs
+    me, x, c = me_ref[0], place_ref[1], place_ref[2]
+    size = 8 * SLOT
+    for k in range(8):
+        owner = jnp.bitwise_xor(c, k // 4) * 4 + jnp.bitwise_xor(x, k % 4)
+        for t in range(TENSOR):
+            low = pl.multiple_of(t * size + owner * SLOT, SLOT)
+            weight[pl.ds(low, SLOT), :] = folds[k][t * SLOT : (t + 1) * SLOT, :]
+    proj = base_ref[...]
     for step in range(TENSOR):
-        rows = pieces[step].shape[0]
-        slot = jnp.bitwise_xor(me, step)
-        encoded[pl.ds(pl.multiple_of(slot * rows, rows), rows), :] = pieces[step][...]
-    proj = jnp.dot(encoded[...], weight_ref[...], preferred_element_type=F32)
+        low = pl.multiple_of(jnp.bitwise_xor(me, step) * size, size)
+        proj = proj + jnp.dot(
+            pieces[step][...], weight[pl.ds(low, size), :], preferred_element_type=F32
+        )
     keys = proj[:, :HD]
     square_mean = jnp.mean(keys * keys, axis=-1, keepdims=True)
     keys = keys * lax.rsqrt(square_mean + EPSILON) * gain_ref[...]
@@ -114,18 +129,51 @@
     out_ref[:, HD:] = proj[:, HD:].astype(BF16)
 
 
+def query_kernel(x_ref, gain_ref, weight_ref, head_gain_ref, image_ref, count_ref, out_ref, total, inverse):
+    step = pl.program_id(0)
+    rows = x_ref.shape[0]
+    depth = weight_ref.shape[0]
+
+    @pl.when(step == 0)
+    def _():
+        square = jnp.zeros((rows, 128), F32)
+        for low in range(0, x_ref.shape[1], 128):
+            part = x_ref[:, low : low + 128].astype(F32)
+            square = square + part * part
+        mean = jnp.sum(square, axis=-1, keepdims=True) / x_ref.shape[1]
+        inverse[...] = jnp.broadcast_to(lax.rsqrt(mean + EPSILON), inverse.shape)
+        total[...] = jnp.zeros_like(total)
+
+    columns = pl.ds(pl.multiple_of(step * depth, depth), depth)
+    normed = x_ref[:, columns].astype(F32) * inverse[:, 0:1] * gain_ref[:, columns]
+    total[...] += jnp.dot(normed.astype(BF16), weight_ref[...], preferred_element_type=F32)
+
+    @pl.when(step == pl.num_programs(0) - 1)
+    def _():
+        for head in range(4):
+            q = total[:, head * HD : (head + 1) * HD]
+            mean = jnp.mean(q * q, axis=-1, keepdims=True)
+            q = q * lax.rsqrt(mean + EPSILON) * head_gain_ref[...] / math.sqrt(HD)
+            out_ref[:rows, head * HD : (head + 1) * HD] = q.astype(BF16)
+        count = count_ref[...]
+        extra = jnp.concatenate([image_ref[...], count >> 4, count & 15], axis=0)
+        extra = jnp.concatenate([extra, jnp.zeros((13, rows), jnp.int32)], axis=0)
+        out_ref[rows:, :rows] = extra.astype(F32).astype(BF16)
+        out_ref[rows:, rows:] = jnp.zeros((16, out_ref.shape[1] - rows), BF16)
+
+
 def decode_kernel(place_ref, query_ref, *refs):
     slabs, out_ref = refs[:8], refs[8]
-    rows = query_ref.shape[0]
     keys = slabs[0].shape[0]
     zh, x, c = place_ref[0], place_ref[1], place_ref[2]
     lane = lax.broadcasted_iota(jnp.int32, (1, keys), 1)
     base = (lane >> 6) * 512 + ((lane >> 5) & 1) * 128 + (lane & 31)
-    extra = query_ref[:, 4 * HD :].astype(F32)
-    limit = extra[:, 1:2] * 16.0 + extra[:, 2:3]
-    limit = jnp.where(extra[:, 0:1] == zh.astype(F32), limit, 0.0)
+    rows = out_ref.shape[0]
+    extra = query_ref[rows : rows + 8, :HD].astype(F32)
+    limit = jnp.where(extra[0:1] == zh.astype(F32), extra[1:2] * 16.0 + extra[2:3], 0.0)
+    limit = jnp.broadcast_to(limit, (8, rows)).T[:, 0:1]
     for head in range(4):
-        q = query_ref[:, head * HD : (head + 1) * HD]
+        q = query_ref[:rows, head * HD : (head + 1) * HD]
         mix = jnp.zeros((rows, HD), F32)
         total = jnp.zeros((rows, 128), F32)
         for j in range(8):
@@ -151,7 +199,10 @@
 
 
 def gather_tensor(piece):
-    return [piece] + [xor_permute(piece, ("y", "zl"), TENSOR, k) for k in range(1, TENSOR)]
+    pieces = {0: piece}
+    for k in (5, 7, 3, 4, 6, 2, 1):
+        pieces[k] = xor_permute(piece, ("y", "zl"), TENSOR, k)
+    return [pieces[k] for k in range(TENSOR)]
 
 
 def on_device(
@@ -178,53 +229,74 @@
     own = image_permute(patches)
 
     dec_rows = dec_hidden.shape[0]
-    dec_normed = rms_norm(dec_hidden.astype(F32), dec_gain).astype(BF16)
-    queries = jnp.dot(dec_normed, query_weight, preferred_element_type=F32)
-    queries = queries.reshape(dec_rows, -1, HD)
-    queries = (rms_norm(queries, query_gain) / math.sqrt(HD)).astype(BF16)
-    columns = jnp.stack([image_of_row, valid_count // 16, valid_count % 16], axis=1)
-    message = jnp.concatenate(
-        [
-            queries.reshape(dec_rows, -1),
-            jnp.pad(columns.astype(BF16), ((0, 0), (0, HD - 3))),
+    depth = 1024
+    query_width = query_weight.shape[1]
+    message = pl.pallas_call(
+        query_kernel,
+        grid=(dec_hidden.shape[1] // depth,),
+        out_shape=jax.ShapeDtypeStruct((dec_rows + 16, query_width), BF16),
+        in_specs=[
+            pl.BlockSpec(dec_hidden.shape, lambda i: (0, 0)),
+            pl.BlockSpec((1, dec_hidden.shape[1]), lambda i: (0, 0)),
+            pl.BlockSpec((depth, query_width), lambda i: (i, 0)),
+            pl.BlockSpec((1, HD), lambda i: (0, 0)),
+            pl.BlockSpec((1, dec_rows), lambda i: (0, 0)),
+            pl.BlockSpec((1, dec_rows), lambda i: (0, 0)),
         ],
-        axis=1,
+        out_specs=pl.BlockSpec((dec_rows + 16, query_width), lambda i: (0, 0)),
+        scratch_shapes=[pltpu.VMEM((dec_rows, query_width), F32), pltpu.VMEM((dec_rows, 128), F32)],
+        compiler_params=limits(56),
+    )(
+        dec_hidden,
+        dec_gain.reshape(1, -1),
+        query_weight,
+        query_gain.reshape(1, -1),
+        image_of_row.reshape(1, -1),
+        valid_count.reshape(1, -1),
     )
 
-    pieces = gather_tensor(own)
-    q, kv = pl.pallas_call(
+    owner = lax.axis_index("c") * XS + lax.axis_index("x")
+    share = lax.dynamic_slice_in_dim(enc_out, owner * SHARE, SHARE, axis=0)
+    share = jnp.pad(share, ((0, 24 - SHARE), (0, 0)))
+    pieces = gather_tensor(jnp.concatenate([own, share], axis=0))
+    q, kv, fold, base = pl.pallas_call(
         qkv_kernel,
         out_shape=(
             jax.ShapeDtypeStruct((2, rows, EHD), BF16),
             jax.ShapeDtypeStruct((4 * EHD, rows), BF16),
+            jax.ShapeDtypeStruct((TENSOR * SLOT, 2 * HD), BF16),
+            jax.ShapeDtypeStruct((rows, 2 * HD), F32),
         ),
-        in_specs=[smem()] + vmem(TENSOR + 2),
-        out_specs=tuple(vmem(2)),
-        scratch_shapes=[pltpu.VMEM((rows, width), BF16)],
-        compiler_params=limits(12),
-    )(me, *pieces, enc_gain.reshape(1, -1), enc_qkv.transpose(0, 2, 1))
+        in_specs=[smem()] + vmem(TENSOR + 3),
+        out_specs=tuple(vmem(4)),
+        scratch_shapes=[
+            pltpu.VMEM((rows, width), BF16),
+            pltpu.VMEM((rows, width), BF16),
+            pltpu.VMEM((TENSOR * SLOT, width), BF16),
+        ],
+        compiler_params=limits(16),
+    )(me, *pieces, enc_gain.reshape(1, -1), enc_qkv.transpose(0, 2, 1), cross_kv)
     kv_pieces = gather_xc(kv)
-
-    partial = pl.pallas_call(
+    every_query = [message] + [xor_permute(message, "zh", ZH, k) for k in range(1, ZH)]
+
+    attended = pl.pallas_call(
         encoder_kernel,
-        out_shape=jax.ShapeDtypeStruct((TENSOR, patch_rows, width), BF16),
-        in_specs=vmem(10),
+        out_shape=jax.ShapeDtypeStruct((rows, 8 * SLOT), BF16),
+        in_specs=vmem(9),
         out_specs=vmem(1)[0],
         scratch_shapes=[pltpu.VMEM((2, rows, 8 * rows), F32)],
         compiler_params=limits(20),
-    )(q, *kv_pieces, enc_out)
-    shares = lax.all_to_all(partial, ("y", "zl"), 0, 0)
-    every_query = [message] + [xor_permute(message, "zh", ZH, k) for k in range(1, ZH)]
-    encoded = (own.astype(F32) + jnp.sum(shares.astype(F32), axis=0)).astype(BF16)
-    encoded_pieces = gather_tensor(encoded)
+    )(q, *kv_pieces)
+    attended_pieces = gather_tensor(attended)
+    folds = gather_xc(fold)
     slab = pl.pallas_call(
         cross_kernel,
         out_shape=jax.ShapeDtypeStruct((rows, 2 * HD), BF16),
-        in_specs=[smem()] + vmem(TENSOR + 2),
+        in_specs=[smem()] * 2 + vmem(TENSOR + 10),
         out_specs=vmem(1)[0],
-        scratch_shapes=[pltpu.VMEM((rows, width), BF16)],
+        scratch_shapes=[pltpu.VMEM((TENSOR * 8 * SLOT, 2 * HD), BF16)],
         compiler_params=limits(12),
-    )(me, *encoded_pieces, cross_kv, key_gain.reshape(1, -1))
+    )(me, place, *attended_pieces, *folds, base, key_gain.reshape(1, -1))
     slabs = gather_xc(slab)
     result = None
     for k in (2, 1, 3, 0):

time: 123 us -> 130 us (1.057)
  Pallas kernels: 16.6 us -> 25.3 us
  starting transfers between devices: 77.7 us -> 84.6 us
  matrix products: 5.39 us -> 0 us
  other arithmetic: 3.27 us -> 0.78 us
    ppermute x34 -> x41, starting transfers between devices: 72.4 us -> 82.9 us  [xor_permute(): return lax.ppermute(values, axes, [(i, i ^ step) for i in range(size)])]
    pallas_call x1 -> x2, Pallas kernels: 3.63 us -> 11.4 us  [the longest x1 9.07 us: on_device(): pl.pallas_call(query_kernel, grid=(dec_hidden.shape[1] // depth,), out_sh...]
    dot_general x1 -> x0, matrix products: 5.39 us -> none  [on_device(): queries = jnp.dot(dec_normed, query_weight, preferred_element_type=F32)]
    all_to_all x1 -> x0, waiting for transfers between devices: 4.9 us -> none  [on_device(): shares = lax.all_to_all(partial, ('y', 'zl'), 0, 0)]
    ppermute x34 -> x41, waiting for transfers between devices: 10.7 us -> 14.6 us  [xor_permute(): return lax.ppermute(values, axes, [(i, i ^ step) for i in range(size)])]
    all_to_all x1 -> x0, starting transfers between devices: 3.72 us -> none  [on_device(): shares = lax.all_to_all(partial, ('y', 'zl'), 0, 0)]
    reduce_sum x3 -> x0, other arithmetic: 2.37 us -> none  [the longest x2 2.28 us: rms_norm(): square_mean = jnp.mean(values * values, axis=-1, keepdims=True)]
  transfers between devices with their start and end apart: 36 -> 42, of which waited for: 10 -> 8; matrix products, arithmetic and copies ran while one was open for 7% -> 1% of each run, Pallas kernels for 10% -> 18%
where the time goes in v1:
time: 130 us; the launch traced here: 129 us
  starting transfers between devices  84.6 us (65%)
  Pallas kernels  25.3 us (19%)
  waiting for transfers between devices  14.6 us (11%)
  local copies, waits for them, and re-layouts  3.11 us (2%)
    ppermute x41, starting transfers between devices, xor_permute(): return lax.ppermute(values, axes, [(i, i ^ step) for i in range(size)])  82.9 us
    ppermute x41, waiting for transfers between devices, xor_permute(): return lax.ppermute(values, axes, [(i, i ^ step) for i in range(size)])  14.6 us
    pallas_call x4, Pallas kernels, on_device(): pl.pallas_call(decode_kernel, out_shape=jax.ShapeDtypeStruct((dec_rows, 4...  11.2 us
    pallas_call x1, Pallas kernels, on_device(): pl.pallas_call(query_kernel, grid=(dec_hidden.shape[1] // depth,), out_sh...  9.07 us
  transfers between devices with their start and end apart: 42, of which 8 were waited for; matrix products, arithmetic and copies ran while one was open for 1% of the time, Pallas kernels for 18%

profile of v1, /device:TPU:1, one launch (start us, length us, event | category | flops | bytes accessed | tf_op | source)
XLA Modules:
  0.0 128.5 jit_solution(5803394312556351684)
XLA Ops:
  1.7 8.8 %collective-permute-start.2 = (bf16[56,1280]{1,0:T(8,128)(2,1)S(1)}, bf16[56,1280]{1,0:T(8,128)(2,1)S(1)}, u32[]{:S(2)}, u32[]{:S(2)}) collective-permute-start(bf16[56,1280]{1,0:T(8,128)(2,1)S(1)} %fusion.1.refs_0_), channel_id=1, source_target_pairs={{0,4},{4,0},{8,12},{12,8},{16,20},{20,16},{24,28},{28,24},{1,5},{5... | collective-permute-start | bytes 430088 | tf_op jit(solution)/shard_map/ppermute | solution.py:31
  10.5 2.6 %collective-permute-start.3 = (bf16[56,1280]{1,0:T(8,128)(2,1)S(1)}, bf16[56,1280]{1,0:T(8,128)(2,1)S(1)}, u32[]{:S(2)}, u32[]{:S(2)}) collective-permute-start(bf16[56,1280]{1,0:T(8,128)(2,1)S(1)} %fusion.1.refs_0_), channel_id=1, source_target_pairs={{0,8},{4,12},{8,0},{12,4},{16,24},{20,28},{24,16},{28,20},{1,9},{5... | collective-permute-start | bytes 430088 | tf_op jit(solution)/shard_map/ppermute | solution.py:31
  14.0 5.0 %collective-permute-start.5 = (bf16[56,1280]{1,0:T(8,128)(2,1)S(1)}, bf16[56,1280]{1,0:T(8,128)(2,1)S(1)}, u32[]{:S(2)}, u32[]{:S(2)}) collective-permute-start(bf16[56,1280]{1,0:T(8,128)(2,1)S(1)} %fusion.1.refs_0_), channel_id=1, source_target_pairs={{0,16},{4,20},{8,24},{12,28},{16,0},{20,4},{24,8},{28,12},{1,17},{... | collective-permute-start | bytes 430088 | tf_op jit(solution)/shard_map/ppermute | solution.py:31
  19.0 3.1 %collective-permute-start.7 = (bf16[56,1280]{1,0:T(8,128)(2,1)S(1)}, bf16[56,1280]{1,0:T(8,128)(2,1)S(1)}, u32[]{:S(2)}, u32[]{:S(2)}) collective-permute-start(bf16[56,1280]{1,0:T(8,128)(2,1)S(1)} %fusion.1.refs_0_), channel_id=1, source_target_pairs={{0,24},{4,28},{8,16},{12,20},{16,8},{20,12},{24,0},{28,4},{1,25},{... | collective-permute-start | bytes 430088 | tf_op jit(solution)/shard_map/ppermute | solution.py:31
  24.7 5.9 %collective-permute-done.5.refs_4_ = bf16[56,1280]{1,0:T(8,128)(2,1)S(1)} collective-permute-done((bf16[56,1280]{1,0:T(8,128)(2,1)S(1)}, bf16[56,1280]{1,0:T(8,128)(2,1)S(1)}, u32[]{:S(2)}, u32[]{:S(2)}) %collective-permute-start.5) | collective-permute-done | bytes 143392 | tf_op jit(solution)/shard_map/ppermute | solution.py:31
  36.3 2.5 %collective-permute-start.24 = (bf16[256,256]{1,0:T(8,128)(2,1)S(1)}, bf16[256,256]{1,0:T(8,128)(2,1)S(1)}, u32[]{:S(2)}, u32[]{:S(2)}) collective-permute-start(bf16[256,256]{1,0:T(8,128)(2,1)S(1)} %get-tuple-element.11.refs_8_), channel_id=1, source_target_pairs={{0,2},{1,3},{2,0},{3,1},{4,6},{5,7},{6,4},{7,5},{8,10},{9,11},{10,... | collective-permute-start | bytes 393224 | tf_op jit(solution)/shard_map/ppermute | solution.py:31
  40.1 2.5 %collective-permute-start.11 = (bf16[320,256]{1,0:T(8,128)(2,1)S(1)}, bf16[320,256]{1,0:T(8,128)(2,1)S(1)}, u32[]{:S(2)}, u32[]{:S(2)}) collective-permute-start(bf16[320,256]{1,0:T(8,128)(2,1)S(1)} %get-tuple-element.10.refs_0_), channel_id=1, source_target_pairs={{0,3},{1,2},{2,1},{3,0},{4,7},{5,6},{6,5},{7,4},{8,11},{9,10},{10,... | collective-permute-start | bytes 491528 | tf_op jit(solution)/shard_map/ppermute | solution.py:31
  42.6 6.0 %collective-permute-start.12 = (bf16[320,256]{1,0:T(8,128)(2,1)S(1)}, bf16[320,256]{1,0:T(8,128)(2,1)S(1)}, u32[]{:S(2)}, u32[]{:S(2)}) collective-permute-start(bf16[320,256]{1,0:T(8,128)(2,1)S(1)} %get-tuple-element.10.refs_0_), channel_id=1, source_target_pairs={{0,32},{32,0},{1,33},{33,1},{2,34},{34,2},{3,35},{35,3},{4,36},{36... | collective-permute-start | bytes 491528 | tf_op jit(solution)/shard_map/ppermute | solution.py:31
  48.7 2.2 %collective-permute-start.13 = (bf16[320,256]{1,0:T(8,128)(2,1)S(1)}, bf16[320,256]{1,0:T(8,128)(2,1)S(1)}, u32[]{:S(2)}, u32[]{:S(2)}) collective-permute-start(bf16[320,256]{1,0:T(8,128)(2,1)S(1)} %collective-permute-done.9.refs_1_), channel_id=1, source_target_pairs={{0,32},{32,0},{1,33},{33,1},{2,34},{34,2},{3,35},{35,3},{4,36},{36... | collective-permute-start | bytes 491528 | tf_op jit(solution)/shard_map/ppermute | solution.py:31
  50.9 2.2 %collective-permute-start.14 = (bf16[320,256]{1,0:T(8,128)(2,1)S(1)}, bf16[320,256]{1,0:T(8,128)(2,1)S(1)}, u32[]{:S(2)}, u32[]{:S(2)}) collective-permute-start(bf16[320,256]{1,0:T(8,128)(2,1)S(1)} %collective-permute-done.10.refs_2_), channel_id=1, source_target_pairs={{0,32},{32,0},{1,33},{33,1},{2,34},{34,2},{3,35},{35,3},{4,36},{36... | collective-permute-start | bytes 491528 | tf_op jit(solution)/shard_map/ppermute | solution.py:31
  57.7 2.3 %shard_map.120.refs_0_ = bf16[256,256]{1,0:T(8,128)(2,1)S(1)} custom-call(bf16[2,256,80]{2,1,0:T(8,128)(2,1)S(1)} %get-tuple-element.9.q_ref, bf16[320,256]{1,0:T(8,128)(2,1)S(1)} %get-tuple-element.10.refs_0_, bf16[320,256]{1,0:T(8,128)(2,1)S(1)} %collective-permute-done.9.refs_1_, bf16[320,256]{1,0:T(8,128)(2,1)S(1)} %collective-permute-done.10.refs_2_, ...), custom_call_target="tpu_custom_call" | custom-call | tf_op jit(solution)/shard_map/pallas_call | solution.py:282
  64.9 2.1 %collective-permute-start.20 = (bf16[256,256]{1,0:T(8,128)(2,1)S(1)}, bf16[256,256]{1,0:T(8,128)(2,1)S(1)}, u32[]{:S(2)}, u32[]{:S(2)}) collective-permute-start(bf16[256,256]{1,0:T(8,128)(2,1)S(1)} %shard_map.120.refs_0_), channel_id=1, source_target_pairs={{0,20},{4,16},{8,28},{12,24},{16,4},{20,0},{24,12},{28,8},{1,21},{... | collective-permute-start | bytes 393224 | tf_op jit(solution)/shard_map/ppermute | solution.py:31
  68.5 3.2 %collective-permute-done.17.refs_2_ = bf16[256,256]{1,0:T(8,128)(2,1)S(1)} collective-permute-done((bf16[256,256]{1,0:T(8,128)(2,1)S(1)}, bf16[256,256]{1,0:T(8,128)(2,1)S(1)}, u32[]{:S(2)}, u32[]{:S(2)}) %collective-permute-start.17) | collective-permute-done | bytes 131104 | tf_op jit(solution)/shard_map/ppermute | solution.py:31
  72.8 9.1 %shard_map.118.query_ref = bf16[144,512]{1,0:T(8,128)(2,1)} custom-call(bf16[128,8192]{1,0:T(8,128)(2,1)} %x_ref.1, f32[1,8192]{1,0:T(1,128)} %bitcast.12, bf16[8192,512]{1,0:T(8,128)(2,1)} %weight_ref.1, f32[1,128]{1,0:T(1,128)} %bitcast.13, s32[1,128]{1,0:T(1,128)} %bitcast.14, s32[1,128]{1,0:T(1,128)} %bitcast.15), custom_call_target="tpu_custom_call" | custom-call | tf_op jit(solution)/shard_map/pallas_call | solution.py:234
  81.8 5.7 %collective-permute-start.38 = (bf16[144,512]{1,0:T(8,128)(2,1)}, bf16[144,512]{1,0:T(8,128)(2,1)S(1)}, u32[]{:S(2)}, u32[]{:S(2)}) collective-permute-start(bf16[144,512]{1,0:T(8,128)(2,1)} %shard_map.118.query_ref), channel_id=1, source_target_pairs={{0,64},{64,0},{128,192},{192,128},{1,65},{65,1},{129,193},{193,129... | collective-permute-start | bytes 442376 | tf_op jit(solution)/shard_map/ppermute | solution.py:31
  88.9 2.5 %collective-permute-start.31 = (bf16[256,256]{1,0:T(8,128)(2,1)S(1)}, bf16[256,256]{1,0:T(8,128)(2,1)S(1)}, u32[]{:S(2)}, u32[]{:S(2)}) collective-permute-start(bf16[256,256]{1,0:T(8,128)(2,1)S(1)} %shard_map.121.refs_0_), channel_id=1, source_target_pairs={{0,2},{1,3},{2,0},{3,1},{4,6},{5,7},{6,4},{7,5},{8,10},{9,11},{10,... | collective-permute-start | bytes 393224 | tf_op jit(solution)/shard_map/ppermute | solution.py:31
  92.7 3.5 %collective-permute-start.33 = (bf16[256,256]{1,0:T(8,128)(2,1)S(1)}, bf16[256,256]{1,0:T(8,128)(2,1)S(1)}, u32[]{:S(2)}, u32[]{:S(2)}) collective-permute-start(bf16[256,256]{1,0:T(8,128)(2,1)S(1)} %shard_map.121.refs_0_), channel_id=1, source_target_pairs={{0,32},{32,0},{1,33},{33,1},{2,34},{34,2},{3,35},{35,3},{4,36},{36... | collective-permute-start | bytes 393224 | tf_op jit(solution)/shard_map/ppermute | solution.py:31
  96.3 5.4 %collective-permute-start = (bf16[144,512]{1,0:T(8,128)(2,1)S(1)}, bf16[144,512]{1,0:T(8,128)(2,1)S(1)}, u32[]{:S(2)}, u32[]{:S(2)}) collective-permute-start(bf16[144,512]{1,0:T(8,128)(2,1)S(1)} %copy-done.3), channel_id=1, source_target_pairs={{0,128},{64,192},{128,0},{192,64},{1,129},{65,193},{129,1},{193,65... | collective-permute-start | bytes 442376 | tf_op jit(solution)/shard_map/ppermute | solution.py:31
  105.1 2.8 %shard_map.123 = bf16[128,512]{1,0:T(8,128)(2,1)S(1)} custom-call(s32[3]{0:T(128)S(1)} %pad_add_fusion.place_ref, bf16[144,512]{1,0:T(8,128)(2,1)S(1)} %collective-permute-done.38.query_ref, bf16[256,256]{1,0:T(8,128)(2,1)S(1)} %shard_map.121.refs_0_, bf16[256,256]{1,0:T(8,128)(2,1)S(1)} %collective-permute-done.30.refs_1_, ...), custom_call_target="tpu_custom_call" | custom-call | tf_op jit(solution)/shard_map/pallas_call | solution.py:303
  109.4 2.8 %shard_map.122 = bf16[128,512]{1,0:T(8,128)(2,1)S(1)} custom-call(s32[3]{0:T(128)S(1)} %pad_add_fusion.place_ref, bf16[144,512]{1,0:T(8,128)(2,1)S(1)} %collective-permute-done.query_ref, bf16[256,256]{1,0:T(8,128)(2,1)S(1)} %shard_map.121.refs_0_, bf16[256,256]{1,0:T(8,128)(2,1)S(1)} %collective-permute-done.30.refs_1_, ...), custom_call_target="tpu_custom_call" | custom-call | tf_op jit(solution)/shard_map/pallas_call | solution.py:303
  112.2 4.5 %collective-permute-start.37 = (bf16[128,512]{1,0:T(8,128)(2,1)S(1)}, bf16[128,512]{1,0:T(8,128)(2,1)S(1)}, u32[]{:S(2)}, u32[]{:S(2)}) collective-permute-start(bf16[128,512]{1,0:T(8,128)(2,1)S(1)} %shard_map.122), channel_id=1, source_target_pairs={{0,128},{64,192},{128,0},{192,64},{1,129},{65,193},{129,1},{193,65... | collective-permute-start | bytes 393224 | tf_op jit(solution)/shard_map/ppermute | solution.py:31
  116.7 2.8 %shard_map.124 = bf16[128,512]{1,0:T(8,128)(2,1)S(1)} custom-call(s32[3]{0:T(128)S(1)} %pad_add_fusion.place_ref, bf16[144,512]{1,0:T(8,128)(2,1)S(1)} %collective-permute-done.40.query_ref, bf16[256,256]{1,0:T(8,128)(2,1)S(1)} %shard_map.121.refs_0_, bf16[256,256]{1,0:T(8,128)(2,1)S(1)} %collective-permute-done.30.refs_1_, ...), custom_call_target="tpu_custom_call" | custom-call | tf_op jit(solution)/shard_map/pallas_call | solution.py:303
  121.6 2.8 %shard_map.125 = bf16[128,512]{1,0:T(8,128)(2,1)S(1)} custom-call(s32[3]{0:T(128)S(1)} %pad_add_fusion.place_ref, bf16[144,512]{1,0:T(8,128)(2,1)S(1)} %copy-done.3, bf16[256,256]{1,0:T(8,128)(2,1)S(1)} %shard_map.121.refs_0_, bf16[256,256]{1,0:T(8,128)(2,1)S(1)} %collective-permute-done.30.refs_1_, bf16[256,256]{1,0:T(8,128)(2,1)S(1)} %collective-permute-done.31.refs_2_, ...), custom_call_target="tpu_custom_call" | custom-call | tf_op jit(solution)/shard_map/pallas_call | solution.py:303
  124.4 3.5 %collective-permute-done.41 = bf16[128,512]{1,0:T(8,128)(2,1)S(1)} collective-permute-done((bf16[128,512]{1,0:T(8,128)(2,1)S(1)}, bf16[128,512]{1,0:T(8,128)(2,1)S(1)}, u32[]{:S(2)}, u32[]{:S(2)}) %collective-permute-start.41) | collective-permute-done | bytes 131104 | tf_op jit(solution)/shard_map/ppermute | solution.py:31
  (83 shorter events, 34.9 us)
Async XLA Ops:
  1.7 17.3 %collective-permute-start.2 = (bf16[56,1280]{1,0:T(8,128)(2,1)S(1)}, bf16[56,1280]{1,0:T(8,128)(2,1)S(1)}, u32[]{:S(2)}, u32[]{:S(2)}) collective-permute-start(bf16[56,1280]{1,0:T(8,128)(2,1)S(1)} %fusion.1.refs_0_), channel_id=1, source_target_pairs={{0,4},{4,0},{8,12},{12,8},{16,20},{20,16},{24,28},{28,24},{1,5},{5... | collective-permute-start | bytes 430088 | tf_op jit(solution)/shard_map/ppermute | solution.py:31
  10.5 11.6 %collective-permute-start.3 = (bf16[56,1280]{1,0:T(8,128)(2,1)S(1)}, bf16[56,1280]{1,0:T(8,128)(2,1)S(1)}, u32[]{:S(2)}, u32[]{:S(2)}) collective-permute-start(bf16[56,1280]{1,0:T(8,128)(2,1)S(1)} %fusion.1.refs_0_), channel_id=1, source_target_pairs={{0,8},{4,12},{8,0},{12,4},{16,24},{20,28},{24,16},{28,20},{1,9},{5... | collective-permute-start | bytes 430088 | tf_op jit(solution)/shard_map/ppermute | solution.py:31
  13.1 11.6 %collective-permute-start.4 = (bf16[56,1280]{1,0:T(8,128)(2,1)S(1)}, bf16[56,1280]{1,0:T(8,128)(2,1)S(1)}, u32[]{:S(2)}, u32[]{:S(2)}) collective-permute-start(bf16[56,1280]{1,0:T(8,128)(2,1)S(1)} %fusion.1.refs_0_), channel_id=1, source_target_pairs={{0,12},{4,8},{8,4},{12,0},{16,28},{20,24},{24,20},{28,16},{1,13},{... | collective-permute-start | bytes 430088 | tf_op jit(solution)/shard_map/ppermute | solution.py:31
  14.0 16.7 %collective-permute-start.5 = (bf16[56,1280]{1,0:T(8,128)(2,1)S(1)}, bf16[56,1280]{1,0:T(8,128)(2,1)S(1)}, u32[]{:S(2)}, u32[]{:S(2)}) collective-permute-start(bf16[56,1280]{1,0:T(8,128)(2,1)S(1)} %fusion.1.refs_0_), channel_id=1, source_target_pairs={{0,16},{4,20},{8,24},{12,28},{16,0},{20,4},{24,8},{28,12},{1,17},{... | collective-permute-start | bytes 430088 | tf_op jit(solution)/shard_map/ppermute | solution.py:31
  19.0 11.7 %collective-permute-start.6 = (bf16[56,1280]{1,0:T(8,128)(2,1)S(1)}, bf16[56,1280]{1,0:T(8,128)(2,1)S(1)}, u32[]{:S(2)}, u32[]{:S(2)}) collective-permute-start(bf16[56,1280]{1,0:T(8,128)(2,1)S(1)} %fusion.1.refs_0_), channel_id=1, source_target_pairs={{0,20},{4,16},{8,28},{12,24},{16,4},{20,0},{24,12},{28,8},{1,21},{... | collective-permute-start | bytes 430088 | tf_op jit(solution)/shard_map/ppermute | solution.py:31
  19.0 12.1 %collective-permute-start.7 = (bf16[56,1280]{1,0:T(8,128)(2,1)S(1)}, bf16[56,1280]{1,0:T(8,128)(2,1)S(1)}, u32[]{:S(2)}, u32[]{:S(2)}) collective-permute-start(bf16[56,1280]{1,0:T(8,128)(2,1)S(1)} %fusion.1.refs_0_), channel_id=1, source_target_pairs={{0,24},{4,28},{8,16},{12,20},{16,8},{20,12},{24,0},{28,4},{1,25},{... | collective-permute-start | bytes 430088 | tf_op jit(solution)/shard_map/ppermute | solution.py:31
  36.3 12.3 %collective-permute-start.24 = (bf16[256,256]{1,0:T(8,128)(2,1)S(1)}, bf16[256,256]{1,0:T(8,128)(2,1)S(1)}, u32[]{:S(2)}, u32[]{:S(2)}) collective-permute-start(bf16[256,256]{1,0:T(8,128)(2,1)S(1)} %get-tuple-element.11.refs_8_), channel_id=1, source_target_pairs={{0,2},{1,3},{2,0},{3,1},{4,6},{5,7},{6,4},{7,5},{8,10},{9,11},{10,... | collective-permute-start | bytes 393224 | tf_op jit(solution)/shard_map/ppermute | solution.py:31
  38.7 12.2 %collective-permute-start.10 = (bf16[320,256]{1,0:T(8,128)(2,1)S(1)}, bf16[320,256]{1,0:T(8,128)(2,1)S(1)}, u32[]{:S(2)}, u32[]{:S(2)}) collective-permute-start(bf16[320,256]{1,0:T(8,128)(2,1)S(1)} %get-tuple-element.10.refs_0_), channel_id=1, source_target_pairs={{0,2},{1,3},{2,0},{3,1},{4,6},{5,7},{6,4},{7,5},{8,10},{9,11},{10,... | collective-permute-start | bytes 491528 | tf_op jit(solution)/shard_map/ppermute | solution.py:31
  40.1 13.0 %collective-permute-start.11 = (bf16[320,256]{1,0:T(8,128)(2,1)S(1)}, bf16[320,256]{1,0:T(8,128)(2,1)S(1)}, u32[]{:S(2)}, u32[]{:S(2)}) collective-permute-start(bf16[320,256]{1,0:T(8,128)(2,1)S(1)} %get-tuple-element.10.refs_0_), channel_id=1, source_target_pairs={{0,3},{1,2},{2,1},{3,0},{4,7},{5,6},{6,5},{7,4},{8,11},{9,10},{10,... | collective-permute-start | bytes 491528 | tf_op jit(solution)/shard_map/ppermute | solution.py:31
  42.6 14.3 %collective-permute-start.12 = (bf16[320,256]{1,0:T(8,128)(2,1)S(1)}, bf16[320,256]{1,0:T(8,128)(2,1)S(1)}, u32[]{:S(2)}, u32[]{:S(2)}) collective-permute-start(bf16[320,256]{1,0:T(8,128)(2,1)S(1)} %get-tuple-element.10.refs_0_), channel_id=1, source_target_pairs={{0,32},{32,0},{1,33},{33,1},{2,34},{34,2},{3,35},{35,3},{4,36},{36... | collective-permute-start | bytes 491528 | tf_op jit(solution)/shard_map/ppermute | solution.py:31
  61.6 20.2 %collective-permute-start.18 = (bf16[256,256]{1,0:T(8,128)(2,1)S(1)}, bf16[256,256]{1,0:T(8,128)(2,1)S(1)}, u32[]{:S(2)}, u32[]{:S(2)}) collective-permute-start(bf16[256,256]{1,0:T(8,128)(2,1)S(1)} %shard_map.120.refs_0_), channel_id=1, source_target_pairs={{0,12},{4,8},{8,4},{12,0},{16,28},{20,24},{24,20},{28,16},{1,13},{... | collective-permute-start | bytes 393224 | tf_op jit(solution)/shard_map/ppermute | solution.py:31
  62.9 24.7 %collective-permute-start.19 = (bf16[256,256]{1,0:T(8,128)(2,1)S(1)}, bf16[256,256]{1,0:T(8,128)(2,1)S(1)}, u32[]{:S(2)}, u32[]{:S(2)}) collective-permute-start(bf16[256,256]{1,0:T(8,128)(2,1)S(1)} %shard_map.120.refs_0_), channel_id=1, source_target_pairs={{0,16},{4,20},{8,24},{12,28},{16,0},{20,4},{24,8},{28,12},{1,17},{... | collective-permute-start | bytes 393224 | tf_op jit(solution)/shard_map/ppermute | solution.py:31
  64.9 22.7 %collective-permute-start.20 = (bf16[256,256]{1,0:T(8,128)(2,1)S(1)}, bf16[256,256]{1,0:T(8,128)(2,1)S(1)}, u32[]{:S(2)}, u32[]{:S(2)}) collective-permute-start(bf16[256,256]{1,0:T(8,128)(2,1)S(1)} %shard_map.120.refs_0_), channel_id=1, source_target_pairs={{0,20},{4,16},{8,28},{12,24},{16,4},{20,0},{24,12},{28,8},{1,21},{... | collective-permute-start | bytes 393224 | tf_op jit(solution)/shard_map/ppermute | solution.py:31
  67.0 20.6 %collective-permute-start.21 = (bf16[256,256]{1,0:T(8,128)(2,1)S(1)}, bf16[256,256]{1,0:T(8,128)(2,1)S(1)}, u32[]{:S(2)}, u32[]{:S(2)}) collective-permute-start(bf16[256,256]{1,0:T(8,128)(2,1)S(1)} %shard_map.120.refs_0_), channel_id=1, source_target_pairs={{0,24},{4,28},{8,16},{12,20},{16,8},{20,12},{24,0},{28,4},{1,25},{... | collective-permute-start | bytes 393224 | tf_op jit(solution)/shard_map/ppermute | solution.py:31
  71.7 16.0 %collective-permute-start.22 = (bf16[256,256]{1,0:T(8,128)(2,1)S(1)}, bf16[256,256]{1,0:T(8,128)(2,1)S(1)}, u32[]{:S(2)}, u32[]{:S(2)}) collective-permute-start(bf16[256,256]{1,0:T(8,128)(2,1)S(1)} %shard_map.120.refs_0_), channel_id=1, source_target_pairs={{0,28},{4,24},{8,20},{12,16},{16,12},{20,8},{24,4},{28,0},{1,29},{... | collective-permute-start | bytes 393224 | tf_op jit(solution)/shard_map/ppermute | solution.py:31
  81.8 14.4 %collective-permute-start.38 = (bf16[144,512]{1,0:T(8,128)(2,1)}, bf16[144,512]{1,0:T(8,128)(2,1)S(1)}, u32[]{:S(2)}, u32[]{:S(2)}) collective-permute-start(bf16[144,512]{1,0:T(8,128)(2,1)} %shard_map.118.query_ref), channel_id=1, source_target_pairs={{0,64},{64,0},{128,192},{192,128},{1,65},{65,1},{129,193},{193,129... | collective-permute-start | bytes 442376 | tf_op jit(solution)/shard_map/ppermute | solution.py:31
  88.8 12.9 %collective-permute-start.30 = (bf16[256,256]{1,0:T(8,128)(2,1)S(1)}, bf16[256,256]{1,0:T(8,128)(2,1)S(1)}, u32[]{:S(2)}, u32[]{:S(2)}) collective-permute-start(bf16[256,256]{1,0:T(8,128)(2,1)S(1)} %shard_map.121.refs_0_), channel_id=1, source_target_pairs={{0,1},{1,0},{2,3},{3,2},{4,5},{5,4},{6,7},{7,6},{8,9},{9,8},{10,11... | collective-permute-start | bytes 393224 | tf_op jit(solution)/shard_map/ppermute | solution.py:31
  88.9 13.5 %collective-permute-start.31 = (bf16[256,256]{1,0:T(8,128)(2,1)S(1)}, bf16[256,256]{1,0:T(8,128)(2,1)S(1)}, u32[]{:S(2)}, u32[]{:S(2)}) collective-permute-start(bf16[256,256]{1,0:T(8,128)(2,1)S(1)} %shard_map.121.refs_0_), channel_id=1, source_target_pairs={{0,2},{1,3},{2,0},{3,1},{4,6},{5,7},{6,4},{7,5},{8,10},{9,11},{10,... | collective-permute-start | bytes 393224 | tf_op jit(solution)/shard_map/ppermute | solution.py:31
  91.4 12.0 %collective-permute-start.32 = (bf16[256,256]{1,0:T(8,128)(2,1)S(1)}, bf16[256,256]{1,0:T(8,128)(2,1)S(1)}, u32[]{:S(2)}, u32[]{:S(2)}) collective-permute-start(bf16[256,256]{1,0:T(8,128)(2,1)S(1)} %shard_map.121.refs_0_), channel_id=1, source_target_pairs={{0,3},{1,2},{2,1},{3,0},{4,7},{5,6},{6,5},{7,4},{8,11},{9,10},{10,... | collective-permute-start | bytes 393224 | tf_op jit(solution)/shard_map/ppermute | solution.py:31
  92.7 11.0 %collective-permute-start.33 = (bf16[256,256]{1,0:T(8,128)(2,1)S(1)}, bf16[256,256]{1,0:T(8,128)(2,1)S(1)}, u32[]{:S(2)}, u32[]{:S(2)}) collective-permute-start(bf16[256,256]{1,0:T(8,128)(2,1)S(1)} %shard_map.121.refs_0_), channel_id=1, source_target_pairs={{0,32},{32,0},{1,33},{33,1},{2,34},{34,2},{3,35},{35,3},{4,36},{36... | collective-permute-start | bytes 393224 | tf_op jit(solution)/shard_map/ppermute | solution.py:31
  96.3 13.1 %collective-permute-start = (bf16[144,512]{1,0:T(8,128)(2,1)S(1)}, bf16[144,512]{1,0:T(8,128)(2,1)S(1)}, u32[]{:S(2)}, u32[]{:S(2)}) collective-permute-start(bf16[144,512]{1,0:T(8,128)(2,1)S(1)} %copy-done.3), channel_id=1, source_target_pairs={{0,128},{64,192},{128,0},{192,64},{1,129},{65,193},{129,1},{193,65... | collective-permute-start | bytes 442376 | tf_op jit(solution)/shard_map/ppermute | solution.py:31
  101.7 15.0 %collective-permute-start.40 = (bf16[144,512]{1,0:T(8,128)(2,1)S(1)}, bf16[144,512]{1,0:T(8,128)(2,1)S(1)}, u32[]{:S(2)}, u32[]{:S(2)}) collective-permute-start(bf16[144,512]{1,0:T(8,128)(2,1)S(1)} %copy-done.3), channel_id=1, source_target_pairs={{0,192},{64,128},{128,64},{192,0},{1,193},{65,129},{129,65},{193,1... | collective-permute-start | bytes 442376 | tf_op jit(solution)/shard_map/ppermute | solution.py:31
  107.9 16.5 %collective-permute-start.39 = (bf16[128,512]{1,0:T(8,128)(2,1)S(1)}, bf16[128,512]{1,0:T(8,128)(2,1)S(1)}, u32[]{:S(2)}, u32[]{:S(2)}) collective-permute-start(bf16[128,512]{1,0:T(8,128)(2,1)S(1)} %shard_map.123), channel_id=1, source_target_pairs={{0,64},{64,0},{128,192},{192,128},{1,65},{65,1},{129,193},{193,129... | collective-permute-start | bytes 393224 | tf_op jit(solution)/shard_map/ppermute | solution.py:31
  112.2 12.2 %collective-permute-start.37 = (bf16[128,512]{1,0:T(8,128)(2,1)S(1)}, bf16[128,512]{1,0:T(8,128)(2,1)S(1)}, u32[]{:S(2)}, u32[]{:S(2)}) collective-permute-start(bf16[128,512]{1,0:T(8,128)(2,1)S(1)} %shard_map.122), channel_id=1, source_target_pairs={{0,128},{64,192},{128,0},{192,64},{1,129},{65,193},{129,1},{193,65... | collective-permute-start | bytes 393224 | tf_op jit(solution)/shard_map/ppermute | solution.py:31
  (23 other events, 142.3 us)

commit v2 on v1

--- a/solution.py
+++ b/solution.py
@@ -43,7 +43,7 @@
 
 def qkv_kernel(me_ref, *refs):
     pieces, refs = refs[:TENSOR], refs[TENSOR:]
-    gain_ref, weight_ref, cross_ref, q_ref, kv_ref, fold_ref, base_ref, normed, raw, out_rows = refs
+    gain_ref, weight_ref, cross_ref, q_ref, kv_ref, base_ref, normed, raw, out_rows = refs
     me = me_ref[0]
     rows = raw.shape[0] // TENSOR
     for step in range(TENSOR):
@@ -69,7 +69,8 @@
     for head in range(2):
         q_ref[head] = q[:, head * EHD : (head + 1) * EHD].astype(BF16)
     cross = cross_ref[...]
-    fold_ref[...] = jnp.dot(out_rows[...], cross, preferred_element_type=F32).astype(BF16)
+    fold = jnp.dot(out_rows[...], cross, preferred_element_type=F32)
+    kv_ref[4 * EHD :, :] = fold.astype(BF16)
     base_ref[...] = jnp.dot(raw[...], cross, preferred_element_type=F32)
 
 
@@ -115,7 +116,8 @@
         owner = jnp.bitwise_xor(c, k // 4) * 4 + jnp.bitwise_xor(x, k % 4)
         for t in range(TENSOR):
             low = pl.multiple_of(t * size + owner * SLOT, SLOT)
-            weight[pl.ds(low, SLOT), :] = folds[k][t * SLOT : (t + 1) * SLOT, :]
+            first = 4 * EHD + t * SLOT
+            weight[pl.ds(low, SLOT), :] = folds[k][first : first + SLOT, :]
     proj = base_ref[...]
     for step in range(TENSOR):
         low = pl.multiple_of(jnp.bitwise_xor(me, step) * size, size)
@@ -129,14 +131,17 @@
     out_ref[:, HD:] = proj[:, HD:].astype(BF16)
 
 
-def query_kernel(x_ref, gain_ref, weight_ref, head_gain_ref, image_ref, count_ref, out_ref, total, inverse):
-    step = pl.program_id(0)
-    rows = x_ref.shape[0]
+def query_part(x_ref, gain_ref, weight_ref, total, inverse):
     depth = weight_ref.shape[0]
-
-    @pl.when(step == 0)
+    columns = pl.ds(pl.multiple_of(pl.program_id(0) * depth, depth), depth)
+    normed = x_ref[:, columns].astype(F32) * inverse[:, 0:1] * gain_ref[:, columns]
+    total[...] += jnp.dot(normed.astype(BF16), weight_ref[...], preferred_element_type=F32)
+
+
+def query_first_kernel(x_ref, gain_ref, weight_ref, total, inverse):
+    @pl.when(pl.program_id(0) == 0)
     def _():
-        square = jnp.zeros((rows, 128), F32)
+        square = jnp.zeros((x_ref.shape[0], 128), F32)
         for low in range(0, x_ref.shape[1], 128):
             part = x_ref[:, low : low + 128].astype(F32)
             square = square + part * part
@@ -144,11 +149,21 @@
         inverse[...] = jnp.broadcast_to(lax.rsqrt(mean + EPSILON), inverse.shape)
         total[...] = jnp.zeros_like(total)
 
-    columns = pl.ds(pl.multiple_of(step * depth, depth), depth)
-    normed = x_ref[:, columns].astype(F32) * inverse[:, 0:1] * gain_ref[:, columns]
-    total[...] += jnp.dot(normed.astype(BF16), weight_ref[...], preferred_element_type=F32)
-
-    @pl.when(step == pl.num_programs(0) - 1)
+    query_part(x_ref, gain_ref, weight_ref, total, inverse)
+
+
+def query_last_kernel(
+    x_ref, gain_ref, weight_ref, begun, inverse, head_gain_ref, image_ref, count_ref, out_ref, total
+):
+    rows = x_ref.shape[0]
+
+    @pl.when(pl.program_id(0) == 0)
+    def _():
+        total[...] = begun[...]
+
+    query_part(x_ref, gain_ref, weight_ref, total, inverse)
+
+    @pl.when(pl.program_id(0) == pl.num_programs(0) - 1)
     def _():
         for head in range(4):
             q = total[:, head * HD : (head + 1) * HD]
@@ -229,27 +244,48 @@
     own = image_permute(patches)
 
     dec_rows = dec_hidden.shape[0]
-    depth = 1024
-    query_width = query_weight.shape[1]
+    depth, steps = 1024, 4
+    dec_width, query_width = query_weight.shape
+    fixed = lambda shape: pl.BlockSpec(shape, lambda i: (0, 0))
+    gain_view = dec_gain.reshape(1, -1)
+    begun, inverse = pl.pallas_call(
+        query_first_kernel,
+        grid=(steps,),
+        out_shape=(
+            jax.ShapeDtypeStruct((dec_rows, query_width), F32),
+            jax.ShapeDtypeStruct((dec_rows, 128), F32),
+        ),
+        in_specs=[
+            fixed((dec_rows, dec_width)),
+            fixed((1, dec_width)),
+            pl.BlockSpec((depth, query_width), lambda i: (i, 0)),
+        ],
+        out_specs=(fixed((dec_rows, query_width)), fixed((dec_rows, 128))),
+        compiler_params=limits(56),
+    )(dec_hidden, gain_view, query_weight)
     message = pl.pallas_call(
-        query_kernel,
-        grid=(dec_hidden.shape[1] // depth,),
+        query_last_kernel,
+        grid=(steps,),
         out_shape=jax.ShapeDtypeStruct((dec_rows + 16, query_width), BF16),
         in_specs=[
-            pl.BlockSpec(dec_hidden.shape, lambda i: (0, 0)),
-            pl.BlockSpec((1, dec_hidden.shape[1]), lambda i: (0, 0)),
-            pl.BlockSpec((depth, query_width), lambda i: (i, 0)),
-            pl.BlockSpec((1, HD), lambda i: (0, 0)),
-            pl.BlockSpec((1, dec_rows), lambda i: (0, 0)),
-            pl.BlockSpec((1, dec_rows), lambda i: (0, 0)),
+            pl.BlockSpec((dec_rows, dec_width // 2), lambda i: (0, 1)),
+            pl.BlockSpec((1, dec_width // 2), lambda i: (0, 1)),
+            pl.BlockSpec((depth, query_width), lambda i: (i + steps, 0)),
+            fixed((dec_rows, query_width)),
+            fixed((dec_rows, 128)),
+            fixed((1, HD)),
+            fixed((1, dec_rows)),
+            fixed((1, dec_rows)),
         ],
-        out_specs=pl.BlockSpec((dec_rows + 16, query_width), lambda i: (0, 0)),
-        scratch_shapes=[pltpu.VMEM((dec_rows, query_width), F32), pltpu.VMEM((dec_rows, 128), F32)],
+        out_specs=fixed((dec_rows + 16, query_width)),
+        scratch_shapes=[pltpu.VMEM((dec_rows, query_width), F32)],
         compiler_params=limits(56),
     )(
         dec_hidden,
-        dec_gain.reshape(1, -1),
+        gain_view,
         query_weight,
+        begun,
+        inverse,
         query_gain.reshape(1, -1),
         image_of_row.reshape(1, -1),
         valid_count.reshape(1, -1),
@@ -258,24 +294,24 @@
     owner = lax.axis_index("c") * XS + lax.axis_index("x")
     share = lax.dynamic_slice_in_dim(enc_out, owner * SHARE, SHARE, axis=0)
     share = jnp.pad(share, ((0, 24 - SHARE), (0, 0)))
+    gain_row = enc_gain.reshape(1, -1)
     pieces = gather_tensor(jnp.concatenate([own, share], axis=0))
-    q, kv, fold, base = pl.pallas_call(
+    q, kv, base = pl.pallas_call(
         qkv_kernel,
         out_shape=(
             jax.ShapeDtypeStruct((2, rows, EHD), BF16),
-            jax.ShapeDtypeStruct((4 * EHD, rows), BF16),
-            jax.ShapeDtypeStruct((TENSOR * SLOT, 2 * HD), BF16),
+            jax.ShapeDtypeStruct((4 * EHD + TENSOR * SLOT, rows), BF16),
             jax.ShapeDtypeStruct((rows, 2 * HD), F32),
         ),
         in_specs=[smem()] + vmem(TENSOR + 3),
-        out_specs=tuple(vmem(4)),
+        out_specs=tuple(vmem(3)),
         scratch_shapes=[
             pltpu.VMEM((rows, width), BF16),
             pltpu.VMEM((rows, width), BF16),
             pltpu.VMEM((TENSOR * SLOT, width), BF16),
         ],
         compiler_params=limits(16),
-    )(me, *pieces, enc_gain.reshape(1, -1), enc_qkv.transpose(0, 2, 1), cross_kv)
+    )(me, *pieces, gain_row, enc_qkv.transpose(0, 2, 1), cross_kv)
     kv_pieces = gather_xc(kv)
     every_query = [message] + [xor_permute(message, "zh", ZH, k) for k in range(1, ZH)]
 
@@ -288,7 +324,6 @@
         compiler_params=limits(20),
     )(q, *kv_pieces)
     attended_pieces = gather_tensor(attended)
-    folds = gather_xc(fold)
     slab = pl.pallas_call(
         cross_kernel,
         out_shape=jax.ShapeDtypeStruct((rows, 2 * HD), BF16),
@@ -296,7 +331,7 @@
         out_specs=vmem(1)[0],
         scratch_shapes=[pltpu.VMEM((TENSOR * 8 * SLOT, 2 * HD), BF16)],
         compiler_params=limits(12),
-    )(me, place, *attended_pieces, *folds, base, key_gain.reshape(1, -1))
+    )(me, place, *attended_pieces, *kv_pieces, base, key_gain.reshape(1, -1))
     slabs = gather_xc(slab)
     result = None
     for k in (2, 1, 3, 0):

time: 130 us -> 131 us (level)
  the two profiles are of different devices: /device:TPU:1 before, /device:TPU:38 now
where the time goes in v2:
time: 131 us; the launch traced here: 130 us
  starting transfers between devices  62.9 us (48%)
  waiting for transfers between devices  36.2 us (28%)
  Pallas kernels  27.2 us (21%)
  local copies, waits for them, and re-layouts  3.11 us (2%)
    ppermute x34, starting transfers between devices, xor_permute(): return lax.ppermute(values, axes, [(i, i ^ step) for i in range(size)])  58.9 us
    ppermute x34, waiting for transfers between devices, xor_permute(): return lax.ppermute(values, axes, [(i, i ^ step) for i in range(size)])  31.2 us
    pallas_call x4, Pallas kernels, on_device(): pl.pallas_call(decode_kernel, out_shape=jax.ShapeDtypeStruct((dec_rows, 4...  11.2 us
    pallas_call x1, Pallas kernels, on_device(): pl.pallas_call(query_first_kernel, grid=(steps,), out_shape=(jax.ShapeDty...  5.55 us
    ppermute x1, waiting for transfers between devices, image_permute(): return lax.ppermute(values, ('zh', 'y', 'zl'), pairs)  5.06 us
    pallas_call x1, Pallas kernels, on_device(): pl.pallas_call(query_last_kernel, grid=(steps,), out_shape=jax.ShapeDtype...  4.91 us
    ppermute x1, starting transfers between devices, image_permute(): return lax.ppermute(values, ('zh', 'y', 'zl'), pairs)  3.94 us
  transfers between devices with their start and end apart: 35, of which 17 were waited for; matrix products, arithmetic and copies ran while one was open for 1% of the time, Pallas kernels for 18%

profile of v2, /device:TPU:38, one launch (start us, length us, event | category | flops | bytes accessed | tf_op | source)
XLA Modules:
  0.0 130.4 jit_solution(18378276940957591835)
XLA Ops:
  0.0 3.9 %collective-permute-start.1 = (bf16[32,1280]{1,0:T(8,128)(2,1)}, bf16[32,1280]{1,0:T(8,128)(2,1)S(1)}, u32[]{:S(2)}, u32[]{:S(2)}) collective-permute-start(bf16[32,1280]{1,0:T(8,128)(2,1)} %param.12), channel_id=1, source_target_pairs={{0,0},{4,64},{8,128},{12,192},{16,4},{20,68},{24,132},{28,196},{64... | collective-permute-start | bytes 245768 | tf_op jit(solution)/shard_map/ppermute | solution.py:41
  4.0 5.1 %collective-permute-done.1 = bf16[32,1280]{1,0:T(8,128)(2,1)S(1)} collective-permute-done((bf16[32,1280]{1,0:T(8,128)(2,1)}, bf16[32,1280]{1,0:T(8,128)(2,1)S(1)}, u32[]{:S(2)}, u32[]{:S(2)}) %collective-permute-start.1) | collective-permute-done | bytes 81952 | tf_op jit(solution)/shard_map/ppermute | solution.py:41
  9.1 7.6 %collective-permute-start.8 = (bf16[56,1280]{1,0:T(8,128)(2,1)S(1)}, bf16[56,1280]{1,0:T(8,128)(2,1)S(1)}, u32[]{:S(2)}, u32[]{:S(2)}) collective-permute-start(bf16[56,1280]{1,0:T(8,128)(2,1)S(1)} %fusion.1.refs_0_), channel_id=1, source_target_pairs={{0,28},{4,24},{8,20},{12,16},{16,12},{20,8},{24,4},{28,0},{1,29},{... | collective-permute-start | bytes 430088 | tf_op jit(solution)/shard_map/ppermute | solution.py:31
  16.6 3.6 %collective-permute-start.6 = (bf16[56,1280]{1,0:T(8,128)(2,1)S(1)}, bf16[56,1280]{1,0:T(8,128)(2,1)S(1)}, u32[]{:S(2)}, u32[]{:S(2)}) collective-permute-start(bf16[56,1280]{1,0:T(8,128)(2,1)S(1)} %fusion.1.refs_0_), channel_id=1, source_target_pairs={{0,20},{4,16},{8,28},{12,24},{16,4},{20,0},{24,12},{28,8},{1,21},{... | collective-permute-start | bytes 430088 | tf_op jit(solution)/shard_map/ppermute | solution.py:31
  23.1 4.0 %collective-permute-done.7.refs_6_ = bf16[56,1280]{1,0:T(8,128)(2,1)S(1)} collective-permute-done((bf16[56,1280]{1,0:T(8,128)(2,1)S(1)}, bf16[56,1280]{1,0:T(8,128)(2,1)S(1)}, u32[]{:S(2)}, u32[]{:S(2)}) %collective-permute-start.7) | collective-permute-done | bytes 143392 | tf_op jit(solution)/shard_map/ppermute | solution.py:31
  36.7 2.4 %collective-permute-start.10 = (bf16[576,256]{1,0:T(8,128)(2,1)S(1)}, bf16[576,256]{1,0:T(8,128)(2,1)S(1)}, u32[]{:S(2)}, u32[]{:S(2)}) collective-permute-start(bf16[576,256]{1,0:T(8,128)(2,1)S(1)} %get-tuple-element.13.refs_0_.refs_8_), channel_id=1, source_target_pairs={{0,2},{1,3},{2,0},{3,1},{4,6},{5,7},{6,4},{7,5},{8,10},{9,11},{10,... | collective-permute-start | bytes 884744 | tf_op jit(solution)/shard_map/ppermute | solution.py:31
  40.4 10.4 %collective-permute-done.11.refs_3_.refs_11_ = bf16[576,256]{1,0:T(8,128)(2,1)S(1)} collective-permute-done((bf16[576,256]{1,0:T(8,128)(2,1)S(1)}, bf16[576,256]{1,0:T(8,128)(2,1)S(1)}, u32[]{:S(2)}, u32[]{:S(2)}) %collective-permute-start.11) | collective-permute-done | bytes 294944 | tf_op jit(solution)/shard_map/ppermute | solution.py:31
  55.5 2.5 %collective-permute-start.22 = (bf16[256,256]{1,0:T(8,128)(2,1)S(1)}, bf16[256,256]{1,0:T(8,128)(2,1)S(1)}, u32[]{:S(2)}, u32[]{:S(2)}) collective-permute-start(bf16[256,256]{1,0:T(8,128)(2,1)S(1)} %shard_map.121.refs_0_), channel_id=1, source_target_pairs={{0,28},{4,24},{8,20},{12,16},{16,12},{20,8},{24,4},{28,0},{1,29},{... | collective-permute-start | bytes 393224 | tf_op jit(solution)/shard_map/ppermute | solution.py:31
  58.1 3.0 %collective-permute-start.21 = (bf16[256,256]{1,0:T(8,128)(2,1)S(1)}, bf16[256,256]{1,0:T(8,128)(2,1)S(1)}, u32[]{:S(2)}, u32[]{:S(2)}) collective-permute-start(bf16[256,256]{1,0:T(8,128)(2,1)S(1)} %shard_map.121.refs_0_), channel_id=1, source_target_pairs={{0,24},{4,28},{8,16},{12,20},{16,8},{20,12},{24,0},{28,4},{1,25},{... | collective-permute-start | bytes 393224 | tf_op jit(solution)/shard_map/ppermute | solution.py:31
  63.8 3.7 %collective-permute-start.17 = (bf16[256,256]{1,0:T(8,128)(2,1)S(1)}, bf16[256,256]{1,0:T(8,128)(2,1)}, u32[]{:S(2)}, u32[]{:S(2)}) collective-permute-start(bf16[256,256]{1,0:T(8,128)(2,1)S(1)} %shard_map.121.refs_0_), channel_id=1, source_target_pairs={{0,8},{4,12},{8,0},{12,4},{16,24},{20,28},{24,16},{28,20},{1,9},{5... | collective-permute-start | bytes 393224 | tf_op jit(solution)/shard_map/ppermute | solution.py:31
  67.5 2.4 %collective-permute-done.21.refs_6_ = bf16[256,256]{1,0:T(8,128)(2,1)S(1)} collective-permute-done((bf16[256,256]{1,0:T(8,128)(2,1)S(1)}, bf16[256,256]{1,0:T(8,128)(2,1)S(1)}, u32[]{:S(2)}, u32[]{:S(2)}) %collective-permute-start.21) | collective-permute-done | bytes 131104 | tf_op jit(solution)/shard_map/ppermute | solution.py:31
  71.7 5.6 %shard_map.118 = (f32[128,512]{1,0:T(8,128)}, f32[128,128]{1,0:T(8,128)}) custom-call(bf16[128,8192]{1,0:T(8,128)(2,1)} %x_ref.3, f32[1,8192]{1,0:T(1,128)} %bitcast.12, bf16[8192,512]{1,0:T(8,128)(2,1)} %weight_ref.3), custom_call_target="tpu_custom_call" | custom-call | tf_op jit(solution)/shard_map/pallas_call | solution.py:251
  77.3 4.9 %shard_map.119.query_ref = bf16[144,512]{1,0:T(8,128)(2,1)} custom-call(bf16[128,8192]{1,0:T(8,128)(2,1)} %x_ref.3, f32[1,8192]{1,0:T(1,128)} %bitcast.13, bf16[8192,512]{1,0:T(8,128)(2,1)} %weight_ref.3, f32[128,512]{1,0:T(8,128)} %get-tuple-element.10.begun, f32[128,128]{1,0:T(8,128)} %get-tuple-element.11.inverse, f32[1,128]{1,0:T(1,128)} %bitcast.14, ...), custom_call_target="tpu_custom_call" | custom-call | tf_op jit(solution)/shard_map/pallas_call | solution.py:266
  82.2 5.3 %collective-permute-start.33 = (bf16[144,512]{1,0:T(8,128)(2,1)}, bf16[144,512]{1,0:T(8,128)(2,1)S(1)}, u32[]{:S(2)}, u32[]{:S(2)}) collective-permute-start(bf16[144,512]{1,0:T(8,128)(2,1)} %shard_map.119.query_ref), channel_id=1, source_target_pairs={{0,192},{64,128},{128,64},{192,0},{1,193},{65,129},{129,65},{193,1... | collective-permute-start | bytes 442376 | tf_op jit(solution)/shard_map/ppermute | solution.py:31
  94.4 3.1 %collective-permute-start.31 = (bf16[144,512]{1,0:T(8,128)(2,1)S(1)}, bf16[144,512]{1,0:T(8,128)(2,1)S(1)}, u32[]{:S(2)}, u32[]{:S(2)}) collective-permute-start(bf16[144,512]{1,0:T(8,128)(2,1)S(1)} %copy-done.3), channel_id=1, source_target_pairs={{0,64},{64,0},{128,192},{192,128},{1,65},{65,1},{129,193},{193,129... | collective-permute-start | bytes 442376 | tf_op jit(solution)/shard_map/ppermute | solution.py:31
  97.4 4.1 %collective-permute-start = (bf16[144,512]{1,0:T(8,128)(2,1)S(1)}, bf16[144,512]{1,0:T(8,128)(2,1)S(1)}, u32[]{:S(2)}, u32[]{:S(2)}) collective-permute-start(bf16[144,512]{1,0:T(8,128)(2,1)S(1)} %copy-done.3), channel_id=1, source_target_pairs={{0,128},{64,192},{128,0},{192,64},{1,129},{65,193},{129,1},{193,65... | collective-permute-start | bytes 442376 | tf_op jit(solution)/shard_map/ppermute | solution.py:31
  103.4 2.8 %shard_map.125 = bf16[128,512]{1,0:T(8,128)(2,1)S(1)} custom-call(s32[3]{0:T(128)S(1)} %pad_add_fusion.place_ref, bf16[144,512]{1,0:T(8,128)(2,1)S(1)} %collective-permute-done.33.query_ref, bf16[256,256]{1,0:T(8,128)(2,1)S(1)} %shard_map.122.refs_0_, bf16[256,256]{1,0:T(8,128)(2,1)S(1)} %collective-permute-done.23.refs_1_, ...), custom_call_target="tpu_custom_call" | custom-call | tf_op jit(solution)/shard_map/pallas_call | solution.py:338
  107.0 2.5 %collective-permute-done.31.query_ref = bf16[144,512]{1,0:T(8,128)(2,1)S(1)} collective-permute-done((bf16[144,512]{1,0:T(8,128)(2,1)S(1)}, bf16[144,512]{1,0:T(8,128)(2,1)S(1)}, u32[]{:S(2)}, u32[]{:S(2)}) %collective-permute-start.31) | collective-permute-done | bytes 147488 | tf_op jit(solution)/shard_map/ppermute | solution.py:31
  109.6 2.8 %shard_map.124 = bf16[128,512]{1,0:T(8,128)(2,1)S(1)} custom-call(s32[3]{0:T(128)S(1)} %pad_add_fusion.place_ref, bf16[144,512]{1,0:T(8,128)(2,1)S(1)} %collective-permute-done.31.query_ref, bf16[256,256]{1,0:T(8,128)(2,1)S(1)} %shard_map.122.refs_0_, bf16[256,256]{1,0:T(8,128)(2,1)S(1)} %collective-permute-done.23.refs_1_, ...), custom_call_target="tpu_custom_call" | custom-call | tf_op jit(solution)/shard_map/pallas_call | solution.py:338
  112.4 3.6 %collective-permute-start.32 = (bf16[128,512]{1,0:T(8,128)(2,1)S(1)}, bf16[128,512]{1,0:T(8,128)(2,1)S(1)}, u32[]{:S(2)}, u32[]{:S(2)}) collective-permute-start(bf16[128,512]{1,0:T(8,128)(2,1)S(1)} %shard_map.124), channel_id=1, source_target_pairs={{0,64},{64,0},{128,192},{192,128},{1,65},{65,1},{129,193},{193,129... | collective-permute-start | bytes 393224 | tf_op jit(solution)/shard_map/ppermute | solution.py:31
  115.9 2.8 %shard_map.123 = bf16[128,512]{1,0:T(8,128)(2,1)S(1)} custom-call(s32[3]{0:T(128)S(1)} %pad_add_fusion.place_ref, bf16[144,512]{1,0:T(8,128)(2,1)S(1)} %collective-permute-done.query_ref, bf16[256,256]{1,0:T(8,128)(2,1)S(1)} %shard_map.122.refs_0_, bf16[256,256]{1,0:T(8,128)(2,1)S(1)} %collective-permute-done.23.refs_1_, ...), custom_call_target="tpu_custom_call" | custom-call | tf_op jit(solution)/shard_map/pallas_call | solution.py:338
  118.7 3.5 %collective-permute-start.30 = (bf16[128,512]{1,0:T(8,128)(2,1)S(1)}, bf16[128,512]{1,0:T(8,128)(2,1)S(1)}, u32[]{:S(2)}, u32[]{:S(2)}) collective-permute-start(bf16[128,512]{1,0:T(8,128)(2,1)S(1)} %shard_map.123), channel_id=1, source_target_pairs={{0,128},{64,192},{128,0},{192,64},{1,129},{65,193},{129,1},{193,65... | collective-permute-start | bytes 393224 | tf_op jit(solution)/shard_map/ppermute | solution.py:31
  122.2 2.8 %shard_map.126 = bf16[128,512]{1,0:T(8,128)(2,1)S(1)} custom-call(s32[3]{0:T(128)S(1)} %pad_add_fusion.place_ref, bf16[144,512]{1,0:T(8,128)(2,1)S(1)} %copy-done.3, bf16[256,256]{1,0:T(8,128)(2,1)S(1)} %shard_map.122.refs_0_, bf16[256,256]{1,0:T(8,128)(2,1)S(1)} %collective-permute-done.23.refs_1_, bf16[256,256]{1,0:T(8,128)(2,1)S(1)} %collective-permute-done.24.refs_2_, ...), custom_call_target="tpu_custom_call" | custom-call | tf_op jit(solution)/shard_map/pallas_call | solution.py:338
  125.1 4.6 %collective-permute-done.30 = bf16[128,512]{1,0:T(8,128)(2,1)S(1)} collective-permute-done((bf16[128,512]{1,0:T(8,128)(2,1)S(1)}, bf16[128,512]{1,0:T(8,128)(2,1)S(1)}, u32[]{:S(2)}, u32[]{:S(2)}) %collective-permute-start.30) | collective-permute-done | bytes 131104 | tf_op jit(solution)/shard_map/ppermute | solution.py:31
  (70 shorter events, 33.3 us)
Async XLA Ops:
  9.1 12.7 %collective-permute-start.8 = (bf16[56,1280]{1,0:T(8,128)(2,1)S(1)}, bf16[56,1280]{1,0:T(8,128)(2,1)S(1)}, u32[]{:S(2)}, u32[]{:S(2)}) collective-permute-start(bf16[56,1280]{1,0:T(8,128)(2,1)S(1)} %fusion.1.refs_0_), channel_id=1, source_target_pairs={{0,28},{4,24},{8,20},{12,16},{16,12},{20,8},{24,4},{28,0},{1,29},{... | collective-permute-start | bytes 430088 | tf_op jit(solution)/shard_map/ppermute | solution.py:31
  16.6 10.5 %collective-permute-start.7 = (bf16[56,1280]{1,0:T(8,128)(2,1)S(1)}, bf16[56,1280]{1,0:T(8,128)(2,1)S(1)}, u32[]{:S(2)}, u32[]{:S(2)}) collective-permute-start(bf16[56,1280]{1,0:T(8,128)(2,1)S(1)} %fusion.1.refs_0_), channel_id=1, source_target_pairs={{0,24},{4,28},{8,16},{12,20},{16,8},{20,12},{24,0},{28,4},{1,25},{... | collective-permute-start | bytes 430088 | tf_op jit(solution)/shard_map/ppermute | solution.py:31
  16.6 12.5 %collective-permute-start.6 = (bf16[56,1280]{1,0:T(8,128)(2,1)S(1)}, bf16[56,1280]{1,0:T(8,128)(2,1)S(1)}, u32[]{:S(2)}, u32[]{:S(2)}) collective-permute-start(bf16[56,1280]{1,0:T(8,128)(2,1)S(1)} %fusion.1.refs_0_), channel_id=1, source_target_pairs={{0,20},{4,16},{8,28},{12,24},{16,4},{20,0},{24,12},{28,8},{1,21},{... | collective-permute-start | bytes 430088 | tf_op jit(solution)/shard_map/ppermute | solution.py:31
  20.2 10.0 %collective-permute-start.5 = (bf16[56,1280]{1,0:T(8,128)(2,1)S(1)}, bf16[56,1280]{1,0:T(8,128)(2,1)S(1)}, u32[]{:S(2)}, u32[]{:S(2)}) collective-permute-start(bf16[56,1280]{1,0:T(8,128)(2,1)S(1)} %fusion.1.refs_0_), channel_id=1, source_target_pairs={{0,16},{4,20},{8,24},{12,28},{16,0},{20,4},{24,8},{28,12},{1,17},{... | collective-permute-start | bytes 430088 | tf_op jit(solution)/shard_map/ppermute | solution.py:31
  20.3 10.0 %collective-permute-start.4 = (bf16[56,1280]{1,0:T(8,128)(2,1)S(1)}, bf16[56,1280]{1,0:T(8,128)(2,1)S(1)}, u32[]{:S(2)}, u32[]{:S(2)}) collective-permute-start(bf16[56,1280]{1,0:T(8,128)(2,1)S(1)} %fusion.1.refs_0_), channel_id=1, source_target_pairs={{0,12},{4,8},{8,4},{12,0},{16,28},{20,24},{24,20},{28,16},{1,13},{... | collective-permute-start | bytes 430088 | tf_op jit(solution)/shard_map/ppermute | solution.py:31
  21.8 10.1 %collective-permute-start.3 = (bf16[56,1280]{1,0:T(8,128)(2,1)S(1)}, bf16[56,1280]{1,0:T(8,128)(2,1)S(1)}, u32[]{:S(2)}, u32[]{:S(2)}) collective-permute-start(bf16[56,1280]{1,0:T(8,128)(2,1)S(1)} %fusion.1.refs_0_), channel_id=1, source_target_pairs={{0,8},{4,12},{8,0},{12,4},{16,24},{20,28},{24,16},{28,20},{1,9},{5... | collective-permute-start | bytes 430088 | tf_op jit(solution)/shard_map/ppermute | solution.py:31
  36.2 14.6 %collective-permute-start.11 = (bf16[576,256]{1,0:T(8,128)(2,1)S(1)}, bf16[576,256]{1,0:T(8,128)(2,1)S(1)}, u32[]{:S(2)}, u32[]{:S(2)}) collective-permute-start(bf16[576,256]{1,0:T(8,128)(2,1)S(1)} %get-tuple-element.13.refs_0_.refs_8_), channel_id=1, source_target_pairs={{0,3},{1,2},{2,1},{3,0},{4,7},{5,6},{6,5},{7,4},{8,11},{9,10},{10,... | collective-permute-start | bytes 884744 | tf_op jit(solution)/shard_map/ppermute | solution.py:31
  36.7 14.1 %collective-permute-start.10 = (bf16[576,256]{1,0:T(8,128)(2,1)S(1)}, bf16[576,256]{1,0:T(8,128)(2,1)S(1)}, u32[]{:S(2)}, u32[]{:S(2)}) collective-permute-start(bf16[576,256]{1,0:T(8,128)(2,1)S(1)} %get-tuple-element.13.refs_0_.refs_8_), channel_id=1, source_target_pairs={{0,2},{1,3},{2,0},{3,1},{4,6},{5,7},{6,4},{7,5},{8,10},{9,11},{10,... | collective-permute-start | bytes 884744 | tf_op jit(solution)/shard_map/ppermute | solution.py:31
  39.2 12.3 %collective-permute-start.9 = (bf16[576,256]{1,0:T(8,128)(2,1)S(1)}, bf16[576,256]{1,0:T(8,128)(2,1)S(1)}, u32[]{:S(2)}, u32[]{:S(2)}) collective-permute-start(bf16[576,256]{1,0:T(8,128)(2,1)S(1)} %get-tuple-element.13.refs_0_.refs_8_), channel_id=1, source_target_pairs={{0,1},{1,0},{2,3},{3,2},{4,5},{5,4},{6,7},{7,6},{8,9},{9,8},{10,11... | collective-permute-start | bytes 884744 | tf_op jit(solution)/shard_map/ppermute | solution.py:31
  40.4 11.1 %collective-permute-start.12 = (bf16[576,256]{1,0:T(8,128)(2,1)S(1)}, bf16[576,256]{1,0:T(8,128)(2,1)S(1)}, u32[]{:S(2)}, u32[]{:S(2)}) collective-permute-start(bf16[576,256]{1,0:T(8,128)(2,1)S(1)} %get-tuple-element.13.refs_0_.refs_8_), channel_id=1, source_target_pairs={{0,32},{32,0},{1,33},{33,1},{2,34},{34,2},{3,35},{35,3},{4,36},{36... | collective-permute-start | bytes 884744 | tf_op jit(solution)/shard_map/ppermute | solution.py:31
  58.1 11.8 %collective-permute-start.21 = (bf16[256,256]{1,0:T(8,128)(2,1)S(1)}, bf16[256,256]{1,0:T(8,128)(2,1)S(1)}, u32[]{:S(2)}, u32[]{:S(2)}) collective-permute-start(bf16[256,256]{1,0:T(8,128)(2,1)S(1)} %shard_map.121.refs_0_), channel_id=1, source_target_pairs={{0,24},{4,28},{8,16},{12,20},{16,8},{20,12},{24,0},{28,4},{1,25},{... | collective-permute-start | bytes 393224 | tf_op jit(solution)/shard_map/ppermute | solution.py:31
  61.0 21.2 %collective-permute-start.20 = (bf16[256,256]{1,0:T(8,128)(2,1)S(1)}, bf16[256,256]{1,0:T(8,128)(2,1)S(1)}, u32[]{:S(2)}, u32[]{:S(2)}) collective-permute-start(bf16[256,256]{1,0:T(8,128)(2,1)S(1)} %shard_map.121.refs_0_), channel_id=1, source_target_pairs={{0,20},{4,16},{8,28},{12,24},{16,4},{20,0},{24,12},{28,8},{1,21},{... | collective-permute-start | bytes 393224 | tf_op jit(solution)/shard_map/ppermute | solution.py:31
  61.0 26.5 %collective-permute-start.19 = (bf16[256,256]{1,0:T(8,128)(2,1)S(1)}, bf16[256,256]{1,0:T(8,128)(2,1)}, u32[]{:S(2)}, u32[]{:S(2)}) collective-permute-start(bf16[256,256]{1,0:T(8,128)(2,1)S(1)} %shard_map.121.refs_0_), channel_id=1, source_target_pairs={{0,16},{4,20},{8,24},{12,28},{16,0},{20,4},{24,8},{28,12},{1,17},{... | collective-permute-start | bytes 393224 | tf_op jit(solution)/shard_map/ppermute | solution.py:31
  63.3 24.3 %collective-permute-start.18 = (bf16[256,256]{1,0:T(8,128)(2,1)S(1)}, bf16[256,256]{1,0:T(8,128)(2,1)}, u32[]{:S(2)}, u32[]{:S(2)}) collective-permute-start(bf16[256,256]{1,0:T(8,128)(2,1)S(1)} %shard_map.121.refs_0_), channel_id=1, source_target_pairs={{0,12},{4,8},{8,4},{12,0},{16,28},{20,24},{24,20},{28,16},{1,13},{... | collective-permute-start | bytes 393224 | tf_op jit(solution)/shard_map/ppermute | solution.py:31
  63.8 23.7 %collective-permute-start.17 = (bf16[256,256]{1,0:T(8,128)(2,1)S(1)}, bf16[256,256]{1,0:T(8,128)(2,1)}, u32[]{:S(2)}, u32[]{:S(2)}) collective-permute-start(bf16[256,256]{1,0:T(8,128)(2,1)S(1)} %shard_map.121.refs_0_), channel_id=1, source_target_pairs={{0,8},{4,12},{8,0},{12,4},{16,24},{20,28},{24,16},{28,20},{1,9},{5... | collective-permute-start | bytes 393224 | tf_op jit(solution)/shard_map/ppermute | solution.py:31
  69.9 17.7 %collective-permute-start.16 = (bf16[256,256]{1,0:T(8,128)(2,1)S(1)}, bf16[256,256]{1,0:T(8,128)(2,1)}, u32[]{:S(2)}, u32[]{:S(2)}) collective-permute-start(bf16[256,256]{1,0:T(8,128)(2,1)S(1)} %shard_map.121.refs_0_), channel_id=1, source_target_pairs={{0,4},{4,0},{8,12},{12,8},{16,20},{20,16},{24,28},{28,24},{1,5},{5... | collective-permute-start | bytes 393224 | tf_op jit(solution)/shard_map/ppermute | solution.py:31
  82.2 12.1 %collective-permute-start.33 = (bf16[144,512]{1,0:T(8,128)(2,1)}, bf16[144,512]{1,0:T(8,128)(2,1)S(1)}, u32[]{:S(2)}, u32[]{:S(2)}) collective-permute-start(bf16[144,512]{1,0:T(8,128)(2,1)} %shard_map.119.query_ref), channel_id=1, source_target_pairs={{0,192},{64,128},{128,64},{192,0},{1,193},{65,129},{129,65},{193,1... | collective-permute-start | bytes 442376 | tf_op jit(solution)/shard_map/ppermute | solution.py:31
  89.4 12.1 %collective-permute-start.25 = (bf16[256,256]{1,0:T(8,128)(2,1)S(1)}, bf16[256,256]{1,0:T(8,128)(2,1)S(1)}, u32[]{:S(2)}, u32[]{:S(2)}) collective-permute-start(bf16[256,256]{1,0:T(8,128)(2,1)S(1)} %shard_map.122.refs_0_), channel_id=1, source_target_pairs={{0,3},{1,2},{2,1},{3,0},{4,7},{5,6},{6,5},{7,4},{8,11},{9,10},{10,... | collective-permute-start | bytes 393224 | tf_op jit(solution)/shard_map/ppermute | solution.py:31
  90.0 11.5 %collective-permute-start.24 = (bf16[256,256]{1,0:T(8,128)(2,1)S(1)}, bf16[256,256]{1,0:T(8,128)(2,1)S(1)}, u32[]{:S(2)}, u32[]{:S(2)}) collective-permute-start(bf16[256,256]{1,0:T(8,128)(2,1)S(1)} %shard_map.122.refs_0_), channel_id=1, source_target_pairs={{0,2},{1,3},{2,0},{3,1},{4,6},{5,7},{6,4},{7,5},{8,10},{9,11},{10,... | collective-permute-start | bytes 393224 | tf_op jit(solution)/shard_map/ppermute | solution.py:31
  94.4 15.2 %collective-permute-start.31 = (bf16[144,512]{1,0:T(8,128)(2,1)S(1)}, bf16[144,512]{1,0:T(8,128)(2,1)S(1)}, u32[]{:S(2)}, u32[]{:S(2)}) collective-permute-start(bf16[144,512]{1,0:T(8,128)(2,1)S(1)} %copy-done.3), channel_id=1, source_target_pairs={{0,64},{64,0},{128,192},{192,128},{1,65},{65,1},{129,193},{193,129... | collective-permute-start | bytes 442376 | tf_op jit(solution)/shard_map/ppermute | solution.py:31
  97.4 18.5 %collective-permute-start = (bf16[144,512]{1,0:T(8,128)(2,1)S(1)}, bf16[144,512]{1,0:T(8,128)(2,1)S(1)}, u32[]{:S(2)}, u32[]{:S(2)}) collective-permute-start(bf16[144,512]{1,0:T(8,128)(2,1)S(1)} %copy-done.3), channel_id=1, source_target_pairs={{0,128},{64,192},{128,0},{192,64},{1,129},{65,193},{129,1},{193,65... | collective-permute-start | bytes 442376 | tf_op jit(solution)/shard_map/ppermute | solution.py:31
  106.2 18.9 %collective-permute-start.34 = (bf16[128,512]{1,0:T(8,128)(2,1)S(1)}, bf16[128,512]{1,0:T(8,128)(2,1)S(1)}, u32[]{:S(2)}, u32[]{:S(2)}) collective-permute-start(bf16[128,512]{1,0:T(8,128)(2,1)S(1)} %shard_map.125), channel_id=1, source_target_pairs={{0,192},{64,128},{128,64},{192,0},{1,193},{65,129},{129,65},{193,1... | collective-permute-start | bytes 393224 | tf_op jit(solution)/shard_map/ppermute | solution.py:31
  112.4 12.7 %collective-permute-start.32 = (bf16[128,512]{1,0:T(8,128)(2,1)S(1)}, bf16[128,512]{1,0:T(8,128)(2,1)S(1)}, u32[]{:S(2)}, u32[]{:S(2)}) collective-permute-start(bf16[128,512]{1,0:T(8,128)(2,1)S(1)} %shard_map.124), channel_id=1, source_target_pairs={{0,64},{64,0},{128,192},{192,128},{1,65},{65,1},{129,193},{193,129... | collective-permute-start | bytes 393224 | tf_op jit(solution)/shard_map/ppermute | solution.py:31
  118.7 11.0 %collective-permute-start.30 = (bf16[128,512]{1,0:T(8,128)(2,1)S(1)}, bf16[128,512]{1,0:T(8,128)(2,1)S(1)}, u32[]{:S(2)}, u32[]{:S(2)}) collective-permute-start(bf16[128,512]{1,0:T(8,128)(2,1)S(1)} %shard_map.123), channel_id=1, source_target_pairs={{0,128},{64,192},{128,0},{192,64},{1,129},{65,193},{129,1},{193,65... | collective-permute-start | bytes 393224 | tf_op jit(solution)/shard_map/ppermute | solution.py:31
  (16 other events, 78.8 us)

commit v3 on v2

--- a/solution.py
+++ b/solution.py
@@ -70,6 +70,10 @@
         q_ref[head] = q[:, head * EHD : (head + 1) * EHD].astype(BF16)
     cross = cross_ref[...]
     fold = jnp.dot(out_rows[...], cross, preferred_element_type=F32)
+    row = lax.broadcasted_iota(jnp.int32, (TENSOR * SHARE, TENSOR * SLOT), 0)
+    column = lax.broadcasted_iota(jnp.int32, (TENSOR * SHARE, TENSOR * SLOT), 1)
+    chosen = (column == row + ((row * 3277) >> 16) * (SLOT - SHARE)).astype(F32).astype(BF16)
+    fold = jnp.dot(chosen, fold.astype(BF16), preferred_element_type=F32)
     kv_ref[4 * EHD :, :] = fold.astype(BF16)
     base_ref[...] = jnp.dot(raw[...], cross, preferred_element_type=F32)
 
@@ -79,7 +83,6 @@
     pieces, (out_ref, scores) = refs[:count], refs[count:]
     rows = q_ref.shape[1]
     scale = 1.0 / math.sqrt(EHD)
-    spread = jnp.zeros(out_ref.shape, F32)
     for head in range(2):
         q = q_ref[head]
         top = None
@@ -98,31 +101,36 @@
             mix = mix + lax.dot_general(
                 p.astype(BF16), pieces[j][low : low + EHD, :], NT, preferred_element_type=F32
             )
-        attended = (mix / jnp.sum(total, axis=-1, keepdims=True)).astype(BF16)
-        feature = lax.broadcasted_iota(jnp.int32, (EHD, out_ref.shape[1]), 0) + head * EHD
-        column = lax.broadcasted_iota(jnp.int32, (EHD, out_ref.shape[1]), 1)
-        block = (feature * 3277) >> 16
-        chosen = (column == feature + block * (SLOT - SHARE)).astype(F32).astype(BF16)
-        spread = spread + jnp.dot(attended, chosen, preferred_element_type=F32)
-    out_ref[...] = spread.astype(BF16)
-
-
-def cross_kernel(me_ref, place_ref, *refs):
-    pieces, folds, refs = refs[:TENSOR], refs[TENSOR : TENSOR + 8], refs[TENSOR + 8 :]
-    base_ref, gain_ref, out_ref, weight = refs
-    me, x, c = me_ref[0], place_ref[1], place_ref[2]
-    size = 8 * SLOT
+        attended = mix / jnp.sum(total, axis=-1, keepdims=True)
+        out_ref[head * EHD : (head + 1) * EHD, :] = attended.T.astype(BF16)
+
+
+def fold_kernel(place_ref, *refs):
+    pieces, (out_ref, stacked) = refs[:8], refs[8:]
+    x, c = place_ref[1], place_ref[2]
+    size = TENSOR * SHARE
     for k in range(8):
         owner = jnp.bitwise_xor(c, k // 4) * 4 + jnp.bitwise_xor(x, k % 4)
-        for t in range(TENSOR):
-            low = pl.multiple_of(t * size + owner * SLOT, SLOT)
-            first = 4 * EHD + t * SLOT
-            weight[pl.ds(low, SLOT), :] = folds[k][first : first + SLOT, :]
+        low = pl.multiple_of(owner * size, size)
+        stacked[pl.ds(low, size), :] = pieces[k][4 * EHD :, :]
+    for t in range(TENSOR):
+        row = lax.broadcasted_iota(jnp.int32, (size, 8 * size), 0)
+        column = lax.broadcasted_iota(jnp.int32, (size, 8 * size), 1)
+        owner = (row * 3277) >> 16
+        source = owner * (size - SHARE) + row + t * SHARE
+        chosen = (column == source).astype(F32).astype(BF16)
+        out = jnp.dot(chosen, stacked[...], preferred_element_type=F32)
+        out_ref[t] = out.astype(BF16)
+
+
+def cross_kernel(me_ref, *refs):
+    pieces, (weight_ref, base_ref, gain_ref, out_ref) = refs[:TENSOR], refs[TENSOR:]
+    me = me_ref[0]
     proj = base_ref[...]
     for step in range(TENSOR):
-        low = pl.multiple_of(jnp.bitwise_xor(me, step) * size, size)
-        proj = proj + jnp.dot(
-            pieces[step][...], weight[pl.ds(low, size), :], preferred_element_type=F32
+        weight = weight_ref[jnp.bitwise_xor(me, step)]
+        proj = proj + lax.dot_general(
+            pieces[step][...], weight, (((0,), (0,)), ((), ())), preferred_element_type=F32
         )
     keys = proj[:, :HD]
     square_mean = jnp.mean(keys * keys, axis=-1, keepdims=True)
@@ -187,21 +195,24 @@
     extra = query_ref[rows : rows + 8, :HD].astype(F32)
     limit = jnp.where(extra[0:1] == zh.astype(F32), extra[1:2] * 16.0 + extra[2:3], 0.0)
     limit = jnp.broadcast_to(limit, (8, rows)).T[:, 0:1]
+    limit = jnp.concatenate([limit] * 4, axis=0)
+    q = [query_ref[:rows, head * HD : (head + 1) * HD] for head in range(4)]
+    q = jnp.concatenate(q, axis=0)
+    mix = jnp.zeros((4 * rows, HD), F32)
+    total = jnp.zeros((4 * rows, 128), F32)
+    for j in range(8):
+        px = jnp.bitwise_xor(x, j % 4)
+        pc = jnp.bitwise_xor(c, j // 4)
+        pos = (base + (pc * 256 + px * 32)).astype(F32)
+        s = lax.dot_general(q, slabs[j][:, :HD], NT, preferred_element_type=F32)
+        w = jnp.where(pos < limit, jnp.exp(s), 0.0)
+        total = total + (w[:, :128] + w[:, 128:])
+        mix = mix + jnp.dot(w.astype(BF16), slabs[j][:, HD:], preferred_element_type=F32)
+    total = jnp.sum(total, axis=-1, keepdims=True)
+    mix = mix / jnp.where(total > 0.0, total, 1.0)
     for head in range(4):
-        q = query_ref[:rows, head * HD : (head + 1) * HD]
-        mix = jnp.zeros((rows, HD), F32)
-        total = jnp.zeros((rows, 128), F32)
-        for j in range(8):
-            px = jnp.bitwise_xor(x, j % 4)
-            pc = jnp.bitwise_xor(c, j // 4)
-            pos = (base + (pc * 256 + px * 32)).astype(F32)
-            s = lax.dot_general(q, slabs[j][:, :HD], NT, preferred_element_type=F32)
-            w = jnp.where(pos < limit, jnp.exp(s), 0.0)
-            total = total + (w[:, :128] + w[:, 128:])
-            mix = mix + jnp.dot(w.astype(BF16), slabs[j][:, HD:], preferred_element_type=F32)
-        total = jnp.sum(total, axis=-1, keepdims=True)
-        total = jnp.where(total > 0.0, total, 1.0)
-        out_ref[:, head * HD : (head + 1) * HD] = (mix / total).astype(BF16)
+        part = mix[head * rows : (head + 1) * rows]
+        out_ref[:, head * HD : (head + 1) * HD] = part.astype(BF16)
 
 
 def limits(mib):
@@ -300,7 +311,7 @@
         qkv_kernel,
         out_shape=(
             jax.ShapeDtypeStruct((2, rows, EHD), BF16),
-            jax.ShapeDtypeStruct((4 * EHD + TENSOR * SLOT, rows), BF16),
+            jax.ShapeDtypeStruct((4 * EHD + TENSOR * SHARE, rows), BF16),
             jax.ShapeDtypeStruct((rows, 2 * HD), F32),
         ),
         in_specs=[smem()] + vmem(TENSOR + 3),
@@ -317,21 +328,28 @@
 
     attended = pl.pallas_call(
         encoder_kernel,
-        out_shape=jax.ShapeDtypeStruct((rows, 8 * SLOT), BF16),
+        out_shape=jax.ShapeDtypeStruct((2 * EHD, rows), BF16),
         in_specs=vmem(9),
         out_specs=vmem(1)[0],
         scratch_shapes=[pltpu.VMEM((2, rows, 8 * rows), F32)],
         compiler_params=limits(20),
     )(q, *kv_pieces)
     attended_pieces = gather_tensor(attended)
+    folded = pl.pallas_call(
+        fold_kernel,
+        out_shape=jax.ShapeDtypeStruct((TENSOR, 2 * EHD, 2 * HD), BF16),
+        in_specs=[smem()] + vmem(8),
+        out_specs=vmem(1)[0],
+        scratch_shapes=[pltpu.VMEM((TENSOR * 2 * EHD, 2 * HD), BF16)],
+        compiler_params=limits(16),
+    )(place, *kv_pieces)
     slab = pl.pallas_call(
         cross_kernel,
         out_shape=jax.ShapeDtypeStruct((rows, 2 * HD), BF16),
-        in_specs=[smem()] * 2 + vmem(TENSOR + 10),
+        in_specs=[smem()] + vmem(TENSOR + 3),
         out_specs=vmem(1)[0],
-        scratch_shapes=[pltpu.VMEM((TENSOR * 8 * SLOT, 2 * HD), BF16)],
         compiler_params=limits(12),
-    )(me, place, *attended_pieces, *kv_pieces, base, key_gain.reshape(1, -1))
+    )(me, *attended_pieces, folded, base, key_gain.reshape(1, -1))
     slabs = gather_xc(slab)
     result = None
     for k in (2, 1, 3, 0):

time: 131 us -> 124 us (0.947)
  starting transfers between devices: 62.9 us -> 55.9 us
  waiting for transfers between devices: 36.2 us -> 38.3 us
  Pallas kernels: 27.2 us -> 25.6 us
    ppermute x34, starting transfers between devices: 58.9 us -> 51.9 us  [xor_permute(): return lax.ppermute(values, axes, [(i, i ^ step) for i in range(size)])]
    pallas_call x4, Pallas kernels: 11.2 us -> 8.97 us  [on_device(): pl.pallas_call(decode_kernel, out_shape=jax.ShapeDtypeStruct((dec_rows, 4...]
    ppermute x34, waiting for transfers between devices: 31.2 us -> 33.2 us  [xor_permute(): return lax.ppermute(values, axes, [(i, i ^ step) for i in range(size)])]
    pallas_call x1 -> x2, Pallas kernels: 2.3 us -> 3.99 us  [the longest x1 2.38 us: on_device(): pl.pallas_call(encoder_kernel, out_shape=jax.ShapeDtypeStruct((2 * EHD, r...]
  transfers between devices with their start and end apart: 35 -> 35, of which waited for: 17 -> 21; matrix products, arithmetic and copies ran while one was open for 1% -> 1% of each run, Pallas kernels for 18% -> 17%
where the time goes in v3:
time: 124 us
  starting transfers between devices  55.9 us (45%)
  waiting for transfers between devices  38.3 us (31%)
  Pallas kernels  25.6 us (21%)
  local copies, waits for them, and re-layouts  3.11 us (3%)
    ppermute x34, starting transfers between devices, xor_permute(): return lax.ppermute(values, axes, [(i, i ^ step) for i in range(size)])  51.9 us
    ppermute x34, waiting for transfers between devices, xor_permute(): return lax.ppermute(values, axes, [(i, i ^ step) for i in range(size)])  33.2 us
    pallas_call x4, Pallas kernels, on_device(): pl.pallas_call(decode_kernel, out_shape=jax.ShapeDtypeStruct((dec_rows, 4...  8.97 us
    pallas_call x1, Pallas kernels, on_device(): pl.pallas_call(query_first_kernel, grid=(steps,), out_shape=(jax.ShapeDty...  5.55 us
    ppermute x1, waiting for transfers between devices, image_permute(): return lax.ppermute(values, ('zh', 'y', 'zl'), pairs)  5.06 us
    pallas_call x1, Pallas kernels, on_device(): pl.pallas_call(query_last_kernel, grid=(steps,), out_shape=jax.ShapeDtype...  4.9 us
    ppermute x1, starting transfers between devices, image_permute(): return lax.ppermute(values, ('zh', 'y', 'zl'), pairs)  3.94 us
  transfers between devices with their start and end apart: 35, of which 21 were waited for; matrix products, arithmetic and copies ran while one was open for 1% of the time, Pallas kernels for 17%

profile of v3, /device:TPU:38, one launch (start us, length us, event | category | flops | bytes accessed | tf_op | source)
XLA Modules:
  0.0 123.7 jit_solution(11728323257085381854)
XLA Ops:
  0.0 3.9 %collective-permute-start.1 = (bf16[32,1280]{1,0:T(8,128)(2,1)}, bf16[32,1280]{1,0:T(8,128)(2,1)S(1)}, u32[]{:S(2)}, u32[]{:S(2)}) collective-permute-start(bf16[32,1280]{1,0:T(8,128)(2,1)} %param.12), channel_id=1, source_target_pairs={{0,0},{4,64},{8,128},{12,192},{16,4},{20,68},{24,132},{28,196},{64... | collective-permute-start | bytes 245768 | tf_op jit(solution)/shard_map/ppermute | solution.py:41
  4.0 5.1 %collective-permute-done.1 = bf16[32,1280]{1,0:T(8,128)(2,1)S(1)} collective-permute-done((bf16[32,1280]{1,0:T(8,128)(2,1)}, bf16[32,1280]{1,0:T(8,128)(2,1)S(1)}, u32[]{:S(2)}, u32[]{:S(2)}) %collective-permute-start.1) | collective-permute-done | bytes 81952 | tf_op jit(solution)/shard_map/ppermute | solution.py:41
  9.1 7.6 %collective-permute-start.8 = (bf16[56,1280]{1,0:T(8,128)(2,1)S(1)}, bf16[56,1280]{1,0:T(8,128)(2,1)S(1)}, u32[]{:S(2)}, u32[]{:S(2)}) collective-permute-start(bf16[56,1280]{1,0:T(8,128)(2,1)S(1)} %fusion.1.refs_0_), channel_id=1, source_target_pairs={{0,28},{4,24},{8,20},{12,16},{16,12},{20,8},{24,4},{28,0},{1,29},{... | collective-permute-start | bytes 430088 | tf_op jit(solution)/shard_map/ppermute | solution.py:31
  16.6 3.6 %collective-permute-start.6 = (bf16[56,1280]{1,0:T(8,128)(2,1)S(1)}, bf16[56,1280]{1,0:T(8,128)(2,1)S(1)}, u32[]{:S(2)}, u32[]{:S(2)}) collective-permute-start(bf16[56,1280]{1,0:T(8,128)(2,1)S(1)} %fusion.1.refs_0_), channel_id=1, source_target_pairs={{0,20},{4,16},{8,28},{12,24},{16,4},{20,0},{24,12},{28,8},{1,21},{... | collective-permute-start | bytes 430088 | tf_op jit(solution)/shard_map/ppermute | solution.py:31
  23.1 4.0 %collective-permute-done.7.refs_6_ = bf16[56,1280]{1,0:T(8,128)(2,1)S(1)} collective-permute-done((bf16[56,1280]{1,0:T(8,128)(2,1)S(1)}, bf16[56,1280]{1,0:T(8,128)(2,1)S(1)}, u32[]{:S(2)}, u32[]{:S(2)}) %collective-permute-start.7) | collective-permute-done | bytes 143392 | tf_op jit(solution)/shard_map/ppermute | solution.py:31
  36.8 2.4 %collective-permute-start.10 = (bf16[480,256]{1,0:T(8,128)(2,1)S(1)}, bf16[480,256]{1,0:T(8,128)(2,1)S(1)}, u32[]{:S(2)}, u32[]{:S(2)}) collective-permute-start(bf16[480,256]{1,0:T(8,128)(2,1)S(1)} %get-tuple-element.13.refs_0_), channel_id=1, source_target_pairs={{0,2},{1,3},{2,0},{3,1},{4,6},{5,7},{6,4},{7,5},{8,10},{9,11},{10,... | collective-permute-start | bytes 737288 | tf_op jit(solution)/shard_map/ppermute | solution.py:31
  40.4 8.3 %collective-permute-done.11.refs_3_ = bf16[480,256]{1,0:T(8,128)(2,1)S(1)} collective-permute-done((bf16[480,256]{1,0:T(8,128)(2,1)S(1)}, bf16[480,256]{1,0:T(8,128)(2,1)S(1)}, u32[]{:S(2)}, u32[]{:S(2)}) %collective-permute-start.11) | collective-permute-done | bytes 245792 | tf_op jit(solution)/shard_map/ppermute | solution.py:31
  51.0 2.4 %shard_map.121.refs_0_ = bf16[160,256]{1,0:T(8,128)(2,1)S(1)} custom-call(bf16[2,256,80]{2,1,0:T(8,128)(2,1)S(1)} %get-tuple-element.12.q_ref, bf16[480,256]{1,0:T(8,128)(2,1)S(1)} %get-tuple-element.13.refs_0_, bf16[480,256]{1,0:T(8,128)(2,1)S(1)} %collective-permute-done.9.refs_1_, bf16[480,256]{1,0:T(8,128)(2,1)S(1)} %collective-permute-done.10.refs_2_, ...), custom_call_target="tpu_custom_call" | custom-call | tf_op jit(solution)/shard_map/pallas_call | solution.py:329
  53.3 2.5 %collective-permute-start.22 = (bf16[160,256]{1,0:T(8,128)(2,1)S(1)}, bf16[160,256]{1,0:T(8,128)(2,1)S(1)}, u32[]{:S(2)}, u32[]{:S(2)}) collective-permute-start(bf16[160,256]{1,0:T(8,128)(2,1)S(1)} %shard_map.121.refs_0_), channel_id=1, source_target_pairs={{0,28},{4,24},{8,20},{12,16},{16,12},{20,8},{24,4},{28,0},{1,29},{... | collective-permute-start | bytes 245768 | tf_op jit(solution)/shard_map/ppermute | solution.py:31
  55.9 3.0 %collective-permute-start.21 = (bf16[160,256]{1,0:T(8,128)(2,1)S(1)}, bf16[160,256]{1,0:T(8,128)(2,1)S(1)}, u32[]{:S(2)}, u32[]{:S(2)}) collective-permute-start(bf16[160,256]{1,0:T(8,128)(2,1)S(1)} %shard_map.121.refs_0_), channel_id=1, source_target_pairs={{0,24},{4,28},{8,16},{12,20},{16,8},{20,12},{24,0},{28,4},{1,25},{... | collective-permute-start | bytes 245768 | tf_op jit(solution)/shard_map/ppermute | solution.py:31
  58.8 5.6 %shard_map.118 = (f32[128,512]{1,0:T(8,128)}, f32[128,128]{1,0:T(8,128)}) custom-call(bf16[128,8192]{1,0:T(8,128)(2,1)} %x_ref.3, f32[1,8192]{1,0:T(1,128)} %bitcast.12, bf16[8192,512]{1,0:T(8,128)(2,1)} %weight_ref.3), custom_call_target="tpu_custom_call" | custom-call | tf_op jit(solution)/shard_map/pallas_call | solution.py:262
  64.4 4.9 %shard_map.119.query_ref = bf16[144,512]{1,0:T(8,128)(2,1)} custom-call(bf16[128,8192]{1,0:T(8,128)(2,1)} %x_ref.3, f32[1,8192]{1,0:T(1,128)} %bitcast.13, bf16[8192,512]{1,0:T(8,128)(2,1)} %weight_ref.3, f32[128,512]{1,0:T(8,128)} %get-tuple-element.10.begun, f32[128,128]{1,0:T(8,128)} %get-tuple-element.11.inverse, f32[1,128]{1,0:T(1,128)} %bitcast.14, ...), custom_call_target="tpu_custom_call" | custom-call | tf_op jit(solution)/shard_map/pallas_call | solution.py:277
  69.3 5.9 %collective-permute-start.33 = (bf16[144,512]{1,0:T(8,128)(2,1)}, bf16[144,512]{1,0:T(8,128)(2,1)S(1)}, u32[]{:S(2)}, u32[]{:S(2)}) collective-permute-start(bf16[144,512]{1,0:T(8,128)(2,1)} %shard_map.119.query_ref), channel_id=1, source_target_pairs={{0,192},{64,128},{128,64},{192,0},{1,193},{65,129},{129,65},{193,1... | collective-permute-start | bytes 442376 | tf_op jit(solution)/shard_map/ppermute | solution.py:31
  77.7 2.2 %collective-permute-start.17 = (bf16[160,256]{1,0:T(8,128)(2,1)S(1)}, bf16[160,256]{1,0:T(8,128)(2,1)S(1)}, u32[]{:S(2)}, u32[]{:S(2)}) collective-permute-start(bf16[160,256]{1,0:T(8,128)(2,1)S(1)} %shard_map.121.refs_0_), channel_id=1, source_target_pairs={{0,8},{4,12},{8,0},{12,4},{16,24},{20,28},{24,16},{28,20},{1,9},{5... | collective-permute-start | bytes 245768 | tf_op jit(solution)/shard_map/ppermute | solution.py:31
  85.8 2.3 %collective-permute-start.24 = (bf16[256,256]{1,0:T(8,128)(2,1)S(1)}, bf16[256,256]{1,0:T(8,128)(2,1)S(1)}, u32[]{:S(2)}, u32[]{:S(2)}) collective-permute-start(bf16[256,256]{1,0:T(8,128)(2,1)S(1)} %shard_map.123.refs_0_), channel_id=1, source_target_pairs={{0,2},{1,3},{2,0},{3,1},{4,6},{5,7},{6,4},{7,5},{8,10},{9,11},{10,... | collective-permute-start | bytes 393224 | tf_op jit(solution)/shard_map/ppermute | solution.py:31
  89.5 2.3 %collective-permute-start.31 = (bf16[144,512]{1,0:T(8,128)(2,1)S(1)}, bf16[144,512]{1,0:T(8,128)(2,1)S(1)}, u32[]{:S(2)}, u32[]{:S(2)}) collective-permute-start(bf16[144,512]{1,0:T(8,128)(2,1)S(1)} %copy-done.3), channel_id=1, source_target_pairs={{0,64},{64,0},{128,192},{192,128},{1,65},{65,1},{129,193},{193,129... | collective-permute-start | bytes 442376 | tf_op jit(solution)/shard_map/ppermute | solution.py:31
  97.1 2.2 %shard_map.126 = bf16[128,512]{1,0:T(8,128)(2,1)S(1)} custom-call(s32[3]{0:T(128)S(1)} %pad_add_fusion.place_ref, bf16[144,512]{1,0:T(8,128)(2,1)S(1)} %collective-permute-done.33.query_ref, bf16[256,256]{1,0:T(8,128)(2,1)S(1)} %shard_map.123.refs_0_, bf16[256,256]{1,0:T(8,128)(2,1)S(1)} %collective-permute-done.23.refs_1_, ...), custom_call_target="tpu_custom_call" | custom-call | tf_op jit(solution)/shard_map/pallas_call | solution.py:356
  100.2 4.0 %collective-permute-done.31.query_ref = bf16[144,512]{1,0:T(8,128)(2,1)S(1)} collective-permute-done((bf16[144,512]{1,0:T(8,128)(2,1)S(1)}, bf16[144,512]{1,0:T(8,128)(2,1)S(1)}, u32[]{:S(2)}, u32[]{:S(2)}) %collective-permute-start.31) | collective-permute-done | bytes 147488 | tf_op jit(solution)/shard_map/ppermute | solution.py:31
  104.2 2.2 %shard_map.125 = bf16[128,512]{1,0:T(8,128)(2,1)S(1)} custom-call(s32[3]{0:T(128)S(1)} %pad_add_fusion.place_ref, bf16[144,512]{1,0:T(8,128)(2,1)S(1)} %collective-permute-done.31.query_ref, bf16[256,256]{1,0:T(8,128)(2,1)S(1)} %shard_map.123.refs_0_, bf16[256,256]{1,0:T(8,128)(2,1)S(1)} %collective-permute-done.23.refs_1_, ...), custom_call_target="tpu_custom_call" | custom-call | tf_op jit(solution)/shard_map/pallas_call | solution.py:356
  106.4 3.5 %collective-permute-start.32 = (bf16[128,512]{1,0:T(8,128)(2,1)S(1)}, bf16[128,512]{1,0:T(8,128)(2,1)S(1)}, u32[]{:S(2)}, u32[]{:S(2)}) collective-permute-start(bf16[128,512]{1,0:T(8,128)(2,1)S(1)} %shard_map.125), channel_id=1, source_target_pairs={{0,64},{64,0},{128,192},{192,128},{1,65},{65,1},{129,193},{193,129... | collective-permute-start | bytes 393224 | tf_op jit(solution)/shard_map/ppermute | solution.py:31
  109.9 2.2 %shard_map.124 = bf16[128,512]{1,0:T(8,128)(2,1)S(1)} custom-call(s32[3]{0:T(128)S(1)} %pad_add_fusion.place_ref, bf16[144,512]{1,0:T(8,128)(2,1)S(1)} %collective-permute-done.query_ref, bf16[256,256]{1,0:T(8,128)(2,1)S(1)} %shard_map.123.refs_0_, bf16[256,256]{1,0:T(8,128)(2,1)S(1)} %collective-permute-done.23.refs_1_, ...), custom_call_target="tpu_custom_call" | custom-call | tf_op jit(solution)/shard_map/pallas_call | solution.py:356
  113.7 2.2 %shard_map.127 = bf16[128,512]{1,0:T(8,128)(2,1)S(1)} custom-call(s32[3]{0:T(128)S(1)} %pad_add_fusion.place_ref, bf16[144,512]{1,0:T(8,128)(2,1)S(1)} %copy-done.3, bf16[256,256]{1,0:T(8,128)(2,1)S(1)} %shard_map.123.refs_0_, bf16[256,256]{1,0:T(8,128)(2,1)S(1)} %collective-permute-done.23.refs_1_, bf16[256,256]{1,0:T(8,128)(2,1)S(1)} %collective-permute-done.24.refs_2_, ...), custom_call_target="tpu_custom_call" | custom-call | tf_op jit(solution)/shard_map/pallas_call | solution.py:356
  115.9 2.9 %collective-permute-done.32 = bf16[128,512]{1,0:T(8,128)(2,1)S(1)} collective-permute-done((bf16[128,512]{1,0:T(8,128)(2,1)S(1)}, bf16[128,512]{1,0:T(8,128)(2,1)S(1)}, u32[]{:S(2)}, u32[]{:S(2)}) %collective-permute-start.32) | collective-permute-done | bytes 131104 | tf_op jit(solution)/shard_map/ppermute | solution.py:31
  118.8 4.2 %collective-permute-done.30 = bf16[128,512]{1,0:T(8,128)(2,1)S(1)} collective-permute-done((bf16[128,512]{1,0:T(8,128)(2,1)S(1)}, bf16[128,512]{1,0:T(8,128)(2,1)S(1)}, u32[]{:S(2)}, u32[]{:S(2)}) %collective-permute-start.30) | collective-permute-done | bytes 131104 | tf_op jit(solution)/shard_map/ppermute | solution.py:31
  (71 shorter events, 33.9 us)
Async XLA Ops:
  0.0 9.1 %collective-permute-start.1 = (bf16[32,1280]{1,0:T(8,128)(2,1)}, bf16[32,1280]{1,0:T(8,128)(2,1)S(1)}, u32[]{:S(2)}, u32[]{:S(2)}) collective-permute-start(bf16[32,1280]{1,0:T(8,128)(2,1)} %param.12), channel_id=1, source_target_pairs={{0,0},{4,64},{8,128},{12,192},{16,4},{20,68},{24,132},{28,196},{64... | collective-permute-start | bytes 245768 | tf_op jit(solution)/shard_map/ppermute | solution.py:41
  9.1 12.7 %collective-permute-start.8 = (bf16[56,1280]{1,0:T(8,128)(2,1)S(1)}, bf16[56,1280]{1,0:T(8,128)(2,1)S(1)}, u32[]{:S(2)}, u32[]{:S(2)}) collective-permute-start(bf16[56,1280]{1,0:T(8,128)(2,1)S(1)} %fusion.1.refs_0_), channel_id=1, source_target_pairs={{0,28},{4,24},{8,20},{12,16},{16,12},{20,8},{24,4},{28,0},{1,29},{... | collective-permute-start | bytes 430088 | tf_op jit(solution)/shard_map/ppermute | solution.py:31
  16.6 10.5 %collective-permute-start.7 = (bf16[56,1280]{1,0:T(8,128)(2,1)S(1)}, bf16[56,1280]{1,0:T(8,128)(2,1)S(1)}, u32[]{:S(2)}, u32[]{:S(2)}) collective-permute-start(bf16[56,1280]{1,0:T(8,128)(2,1)S(1)} %fusion.1.refs_0_), channel_id=1, source_target_pairs={{0,24},{4,28},{8,16},{12,20},{16,8},{20,12},{24,0},{28,4},{1,25},{... | collective-permute-start | bytes 430088 | tf_op jit(solution)/shard_map/ppermute | solution.py:31
  16.6 12.5 %collective-permute-start.6 = (bf16[56,1280]{1,0:T(8,128)(2,1)S(1)}, bf16[56,1280]{1,0:T(8,128)(2,1)S(1)}, u32[]{:S(2)}, u32[]{:S(2)}) collective-permute-start(bf16[56,1280]{1,0:T(8,128)(2,1)S(1)} %fusion.1.refs_0_), channel_id=1, source_target_pairs={{0,20},{4,16},{8,28},{12,24},{16,4},{20,0},{24,12},{28,8},{1,21},{... | collective-permute-start | bytes 430088 | tf_op jit(solution)/shard_map/ppermute | solution.py:31
  20.2 10.0 %collective-permute-start.5 = (bf16[56,1280]{1,0:T(8,128)(2,1)S(1)}, bf16[56,1280]{1,0:T(8,128)(2,1)S(1)}, u32[]{:S(2)}, u32[]{:S(2)}) collective-permute-start(bf16[56,1280]{1,0:T(8,128)(2,1)S(1)} %fusion.1.refs_0_), channel_id=1, source_target_pairs={{0,16},{4,20},{8,24},{12,28},{16,0},{20,4},{24,8},{28,12},{1,17},{... | collective-permute-start | bytes 430088 | tf_op jit(solution)/shard_map/ppermute | solution.py:31
  20.3 10.0 %collective-permute-start.4 = (bf16[56,1280]{1,0:T(8,128)(2,1)S(1)}, bf16[56,1280]{1,0:T(8,128)(2,1)S(1)}, u32[]{:S(2)}, u32[]{:S(2)}) collective-permute-start(bf16[56,1280]{1,0:T(8,128)(2,1)S(1)} %fusion.1.refs_0_), channel_id=1, source_target_pairs={{0,12},{4,8},{8,4},{12,0},{16,28},{20,24},{24,20},{28,16},{1,13},{... | collective-permute-start | bytes 430088 | tf_op jit(solution)/shard_map/ppermute | solution.py:31
  21.8 10.1 %collective-permute-start.3 = (bf16[56,1280]{1,0:T(8,128)(2,1)S(1)}, bf16[56,1280]{1,0:T(8,128)(2,1)S(1)}, u32[]{:S(2)}, u32[]{:S(2)}) collective-permute-start(bf16[56,1280]{1,0:T(8,128)(2,1)S(1)} %fusion.1.refs_0_), channel_id=1, source_target_pairs={{0,8},{4,12},{8,0},{12,4},{16,24},{20,28},{24,16},{28,20},{1,9},{5... | collective-permute-start | bytes 430088 | tf_op jit(solution)/shard_map/ppermute | solution.py:31
  36.2 12.5 %collective-permute-start.11 = (bf16[480,256]{1,0:T(8,128)(2,1)S(1)}, bf16[480,256]{1,0:T(8,128)(2,1)S(1)}, u32[]{:S(2)}, u32[]{:S(2)}) collective-permute-start(bf16[480,256]{1,0:T(8,128)(2,1)S(1)} %get-tuple-element.13.refs_0_), channel_id=1, source_target_pairs={{0,3},{1,2},{2,1},{3,0},{4,7},{5,6},{6,5},{7,4},{8,11},{9,10},{10,... | collective-permute-start | bytes 737288 | tf_op jit(solution)/shard_map/ppermute | solution.py:31
  36.8 12.0 %collective-permute-start.10 = (bf16[480,256]{1,0:T(8,128)(2,1)S(1)}, bf16[480,256]{1,0:T(8,128)(2,1)S(1)}, u32[]{:S(2)}, u32[]{:S(2)}) collective-permute-start(bf16[480,256]{1,0:T(8,128)(2,1)S(1)} %get-tuple-element.13.refs_0_), channel_id=1, source_target_pairs={{0,2},{1,3},{2,0},{3,1},{4,6},{5,7},{6,4},{7,5},{8,10},{9,11},{10,... | collective-permute-start | bytes 737288 | tf_op jit(solution)/shard_map/ppermute | solution.py:31
  39.2 10.2 %collective-permute-start.9 = (bf16[480,256]{1,0:T(8,128)(2,1)S(1)}, bf16[480,256]{1,0:T(8,128)(2,1)S(1)}, u32[]{:S(2)}, u32[]{:S(2)}) collective-permute-start(bf16[480,256]{1,0:T(8,128)(2,1)S(1)} %get-tuple-element.13.refs_0_), channel_id=1, source_target_pairs={{0,1},{1,0},{2,3},{3,2},{4,5},{5,4},{6,7},{7,6},{8,9},{9,8},{10,11... | collective-permute-start | bytes 737288 | tf_op jit(solution)/shard_map/ppermute | solution.py:31
  40.4 9.0 %collective-permute-start.12 = (bf16[480,256]{1,0:T(8,128)(2,1)S(1)}, bf16[480,256]{1,0:T(8,128)(2,1)S(1)}, u32[]{:S(2)}, u32[]{:S(2)}) collective-permute-start(bf16[480,256]{1,0:T(8,128)(2,1)S(1)} %get-tuple-element.13.refs_0_), channel_id=1, source_target_pairs={{0,32},{32,0},{1,33},{33,1},{2,34},{34,2},{3,35},{35,3},{4,36},{36... | collective-permute-start | bytes 737288 | tf_op jit(solution)/shard_map/ppermute | solution.py:31
  53.3 23.7 %collective-permute-start.22 = (bf16[160,256]{1,0:T(8,128)(2,1)S(1)}, bf16[160,256]{1,0:T(8,128)(2,1)S(1)}, u32[]{:S(2)}, u32[]{:S(2)}) collective-permute-start(bf16[160,256]{1,0:T(8,128)(2,1)S(1)} %shard_map.121.refs_0_), channel_id=1, source_target_pairs={{0,28},{4,24},{8,20},{12,16},{16,12},{20,8},{24,4},{28,0},{1,29},{... | collective-permute-start | bytes 245768 | tf_op jit(solution)/shard_map/ppermute | solution.py:31
  55.9 21.8 %collective-permute-start.21 = (bf16[160,256]{1,0:T(8,128)(2,1)S(1)}, bf16[160,256]{1,0:T(8,128)(2,1)S(1)}, u32[]{:S(2)}, u32[]{:S(2)}) collective-permute-start(bf16[160,256]{1,0:T(8,128)(2,1)S(1)} %shard_map.121.refs_0_), channel_id=1, source_target_pairs={{0,24},{4,28},{8,16},{12,20},{16,8},{20,12},{24,0},{28,4},{1,25},{... | collective-permute-start | bytes 245768 | tf_op jit(solution)/shard_map/ppermute | solution.py:31
  58.8 21.1 %collective-permute-start.20 = (bf16[160,256]{1,0:T(8,128)(2,1)S(1)}, bf16[160,256]{1,0:T(8,128)(2,1)S(1)}, u32[]{:S(2)}, u32[]{:S(2)}) collective-permute-start(bf16[160,256]{1,0:T(8,128)(2,1)S(1)} %shard_map.121.refs_0_), channel_id=1, source_target_pairs={{0,20},{4,16},{8,28},{12,24},{16,4},{20,0},{24,12},{28,8},{1,21},{... | collective-permute-start | bytes 245768 | tf_op jit(solution)/shard_map/ppermute | solution.py:31
  69.3 20.2 %collective-permute-start.33 = (bf16[144,512]{1,0:T(8,128)(2,1)}, bf16[144,512]{1,0:T(8,128)(2,1)S(1)}, u32[]{:S(2)}, u32[]{:S(2)}) collective-permute-start(bf16[144,512]{1,0:T(8,128)(2,1)} %shard_map.119.query_ref), channel_id=1, source_target_pairs={{0,192},{64,128},{128,64},{192,0},{1,193},{65,129},{129,65},{193,1... | collective-permute-start | bytes 442376 | tf_op jit(solution)/shard_map/ppermute | solution.py:31
  75.2 7.4 %collective-permute-start.19 = (bf16[160,256]{1,0:T(8,128)(2,1)S(1)}, bf16[160,256]{1,0:T(8,128)(2,1)S(1)}, u32[]{:S(2)}, u32[]{:S(2)}) collective-permute-start(bf16[160,256]{1,0:T(8,128)(2,1)S(1)} %shard_map.121.refs_0_), channel_id=1, source_target_pairs={{0,16},{4,20},{8,24},{12,28},{16,0},{20,4},{24,8},{28,12},{1,17},{... | collective-permute-start | bytes 245768 | tf_op jit(solution)/shard_map/ppermute | solution.py:31
  85.3 9.9 %collective-permute-start.25 = (bf16[256,256]{1,0:T(8,128)(2,1)S(1)}, bf16[256,256]{1,0:T(8,128)(2,1)S(1)}, u32[]{:S(2)}, u32[]{:S(2)}) collective-permute-start(bf16[256,256]{1,0:T(8,128)(2,1)S(1)} %shard_map.123.refs_0_), channel_id=1, source_target_pairs={{0,3},{1,2},{2,1},{3,0},{4,7},{5,6},{6,5},{7,4},{8,11},{9,10},{10,... | collective-permute-start | bytes 393224 | tf_op jit(solution)/shard_map/ppermute | solution.py:31
  85.8 9.4 %collective-permute-start.24 = (bf16[256,256]{1,0:T(8,128)(2,1)S(1)}, bf16[256,256]{1,0:T(8,128)(2,1)S(1)}, u32[]{:S(2)}, u32[]{:S(2)}) collective-permute-start(bf16[256,256]{1,0:T(8,128)(2,1)S(1)} %shard_map.123.refs_0_), channel_id=1, source_target_pairs={{0,2},{1,3},{2,0},{3,1},{4,6},{5,7},{6,4},{7,5},{8,10},{9,11},{10,... | collective-permute-start | bytes 393224 | tf_op jit(solution)/shard_map/ppermute | solution.py:31
  88.1 7.6 %collective-permute-start.23 = (bf16[256,256]{1,0:T(8,128)(2,1)S(1)}, bf16[256,256]{1,0:T(8,128)(2,1)S(1)}, u32[]{:S(2)}, u32[]{:S(2)}) collective-permute-start(bf16[256,256]{1,0:T(8,128)(2,1)S(1)} %shard_map.123.refs_0_), channel_id=1, source_target_pairs={{0,1},{1,0},{2,3},{3,2},{4,5},{5,4},{6,7},{7,6},{8,9},{9,8},{10,11... | collective-permute-start | bytes 393224 | tf_op jit(solution)/shard_map/ppermute | solution.py:31
  89.5 14.7 %collective-permute-start.31 = (bf16[144,512]{1,0:T(8,128)(2,1)S(1)}, bf16[144,512]{1,0:T(8,128)(2,1)S(1)}, u32[]{:S(2)}, u32[]{:S(2)}) collective-permute-start(bf16[144,512]{1,0:T(8,128)(2,1)S(1)} %copy-done.3), channel_id=1, source_target_pairs={{0,64},{64,0},{128,192},{192,128},{1,65},{65,1},{129,193},{193,129... | collective-permute-start | bytes 442376 | tf_op jit(solution)/shard_map/ppermute | solution.py:31
  91.8 18.1 %collective-permute-start = (bf16[144,512]{1,0:T(8,128)(2,1)S(1)}, bf16[144,512]{1,0:T(8,128)(2,1)S(1)}, u32[]{:S(2)}, u32[]{:S(2)}) collective-permute-start(bf16[144,512]{1,0:T(8,128)(2,1)S(1)} %copy-done.3), channel_id=1, source_target_pairs={{0,128},{64,192},{128,0},{192,64},{1,129},{65,193},{129,1},{193,65... | collective-permute-start | bytes 442376 | tf_op jit(solution)/shard_map/ppermute | solution.py:31
  99.4 16.6 %collective-permute-start.34 = (bf16[128,512]{1,0:T(8,128)(2,1)S(1)}, bf16[128,512]{1,0:T(8,128)(2,1)S(1)}, u32[]{:S(2)}, u32[]{:S(2)}) collective-permute-start(bf16[128,512]{1,0:T(8,128)(2,1)S(1)} %shard_map.126), channel_id=1, source_target_pairs={{0,192},{64,128},{128,64},{192,0},{1,193},{65,129},{129,65},{193,1... | collective-permute-start | bytes 393224 | tf_op jit(solution)/shard_map/ppermute | solution.py:31
  106.4 12.4 %collective-permute-start.32 = (bf16[128,512]{1,0:T(8,128)(2,1)S(1)}, bf16[128,512]{1,0:T(8,128)(2,1)S(1)}, u32[]{:S(2)}, u32[]{:S(2)}) collective-permute-start(bf16[128,512]{1,0:T(8,128)(2,1)S(1)} %shard_map.125), channel_id=1, source_target_pairs={{0,64},{64,0},{128,192},{192,128},{1,65},{65,1},{129,193},{193,129... | collective-permute-start | bytes 393224 | tf_op jit(solution)/shard_map/ppermute | solution.py:31
  112.2 10.9 %collective-permute-start.30 = (bf16[128,512]{1,0:T(8,128)(2,1)S(1)}, bf16[128,512]{1,0:T(8,128)(2,1)S(1)}, u32[]{:S(2)}, u32[]{:S(2)}) collective-permute-start(bf16[128,512]{1,0:T(8,128)(2,1)S(1)} %shard_map.124), channel_id=1, source_target_pairs={{0,128},{64,192},{128,0},{192,64},{1,129},{65,193},{129,1},{193,65... | collective-permute-start | bytes 393224 | tf_op jit(solution)/shard_map/ppermute | solution.py:31
  (16 other events, 68.4 us)

commit v4 on v3

--- a/solution.py
+++ b/solution.py
@@ -15,6 +15,7 @@
 BF16 = jnp.bfloat16
 ZH, CORES, YS, ZL, XS = 4, 2, 4, 2, 4
 SHARE, SLOT = 20, 32
+TENSOR_ORDER, X_ORDER = (5, 7, 3, 4, 6, 2, 1), (2, 3, 1)
 TENSOR = YS * ZL
 NT = (((1,), (1,)), ((), ()))
 
@@ -36,7 +37,7 @@
     for zh in range(ZH):
         for y in range(YS):
             for zl in range(ZL):
-                image, slot = (y % 2) * 2 + zl, zh * 2 + y // 2
+                image, slot = (y % 2) * 2 + zl, (y // 2) * ZH + zh
                 pairs.append(((zh * YS + y) * ZL + zl, image * TENSOR + slot))
     return lax.ppermute(values, ("zh", "y", "zl"), pairs)
 
@@ -139,9 +140,9 @@
     out_ref[:, HD:] = proj[:, HD:].astype(BF16)
 
 
-def query_part(x_ref, gain_ref, weight_ref, total, inverse):
+def query_part(x_ref, gain_ref, weight_ref, total, inverse, step):
     depth = weight_ref.shape[0]
-    columns = pl.ds(pl.multiple_of(pl.program_id(0) * depth, depth), depth)
+    columns = pl.ds(pl.multiple_of(step * depth, depth), depth)
     normed = x_ref[:, columns].astype(F32) * inverse[:, 0:1] * gain_ref[:, columns]
     total[...] += jnp.dot(normed.astype(BF16), weight_ref[...], preferred_element_type=F32)
 
@@ -157,7 +158,7 @@
         inverse[...] = jnp.broadcast_to(lax.rsqrt(mean + EPSILON), inverse.shape)
         total[...] = jnp.zeros_like(total)
 
-    query_part(x_ref, gain_ref, weight_ref, total, inverse)
+    query_part(x_ref, gain_ref, weight_ref, total, inverse, pl.program_id(0))
 
 
 def query_last_kernel(
@@ -169,7 +170,7 @@
     def _():
         total[...] = begun[...]
 
-    query_part(x_ref, gain_ref, weight_ref, total, inverse)
+    query_part(x_ref, gain_ref, weight_ref, total, inverse, 0)
 
     @pl.when(pl.program_id(0) == pl.num_programs(0) - 1)
     def _():
@@ -190,7 +191,7 @@
     keys = slabs[0].shape[0]
     zh, x, c = place_ref[0], place_ref[1], place_ref[2]
     lane = lax.broadcasted_iota(jnp.int32, (1, keys), 1)
-    base = (lane >> 6) * 512 + ((lane >> 5) & 1) * 128 + (lane & 31)
+    base = ((lane >> 5) & 3) * 512 + (lane >> 7) * 128 + (lane & 31)
     rows = out_ref.shape[0]
     extra = query_ref[rows : rows + 8, :HD].astype(F32)
     limit = jnp.where(extra[0:1] == zh.astype(F32), extra[1:2] * 16.0 + extra[2:3], 0.0)
@@ -220,13 +221,16 @@
 
 
 def gather_xc(piece):
-    along_x = [piece] + [xor_permute(piece, "x", XS, k) for k in range(1, XS)]
+    along_x = {0: piece}
+    for k in X_ORDER:
+        along_x[k] = xor_permute(piece, "x", XS, k)
+    along_x = [along_x[k] for k in range(XS)]
     return along_x + [xor_permute(value, "c", CORES, 1) for value in along_x]
 
 
 def gather_tensor(piece):
     pieces = {0: piece}
-    for k in (5, 7, 3, 4, 6, 2, 1):
+    for k in TENSOR_ORDER:
         pieces[k] = xor_permute(piece, ("y", "zl"), TENSOR, k)
     return [pieces[k] for k in range(TENSOR)]
 
@@ -255,13 +259,13 @@
     own = image_permute(patches)
 
     dec_rows = dec_hidden.shape[0]
-    depth, steps = 1024, 4
+    depth, first_steps, last_steps = 1024, 2, 6
     dec_width, query_width = query_weight.shape
     fixed = lambda shape: pl.BlockSpec(shape, lambda i: (0, 0))
     gain_view = dec_gain.reshape(1, -1)
     begun, inverse = pl.pallas_call(
         query_first_kernel,
-        grid=(steps,),
+        grid=(first_steps,),
         out_shape=(
             jax.ShapeDtypeStruct((dec_rows, query_width), F32),
             jax.ShapeDtypeStruct((dec_rows, 128), F32),
@@ -276,12 +280,12 @@
     )(dec_hidden, gain_view, query_weight)
     message = pl.pallas_call(
         query_last_kernel,
-        grid=(steps,),
+        grid=(last_steps,),
         out_shape=jax.ShapeDtypeStruct((dec_rows + 16, query_width), BF16),
         in_specs=[
-            pl.BlockSpec((dec_rows, dec_width // 2), lambda i: (0, 1)),
-            pl.BlockSpec((1, dec_width // 2), lambda i: (0, 1)),
-            pl.BlockSpec((depth, query_width), lambda i: (i + steps, 0)),
+            pl.BlockSpec((dec_rows, depth), lambda i: (0, i + first_steps)),
+            pl.BlockSpec((1, depth), lambda i: (0, i + first_steps)),
+            pl.BlockSpec((depth, query_width), lambda i: (i + first_steps, 0)),
             fixed((dec_rows, query_width)),
             fixed((dec_rows, 128)),
             fixed((1, HD)),

time: 124 us -> 122 us (0.984)
  the two profiles are of different devices: /device:TPU:38 before, /device:TPU:32 now
where the time goes in v4:
time: 122 us
  starting transfers between devices  59 us (48%)
  waiting for transfers between devices  33.3 us (27%)
  Pallas kernels  25.7 us (21%)
  local copies, waits for them, and re-layouts  3.11 us (3%)
    ppermute x34, starting transfers between devices, xor_permute(): return lax.ppermute(values, axes, [(i, i ^ step) for i in range(size)])  55 us
    ppermute x34, waiting for transfers between devices, xor_permute(): return lax.ppermute(values, axes, [(i, i ^ step) for i in range(size)])  30.6 us
    pallas_call x4, Pallas kernels, on_device(): pl.pallas_call(decode_kernel, out_shape=jax.ShapeDtypeStruct((dec_rows, 4...  8.97 us
    pallas_call x1, Pallas kernels, on_device(): pl.pallas_call(query_last_kernel, grid=(last_steps,), out_shape=jax.Shape...  6.68 us
    ppermute x1, starting transfers between devices, image_permute(): return lax.ppermute(values, ('zh', 'y', 'zl'), pairs)  3.94 us
    pallas_call x1, Pallas kernels, on_device(): pl.pallas_call(query_first_kernel, grid=(first_steps,), out_shape=(jax.Sh...  3.88 us
    ppermute x1, waiting for transfers between devices, image_permute(): return lax.ppermute(values, ('zh', 'y', 'zl'), pairs)  2.66 us
  transfers between devices with their start and end apart: 35, of which 19 were waited for; matrix products, arithmetic and copies ran while one was open for 1% of the time, Pallas kernels for 18%

profile of v4, /device:TPU:32, one launch (start us, length us, event | category | flops | bytes accessed | tf_op | source)
XLA Modules:
  0.0 122.0 jit_solution(7784678722255407854)
XLA Ops:
  0.0 3.9 %collective-permute-start.1 = (bf16[32,1280]{1,0:T(8,128)(2,1)}, bf16[32,1280]{1,0:T(8,128)(2,1)S(1)}, u32[]{:S(2)}, u32[]{:S(2)}) collective-permute-start(bf16[32,1280]{1,0:T(8,128)(2,1)} %param.12), channel_id=1, source_target_pairs={{0,0},{4,64},{8,128},{12,192},{16,16},{20,80},{24,144},{28,208},{6... | collective-permute-start | bytes 245768 | tf_op jit(solution)/shard_map/ppermute | solution.py:42
  4.0 2.7 %collective-permute-done.1 = bf16[32,1280]{1,0:T(8,128)(2,1)S(1)} collective-permute-done((bf16[32,1280]{1,0:T(8,128)(2,1)}, bf16[32,1280]{1,0:T(8,128)(2,1)S(1)}, u32[]{:S(2)}, u32[]{:S(2)}) %collective-permute-start.1) | collective-permute-done | bytes 81952 | tf_op jit(solution)/shard_map/ppermute | solution.py:42
  6.7 8.1 %collective-permute-start.8 = (bf16[56,1280]{1,0:T(8,128)(2,1)S(1)}, bf16[56,1280]{1,0:T(8,128)(2,1)S(1)}, u32[]{:S(2)}, u32[]{:S(2)}) collective-permute-start(bf16[56,1280]{1,0:T(8,128)(2,1)S(1)} %fusion.1.refs_0_), channel_id=1, source_target_pairs={{0,28},{4,24},{8,20},{12,16},{16,12},{20,8},{24,4},{28,0},{1,29},{... | collective-permute-start | bytes 430088 | tf_op jit(solution)/shard_map/ppermute | solution.py:32
  17.0 3.2 %collective-permute-start.5 = (bf16[56,1280]{1,0:T(8,128)(2,1)S(1)}, bf16[56,1280]{1,0:T(8,128)(2,1)S(1)}, u32[]{:S(2)}, u32[]{:S(2)}) collective-permute-start(bf16[56,1280]{1,0:T(8,128)(2,1)S(1)} %fusion.1.refs_0_), channel_id=1, source_target_pairs={{0,16},{4,20},{8,24},{12,28},{16,0},{20,4},{24,8},{28,12},{1,17},{... | collective-permute-start | bytes 430088 | tf_op jit(solution)/shard_map/ppermute | solution.py:32
  22.3 4.0 %collective-permute-done.7.refs_6_ = bf16[56,1280]{1,0:T(8,128)(2,1)S(1)} collective-permute-done((bf16[56,1280]{1,0:T(8,128)(2,1)S(1)}, bf16[56,1280]{1,0:T(8,128)(2,1)S(1)}, u32[]{:S(2)}, u32[]{:S(2)}) %collective-permute-start.7) | collective-permute-done | bytes 143392 | tf_op jit(solution)/shard_map/ppermute | solution.py:32
  26.3 2.2 %collective-permute-start.2 = (bf16[56,1280]{1,0:T(8,128)(2,1)S(1)}, bf16[56,1280]{1,0:T(8,128)(2,1)S(1)}, u32[]{:S(2)}, u32[]{:S(2)}) collective-permute-start(bf16[56,1280]{1,0:T(8,128)(2,1)S(1)} %fusion.1.refs_0_), channel_id=1, source_target_pairs={{0,4},{4,0},{8,12},{12,8},{16,20},{20,16},{24,28},{28,24},{1,5},{5... | collective-permute-start | bytes 430088 | tf_op jit(solution)/shard_map/ppermute | solution.py:32
  35.8 2.8 %collective-permute-start.11 = (bf16[480,256]{1,0:T(8,128)(2,1)S(1)}, bf16[480,256]{1,0:T(8,128)(2,1)S(1)}, u32[]{:S(2)}, u32[]{:S(2)}) collective-permute-start(bf16[480,256]{1,0:T(8,128)(2,1)S(1)} %get-tuple-element.13.refs_0_), channel_id=1, source_target_pairs={{0,3},{1,2},{2,1},{3,0},{4,7},{5,6},{6,5},{7,4},{8,11},{9,10},{10,... | collective-permute-start | bytes 737288 | tf_op jit(solution)/shard_map/ppermute | solution.py:32
  40.0 9.2 %collective-permute-done.11.refs_3_ = bf16[480,256]{1,0:T(8,128)(2,1)S(1)} collective-permute-done((bf16[480,256]{1,0:T(8,128)(2,1)S(1)}, bf16[480,256]{1,0:T(8,128)(2,1)S(1)}, u32[]{:S(2)}, u32[]{:S(2)}) %collective-permute-start.11) | collective-permute-done | bytes 245792 | tf_op jit(solution)/shard_map/ppermute | solution.py:32
  51.4 2.4 %shard_map.121.refs_0_ = bf16[160,256]{1,0:T(8,128)(2,1)S(1)} custom-call(bf16[2,256,80]{2,1,0:T(8,128)(2,1)S(1)} %get-tuple-element.12.q_ref, bf16[480,256]{1,0:T(8,128)(2,1)S(1)} %get-tuple-element.13.refs_0_, bf16[480,256]{1,0:T(8,128)(2,1)S(1)} %collective-permute-done.9.refs_1_, bf16[480,256]{1,0:T(8,128)(2,1)S(1)} %collective-permute-done.10.refs_2_, ...), custom_call_target="tpu_custom_call" | custom-call | tf_op jit(solution)/shard_map/pallas_call | solution.py:333
  54.8 3.0 %collective-permute-start.21 = (bf16[160,256]{1,0:T(8,128)(2,1)S(1)}, bf16[160,256]{1,0:T(8,128)(2,1)S(1)}, u32[]{:S(2)}, u32[]{:S(2)}) collective-permute-start(bf16[160,256]{1,0:T(8,128)(2,1)S(1)} %shard_map.121.refs_0_), channel_id=1, source_target_pairs={{0,24},{4,28},{8,16},{12,20},{16,8},{20,12},{24,0},{28,4},{1,25},{... | collective-permute-start | bytes 245768 | tf_op jit(solution)/shard_map/ppermute | solution.py:32
  58.0 3.9 %shard_map.118 = (f32[128,512]{1,0:T(8,128)}, f32[128,128]{1,0:T(8,128)}) custom-call(bf16[128,8192]{1,0:T(8,128)(2,1)} %x_ref.3, f32[1,8192]{1,0:T(1,128)} %bitcast.12, bf16[8192,512]{1,0:T(8,128)(2,1)} %weight_ref.3), custom_call_target="tpu_custom_call" | custom-call | tf_op jit(solution)/shard_map/pallas_call | solution.py:266
  61.9 6.7 %shard_map.119.query_ref = bf16[144,512]{1,0:T(8,128)(2,1)} custom-call(bf16[128,8192]{1,0:T(8,128)(2,1)} %x_ref.3, f32[1,8192]{1,0:T(1,128)} %bitcast.13, bf16[8192,512]{1,0:T(8,128)(2,1)} %weight_ref.3, f32[128,512]{1,0:T(8,128)} %get-tuple-element.10.begun, f32[128,128]{1,0:T(8,128)} %get-tuple-element.11.inverse, f32[1,128]{1,0:T(1,128)} %bitcast.14, ...), custom_call_target="tpu_custom_call" | custom-call | tf_op jit(solution)/shard_map/pallas_call | solution.py:281
  68.6 4.9 %collective-permute-start.33 = (bf16[144,512]{1,0:T(8,128)(2,1)}, bf16[144,512]{1,0:T(8,128)(2,1)S(1)}, u32[]{:S(2)}, u32[]{:S(2)}) collective-permute-start(bf16[144,512]{1,0:T(8,128)(2,1)} %shard_map.119.query_ref), channel_id=1, source_target_pairs={{0,192},{64,128},{128,64},{192,0},{1,193},{65,129},{129,65},{193,1... | collective-permute-start | bytes 442376 | tf_op jit(solution)/shard_map/ppermute | solution.py:32
  74.7 2.6 %collective-permute-start.18 = (bf16[160,256]{1,0:T(8,128)(2,1)S(1)}, bf16[160,256]{1,0:T(8,128)(2,1)S(1)}, u32[]{:S(2)}, u32[]{:S(2)}) collective-permute-start(bf16[160,256]{1,0:T(8,128)(2,1)S(1)} %shard_map.121.refs_0_), channel_id=1, source_target_pairs={{0,12},{4,8},{8,4},{12,0},{16,28},{20,24},{24,20},{28,16},{1,13},{... | collective-permute-start | bytes 245768 | tf_op jit(solution)/shard_map/ppermute | solution.py:32
  83.5 2.8 %collective-permute-start.25 = (bf16[256,256]{1,0:T(8,128)(2,1)S(1)}, bf16[256,256]{1,0:T(8,128)(2,1)S(1)}, u32[]{:S(2)}, u32[]{:S(2)}) collective-permute-start(bf16[256,256]{1,0:T(8,128)(2,1)S(1)} %shard_map.123.refs_0_), channel_id=1, source_target_pairs={{0,3},{1,2},{2,1},{3,0},{4,7},{5,6},{6,5},{7,4},{8,11},{9,10},{10,... | collective-permute-start | bytes 393224 | tf_op jit(solution)/shard_map/ppermute | solution.py:32
  88.3 4.3 %collective-permute-start = (bf16[144,512]{1,0:T(8,128)(2,1)S(1)}, bf16[144,512]{1,0:T(8,128)(2,1)S(1)}, u32[]{:S(2)}, u32[]{:S(2)}) collective-permute-start(bf16[144,512]{1,0:T(8,128)(2,1)S(1)} %copy-done.3), channel_id=1, source_target_pairs={{0,128},{64,192},{128,0},{192,64},{1,129},{65,193},{129,1},{193,65... | collective-permute-start | bytes 442376 | tf_op jit(solution)/shard_map/ppermute | solution.py:32
  95.8 2.2 %shard_map.126 = bf16[128,512]{1,0:T(8,128)(2,1)S(1)} custom-call(s32[3]{0:T(128)S(1)} %pad_add_fusion.place_ref, bf16[144,512]{1,0:T(8,128)(2,1)S(1)} %collective-permute-done.33.query_ref, bf16[256,256]{1,0:T(8,128)(2,1)S(1)} %shard_map.123.refs_0_, bf16[256,256]{1,0:T(8,128)(2,1)S(1)} %collective-permute-done.23.refs_1_, ...), custom_call_target="tpu_custom_call" | custom-call | tf_op jit(solution)/shard_map/pallas_call | solution.py:360
  98.9 1.7 %collective-permute-done.31.query_ref = bf16[144,512]{1,0:T(8,128)(2,1)S(1)} collective-permute-done((bf16[144,512]{1,0:T(8,128)(2,1)S(1)}, bf16[144,512]{1,0:T(8,128)(2,1)S(1)}, u32[]{:S(2)}, u32[]{:S(2)}) %collective-permute-start.31) | collective-permute-done | bytes 147488 | tf_op jit(solution)/shard_map/ppermute | solution.py:32
  100.6 2.2 %shard_map.125 = bf16[128,512]{1,0:T(8,128)(2,1)S(1)} custom-call(s32[3]{0:T(128)S(1)} %pad_add_fusion.place_ref, bf16[144,512]{1,0:T(8,128)(2,1)S(1)} %collective-permute-done.31.query_ref, bf16[256,256]{1,0:T(8,128)(2,1)S(1)} %shard_map.123.refs_0_, bf16[256,256]{1,0:T(8,128)(2,1)S(1)} %collective-permute-done.23.refs_1_, ...), custom_call_target="tpu_custom_call" | custom-call | tf_op jit(solution)/shard_map/pallas_call | solution.py:360
  102.8 3.5 %collective-permute-start.32 = (bf16[128,512]{1,0:T(8,128)(2,1)S(1)}, bf16[128,512]{1,0:T(8,128)(2,1)S(1)}, u32[]{:S(2)}, u32[]{:S(2)}) collective-permute-start(bf16[128,512]{1,0:T(8,128)(2,1)S(1)} %shard_map.125), channel_id=1, source_target_pairs={{0,64},{64,0},{128,192},{192,128},{1,65},{65,1},{129,193},{193,129... | collective-permute-start | bytes 393224 | tf_op jit(solution)/shard_map/ppermute | solution.py:32
  106.3 2.2 %shard_map.124 = bf16[128,512]{1,0:T(8,128)(2,1)S(1)} custom-call(s32[3]{0:T(128)S(1)} %pad_add_fusion.place_ref, bf16[144,512]{1,0:T(8,128)(2,1)S(1)} %collective-permute-done.query_ref, bf16[256,256]{1,0:T(8,128)(2,1)S(1)} %shard_map.123.refs_0_, bf16[256,256]{1,0:T(8,128)(2,1)S(1)} %collective-permute-done.23.refs_1_, ...), custom_call_target="tpu_custom_call" | custom-call | tf_op jit(solution)/shard_map/pallas_call | solution.py:360
  108.6 4.7 %collective-permute-start.30 = (bf16[128,512]{1,0:T(8,128)(2,1)S(1)}, bf16[128,512]{1,0:T(8,128)(2,1)S(1)}, u32[]{:S(2)}, u32[]{:S(2)}) collective-permute-start(bf16[128,512]{1,0:T(8,128)(2,1)S(1)} %shard_map.124), channel_id=1, source_target_pairs={{0,128},{64,192},{128,0},{192,64},{1,129},{65,193},{129,1},{193,65... | collective-permute-start | bytes 393224 | tf_op jit(solution)/shard_map/ppermute | solution.py:32
  113.2 2.3 %shard_map.127 = bf16[128,512]{1,0:T(8,128)(2,1)S(1)} custom-call(s32[3]{0:T(128)S(1)} %pad_add_fusion.place_ref, bf16[144,512]{1,0:T(8,128)(2,1)S(1)} %copy-done.3, bf16[256,256]{1,0:T(8,128)(2,1)S(1)} %shard_map.123.refs_0_, bf16[256,256]{1,0:T(8,128)(2,1)S(1)} %collective-permute-done.23.refs_1_, bf16[256,256]{1,0:T(8,128)(2,1)S(1)} %collective-permute-done.24.refs_2_, ...), custom_call_target="tpu_custom_call" | custom-call | tf_op jit(solution)/shard_map/pallas_call | solution.py:360
  115.5 5.8 %collective-permute-done.30 = bf16[128,512]{1,0:T(8,128)(2,1)S(1)} collective-permute-done((bf16[128,512]{1,0:T(8,128)(2,1)S(1)}, bf16[128,512]{1,0:T(8,128)(2,1)S(1)}, u32[]{:S(2)}, u32[]{:S(2)}) %collective-permute-start.30) | collective-permute-done | bytes 131104 | tf_op jit(solution)/shard_map/ppermute | solution.py:32
  (71 shorter events, 30.6 us)
Async XLA Ops:
  6.7 14.1 %collective-permute-start.8 = (bf16[56,1280]{1,0:T(8,128)(2,1)S(1)}, bf16[56,1280]{1,0:T(8,128)(2,1)S(1)}, u32[]{:S(2)}, u32[]{:S(2)}) collective-permute-start(bf16[56,1280]{1,0:T(8,128)(2,1)S(1)} %fusion.1.refs_0_), channel_id=1, source_target_pairs={{0,28},{4,24},{8,20},{12,16},{16,12},{20,8},{24,4},{28,0},{1,29},{... | collective-permute-start | bytes 430088 | tf_op jit(solution)/shard_map/ppermute | solution.py:32
  14.8 11.5 %collective-permute-start.7 = (bf16[56,1280]{1,0:T(8,128)(2,1)S(1)}, bf16[56,1280]{1,0:T(8,128)(2,1)S(1)}, u32[]{:S(2)}, u32[]{:S(2)}) collective-permute-start(bf16[56,1280]{1,0:T(8,128)(2,1)S(1)} %fusion.1.refs_0_), channel_id=1, source_target_pairs={{0,24},{4,28},{8,16},{12,20},{16,8},{20,12},{24,0},{28,4},{1,25},{... | collective-permute-start | bytes 430088 | tf_op jit(solution)/shard_map/ppermute | solution.py:32
  15.8 13.3 %collective-permute-start.6 = (bf16[56,1280]{1,0:T(8,128)(2,1)S(1)}, bf16[56,1280]{1,0:T(8,128)(2,1)S(1)}, u32[]{:S(2)}, u32[]{:S(2)}) collective-permute-start(bf16[56,1280]{1,0:T(8,128)(2,1)S(1)} %fusion.1.refs_0_), channel_id=1, source_target_pairs={{0,20},{4,16},{8,28},{12,24},{16,4},{20,0},{24,12},{28,8},{1,21},{... | collective-permute-start | bytes 430088 | tf_op jit(solution)/shard_map/ppermute | solution.py:32
  17.0 12.5 %collective-permute-start.5 = (bf16[56,1280]{1,0:T(8,128)(2,1)S(1)}, bf16[56,1280]{1,0:T(8,128)(2,1)S(1)}, u32[]{:S(2)}, u32[]{:S(2)}) collective-permute-start(bf16[56,1280]{1,0:T(8,128)(2,1)S(1)} %fusion.1.refs_0_), channel_id=1, source_target_pairs={{0,16},{4,20},{8,24},{12,28},{16,0},{20,4},{24,8},{28,12},{1,17},{... | collective-permute-start | bytes 430088 | tf_op jit(solution)/shard_map/ppermute | solution.py:32
  20.2 9.3 %collective-permute-start.4 = (bf16[56,1280]{1,0:T(8,128)(2,1)S(1)}, bf16[56,1280]{1,0:T(8,128)(2,1)S(1)}, u32[]{:S(2)}, u32[]{:S(2)}) collective-permute-start(bf16[56,1280]{1,0:T(8,128)(2,1)S(1)} %fusion.1.refs_0_), channel_id=1, source_target_pairs={{0,12},{4,8},{8,4},{12,0},{16,28},{20,24},{24,20},{28,16},{1,13},{... | collective-permute-start | bytes 430088 | tf_op jit(solution)/shard_map/ppermute | solution.py:32
  20.7 10.4 %collective-permute-start.3 = (bf16[56,1280]{1,0:T(8,128)(2,1)S(1)}, bf16[56,1280]{1,0:T(8,128)(2,1)S(1)}, u32[]{:S(2)}, u32[]{:S(2)}) collective-permute-start(bf16[56,1280]{1,0:T(8,128)(2,1)S(1)} %fusion.1.refs_0_), channel_id=1, source_target_pairs={{0,8},{4,12},{8,0},{12,4},{16,24},{20,28},{24,16},{28,20},{1,9},{5... | collective-permute-start | bytes 430088 | tf_op jit(solution)/shard_map/ppermute | solution.py:32
  35.8 13.3 %collective-permute-start.11 = (bf16[480,256]{1,0:T(8,128)(2,1)S(1)}, bf16[480,256]{1,0:T(8,128)(2,1)S(1)}, u32[]{:S(2)}, u32[]{:S(2)}) collective-permute-start(bf16[480,256]{1,0:T(8,128)(2,1)S(1)} %get-tuple-element.13.refs_0_), channel_id=1, source_target_pairs={{0,3},{1,2},{2,1},{3,0},{4,7},{5,6},{6,5},{7,4},{8,11},{9,10},{10,... | collective-permute-start | bytes 737288 | tf_op jit(solution)/shard_map/ppermute | solution.py:32
  38.7 10.5 %collective-permute-start.10 = (bf16[480,256]{1,0:T(8,128)(2,1)S(1)}, bf16[480,256]{1,0:T(8,128)(2,1)S(1)}, u32[]{:S(2)}, u32[]{:S(2)}) collective-permute-start(bf16[480,256]{1,0:T(8,128)(2,1)S(1)} %get-tuple-element.13.refs_0_), channel_id=1, source_target_pairs={{0,2},{1,3},{2,0},{3,1},{4,6},{5,7},{6,4},{7,5},{8,10},{9,11},{10,... | collective-permute-start | bytes 737288 | tf_op jit(solution)/shard_map/ppermute | solution.py:32
  39.5 10.3 %collective-permute-start.9 = (bf16[480,256]{1,0:T(8,128)(2,1)S(1)}, bf16[480,256]{1,0:T(8,128)(2,1)S(1)}, u32[]{:S(2)}, u32[]{:S(2)}) collective-permute-start(bf16[480,256]{1,0:T(8,128)(2,1)S(1)} %get-tuple-element.13.refs_0_), channel_id=1, source_target_pairs={{0,1},{1,0},{2,3},{3,2},{4,5},{5,4},{6,7},{7,6},{8,9},{9,8},{10,11... | collective-permute-start | bytes 737288 | tf_op jit(solution)/shard_map/ppermute | solution.py:32
  40.0 9.8 %collective-permute-start.12 = (bf16[480,256]{1,0:T(8,128)(2,1)S(1)}, bf16[480,256]{1,0:T(8,128)(2,1)S(1)}, u32[]{:S(2)}, u32[]{:S(2)}) collective-permute-start(bf16[480,256]{1,0:T(8,128)(2,1)S(1)} %get-tuple-element.13.refs_0_), channel_id=1, source_target_pairs={{0,32},{32,0},{1,33},{33,1},{2,34},{34,2},{3,35},{35,3},{4,36},{36... | collective-permute-start | bytes 737288 | tf_op jit(solution)/shard_map/ppermute | solution.py:32
  53.8 21.0 %collective-permute-start.22 = (bf16[160,256]{1,0:T(8,128)(2,1)S(1)}, bf16[160,256]{1,0:T(8,128)(2,1)S(1)}, u32[]{:S(2)}, u32[]{:S(2)}) collective-permute-start(bf16[160,256]{1,0:T(8,128)(2,1)S(1)} %shard_map.121.refs_0_), channel_id=1, source_target_pairs={{0,28},{4,24},{8,20},{12,16},{16,12},{20,8},{24,4},{28,0},{1,29},{... | collective-permute-start | bytes 245768 | tf_op jit(solution)/shard_map/ppermute | solution.py:32
  54.8 22.5 %collective-permute-start.21 = (bf16[160,256]{1,0:T(8,128)(2,1)S(1)}, bf16[160,256]{1,0:T(8,128)(2,1)S(1)}, u32[]{:S(2)}, u32[]{:S(2)}) collective-permute-start(bf16[160,256]{1,0:T(8,128)(2,1)S(1)} %shard_map.121.refs_0_), channel_id=1, source_target_pairs={{0,24},{4,28},{8,16},{12,20},{16,8},{20,12},{24,0},{28,4},{1,25},{... | collective-permute-start | bytes 245768 | tf_op jit(solution)/shard_map/ppermute | solution.py:32
  57.8 20.1 %collective-permute-start.20 = (bf16[160,256]{1,0:T(8,128)(2,1)S(1)}, bf16[160,256]{1,0:T(8,128)(2,1)S(1)}, u32[]{:S(2)}, u32[]{:S(2)}) collective-permute-start(bf16[160,256]{1,0:T(8,128)(2,1)S(1)} %shard_map.121.refs_0_), channel_id=1, source_target_pairs={{0,20},{4,16},{8,28},{12,24},{16,4},{20,0},{24,12},{28,8},{1,21},{... | collective-permute-start | bytes 245768 | tf_op jit(solution)/shard_map/ppermute | solution.py:32
  68.6 19.1 %collective-permute-start.33 = (bf16[144,512]{1,0:T(8,128)(2,1)}, bf16[144,512]{1,0:T(8,128)(2,1)S(1)}, u32[]{:S(2)}, u32[]{:S(2)}) collective-permute-start(bf16[144,512]{1,0:T(8,128)(2,1)} %shard_map.119.query_ref), channel_id=1, source_target_pairs={{0,192},{64,128},{128,64},{192,0},{1,193},{65,129},{129,65},{193,1... | collective-permute-start | bytes 442376 | tf_op jit(solution)/shard_map/ppermute | solution.py:32
  73.5 7.5 %collective-permute-start.19 = (bf16[160,256]{1,0:T(8,128)(2,1)S(1)}, bf16[160,256]{1,0:T(8,128)(2,1)S(1)}, u32[]{:S(2)}, u32[]{:S(2)}) collective-permute-start(bf16[160,256]{1,0:T(8,128)(2,1)S(1)} %shard_map.121.refs_0_), channel_id=1, source_target_pairs={{0,16},{4,20},{8,24},{12,28},{16,0},{20,4},{24,8},{28,12},{1,17},{... | collective-permute-start | bytes 245768 | tf_op jit(solution)/shard_map/ppermute | solution.py:32
  74.7 6.9 %collective-permute-start.18 = (bf16[160,256]{1,0:T(8,128)(2,1)S(1)}, bf16[160,256]{1,0:T(8,128)(2,1)S(1)}, u32[]{:S(2)}, u32[]{:S(2)}) collective-permute-start(bf16[160,256]{1,0:T(8,128)(2,1)S(1)} %shard_map.121.refs_0_), channel_id=1, source_target_pairs={{0,12},{4,8},{8,4},{12,0},{16,28},{20,24},{24,20},{28,16},{1,13},{... | collective-permute-start | bytes 245768 | tf_op jit(solution)/shard_map/ppermute | solution.py:32
  83.5 9.1 %collective-permute-start.25 = (bf16[256,256]{1,0:T(8,128)(2,1)S(1)}, bf16[256,256]{1,0:T(8,128)(2,1)S(1)}, u32[]{:S(2)}, u32[]{:S(2)}) collective-permute-start(bf16[256,256]{1,0:T(8,128)(2,1)S(1)} %shard_map.123.refs_0_), channel_id=1, source_target_pairs={{0,3},{1,2},{2,1},{3,0},{4,7},{5,6},{6,5},{7,4},{8,11},{9,10},{10,... | collective-permute-start | bytes 393224 | tf_op jit(solution)/shard_map/ppermute | solution.py:32
  86.3 7.9 %collective-permute-start.24 = (bf16[256,256]{1,0:T(8,128)(2,1)S(1)}, bf16[256,256]{1,0:T(8,128)(2,1)S(1)}, u32[]{:S(2)}, u32[]{:S(2)}) collective-permute-start(bf16[256,256]{1,0:T(8,128)(2,1)S(1)} %shard_map.123.refs_0_), channel_id=1, source_target_pairs={{0,2},{1,3},{2,0},{3,1},{4,6},{5,7},{6,4},{7,5},{8,10},{9,11},{10,... | collective-permute-start | bytes 393224 | tf_op jit(solution)/shard_map/ppermute | solution.py:32
  87.0 7.2 %collective-permute-start.23 = (bf16[256,256]{1,0:T(8,128)(2,1)S(1)}, bf16[256,256]{1,0:T(8,128)(2,1)S(1)}, u32[]{:S(2)}, u32[]{:S(2)}) collective-permute-start(bf16[256,256]{1,0:T(8,128)(2,1)S(1)} %shard_map.123.refs_0_), channel_id=1, source_target_pairs={{0,1},{1,0},{2,3},{3,2},{4,5},{5,4},{6,7},{7,6},{8,9},{9,8},{10,11... | collective-permute-start | bytes 393224 | tf_op jit(solution)/shard_map/ppermute | solution.py:32
  87.7 12.9 %collective-permute-start.31 = (bf16[144,512]{1,0:T(8,128)(2,1)S(1)}, bf16[144,512]{1,0:T(8,128)(2,1)S(1)}, u32[]{:S(2)}, u32[]{:S(2)}) collective-permute-start(bf16[144,512]{1,0:T(8,128)(2,1)S(1)} %copy-done.3), channel_id=1, source_target_pairs={{0,64},{64,0},{128,192},{192,128},{1,65},{65,1},{129,193},{193,129... | collective-permute-start | bytes 442376 | tf_op jit(solution)/shard_map/ppermute | solution.py:32
  88.3 18.1 %collective-permute-start = (bf16[144,512]{1,0:T(8,128)(2,1)S(1)}, bf16[144,512]{1,0:T(8,128)(2,1)S(1)}, u32[]{:S(2)}, u32[]{:S(2)}) collective-permute-start(bf16[144,512]{1,0:T(8,128)(2,1)S(1)} %copy-done.3), channel_id=1, source_target_pairs={{0,128},{64,192},{128,0},{192,64},{1,129},{65,193},{129,1},{193,65... | collective-permute-start | bytes 442376 | tf_op jit(solution)/shard_map/ppermute | solution.py:32
  98.0 17.5 %collective-permute-start.34 = (bf16[128,512]{1,0:T(8,128)(2,1)S(1)}, bf16[128,512]{1,0:T(8,128)(2,1)S(1)}, u32[]{:S(2)}, u32[]{:S(2)}) collective-permute-start(bf16[128,512]{1,0:T(8,128)(2,1)S(1)} %shard_map.126), channel_id=1, source_target_pairs={{0,192},{64,128},{128,64},{192,0},{1,193},{65,129},{129,65},{193,1... | collective-permute-start | bytes 393224 | tf_op jit(solution)/shard_map/ppermute | solution.py:32
  102.8 12.7 %collective-permute-start.32 = (bf16[128,512]{1,0:T(8,128)(2,1)S(1)}, bf16[128,512]{1,0:T(8,128)(2,1)S(1)}, u32[]{:S(2)}, u32[]{:S(2)}) collective-permute-start(bf16[128,512]{1,0:T(8,128)(2,1)S(1)} %shard_map.125), channel_id=1, source_target_pairs={{0,64},{64,0},{128,192},{192,128},{1,65},{65,1},{129,193},{193,129... | collective-permute-start | bytes 393224 | tf_op jit(solution)/shard_map/ppermute | solution.py:32
  108.6 12.7 %collective-permute-start.30 = (bf16[128,512]{1,0:T(8,128)(2,1)S(1)}, bf16[128,512]{1,0:T(8,128)(2,1)S(1)}, u32[]{:S(2)}, u32[]{:S(2)}) collective-permute-start(bf16[128,512]{1,0:T(8,128)(2,1)S(1)} %shard_map.124), channel_id=1, source_target_pairs={{0,128},{64,192},{128,0},{192,64},{1,129},{65,193},{129,1},{193,65... | collective-permute-start | bytes 393224 | tf_op jit(solution)/shard_map/ppermute | solution.py:32
  (16 other events, 66.8 us)

commit v5 on v4

--- a/solution.py
+++ b/solution.py
@@ -14,7 +14,7 @@
 F32 = jnp.float32
 BF16 = jnp.bfloat16
 ZH, CORES, YS, ZL, XS = 4, 2, 4, 2, 4
-SHARE, SLOT = 20, 32
+SHARE, SLOT, STREAMS = 20, 32, 4
 TENSOR_ORDER, X_ORDER = (5, 7, 3, 4, 6, 2, 1), (2, 3, 1)
 TENSOR = YS * ZL
 NT = (((1,), (1,)), ((), ()))
@@ -140,14 +140,20 @@
     out_ref[:, HD:] = proj[:, HD:].astype(BF16)
 
 
-def query_part(x_ref, gain_ref, weight_ref, total, inverse, step):
-    depth = weight_ref.shape[0]
-    columns = pl.ds(pl.multiple_of(step * depth, depth), depth)
-    normed = x_ref[:, columns].astype(F32) * inverse[:, 0:1] * gain_ref[:, columns]
-    total[...] += jnp.dot(normed.astype(BF16), weight_ref[...], preferred_element_type=F32)
-
-
-def query_first_kernel(x_ref, gain_ref, weight_ref, total, inverse):
+def query_part(x_ref, gain_ref, weights, total, inverse, step):
+    depth = weights[0].shape[0]
+    out = total[...]
+    for k, weight_ref in enumerate(weights):
+        low = (step * STREAMS + k) * depth
+        columns = pl.ds(pl.multiple_of(low, depth), depth)
+        normed = x_ref[:, columns].astype(F32) * inverse[:, 0:1] * gain_ref[:, columns]
+        out = out + jnp.dot(normed.astype(BF16), weight_ref[...], preferred_element_type=F32)
+    total[...] = out
+
+
+def query_first_kernel(x_ref, gain_ref, *refs):
+    weights, (total, inverse) = refs[:STREAMS], refs[STREAMS:]
+
     @pl.when(pl.program_id(0) == 0)
     def _():
         square = jnp.zeros((x_ref.shape[0], 128), F32)
@@ -158,19 +164,19 @@
         inverse[...] = jnp.broadcast_to(lax.rsqrt(mean + EPSILON), inverse.shape)
         total[...] = jnp.zeros_like(total)
 
-    query_part(x_ref, gain_ref, weight_ref, total, inverse, pl.program_id(0))
-
-
-def query_last_kernel(
-    x_ref, gain_ref, weight_ref, begun, inverse, head_gain_ref, image_ref, count_ref, out_ref, total
-):
+    query_part(x_ref, gain_ref, weights, total, inverse, pl.program_id(0))
+
+
+def query_last_kernel(x_ref, gain_ref, *refs):
+    weights, refs = refs[:STREAMS], refs[STREAMS:]
+    begun, inverse, head_gain_ref, image_ref, count_ref, out_ref, total = refs
     rows = x_ref.shape[0]
 
     @pl.when(pl.program_id(0) == 0)
     def _():
         total[...] = begun[...]
 
-    query_part(x_ref, gain_ref, weight_ref, total, inverse, 0)
+    query_part(x_ref, gain_ref, weights, total, inverse, 0)
 
     @pl.when(pl.program_id(0) == pl.num_programs(0) - 1)
     def _():
@@ -186,34 +192,62 @@
         out_ref[rows:, rows:] = jnp.zeros((16, out_ref.shape[1] - rows), BF16)
 
 
-def decode_kernel(place_ref, query_ref, *refs):
-    slabs, out_ref = refs[:8], refs[8]
+def decode_rows(q, limit, first, slabs):
     keys = slabs[0].shape[0]
-    zh, x, c = place_ref[0], place_ref[1], place_ref[2]
     lane = lax.broadcasted_iota(jnp.int32, (1, keys), 1)
     base = ((lane >> 5) & 3) * 512 + (lane >> 7) * 128 + (lane & 31)
-    rows = out_ref.shape[0]
-    extra = query_ref[rows : rows + 8, :HD].astype(F32)
-    limit = jnp.where(extra[0:1] == zh.astype(F32), extra[1:2] * 16.0 + extra[2:3], 0.0)
-    limit = jnp.broadcast_to(limit, (8, rows)).T[:, 0:1]
-    limit = jnp.concatenate([limit] * 4, axis=0)
-    q = [query_ref[:rows, head * HD : (head + 1) * HD] for head in range(4)]
-    q = jnp.concatenate(q, axis=0)
-    mix = jnp.zeros((4 * rows, HD), F32)
-    total = jnp.zeros((4 * rows, 128), F32)
+    mix = jnp.zeros((q.shape[0], HD), F32)
+    total = jnp.zeros((q.shape[0], 128), F32)
     for j in range(8):
-        px = jnp.bitwise_xor(x, j % 4)
-        pc = jnp.bitwise_xor(c, j // 4)
-        pos = (base + (pc * 256 + px * 32)).astype(F32)
+        pos = (base + first[j]).astype(F32)
         s = lax.dot_general(q, slabs[j][:, :HD], NT, preferred_element_type=F32)
         w = jnp.where(pos < limit, jnp.exp(s), 0.0)
         total = total + (w[:, :128] + w[:, 128:])
         mix = mix + jnp.dot(w.astype(BF16), slabs[j][:, HD:], preferred_element_type=F32)
     total = jnp.sum(total, axis=-1, keepdims=True)
-    mix = mix / jnp.where(total > 0.0, total, 1.0)
-    for head in range(4):
-        part = mix[head * rows : (head + 1) * rows]
-        out_ref[:, head * HD : (head + 1) * HD] = part.astype(BF16)
+    return (mix / jnp.where(total > 0.0, total, 1.0)).astype(BF16)
+
+
+def decode_kernel(place_ref, query_ref, *refs):
+    slabs, out_ref = refs[:8], refs[8]
+    rows = out_ref.shape[0]
+    few = rows // 2
+    zh, x, c = place_ref[0], place_ref[1], place_ref[2]
+    first = [jnp.bitwise_xor(c, j // 4) * 256 + jnp.bitwise_xor(x, j % 4) * 32 for j in range(8)]
+    extra = query_ref[rows : rows + 8, :HD].astype(F32)
+    mine = extra[0:1] == zh.astype(F32)
+    limit = jnp.where(mine, extra[1:2] * 16.0 + extra[2:3], 0.0)
+    member = mine.astype(F32)
+    count = jnp.sum(member)
+
+    @pl.when(count <= few)
+    def _():
+        below = lax.broadcasted_iota(jnp.int32, (rows, rows), 0)
+        below = below < lax.broadcasted_iota(jnp.int32, (rows, rows), 1)
+        rank = jnp.dot(
+            jnp.broadcast_to(member, (8, rows)).astype(BF16),
+            below.astype(F32).astype(BF16),
+            preferred_element_type=F32,
+        )[0:1]
+        slot = lax.broadcasted_iota(jnp.int32, (few, rows), 0).astype(F32)
+        chosen = jnp.where(rank == slot, member, 0.0)
+        picked = chosen.astype(BF16)
+        q = jnp.dot(picked, query_ref[:rows, :], preferred_element_type=F32).astype(BF16)
+        q = jnp.concatenate([q[:, head * HD : (head + 1) * HD] for head in range(4)], axis=0)
+        bound = jnp.sum(chosen * limit, axis=-1, keepdims=True)
+        out = decode_rows(q, jnp.concatenate([bound] * 4, axis=0), first, slabs)
+        out = jnp.concatenate([out[head * few : (head + 1) * few] for head in range(4)], axis=1)
+        back = chosen.T.astype(BF16)
+        out_ref[...] = jnp.dot(back, out, preferred_element_type=F32).astype(BF16)
+
+    @pl.when(count > few)
+    def _():
+        bound = jnp.broadcast_to(limit, (8, rows)).T[:, 0:1]
+        q = [query_ref[:rows, head * HD : (head + 1) * HD] for head in range(4)]
+        q = jnp.concatenate(q, axis=0)
+        out = decode_rows(q, jnp.concatenate([bound] * 4, axis=0), first, slabs)
+        for head in range(4):
+            out_ref[:, head * HD : (head + 1) * HD] = out[head * rows : (head + 1) * rows]
 
 
 def limits(mib):
@@ -263,6 +297,15 @@
     dec_width, query_width = query_weight.shape
     fixed = lambda shape: pl.BlockSpec(shape, lambda i: (0, 0))
     gain_view = dec_gain.reshape(1, -1)
+    weights = [query_weight] * STREAMS
+
+    def weight_blocks(begin):
+        shape = (depth // STREAMS, query_width)
+        return [
+            pl.BlockSpec(shape, lambda i, k=k: ((i + begin) * STREAMS + k, 0))
+            for k in range(STREAMS)
+        ]
+
     begun, inverse = pl.pallas_call(
         query_first_kernel,
         grid=(first_steps,),
@@ -273,11 +316,11 @@
         in_specs=[
             fixed((dec_rows, dec_width)),
             fixed((1, dec_width)),
-            pl.BlockSpec((depth, query_width), lambda i: (i, 0)),
-        ],
+        ]
+        + weight_blocks(0),
         out_specs=(fixed((dec_rows, query_width)), fixed((dec_rows, 128))),
         compiler_params=limits(56),
-    )(dec_hidden, gain_view, query_weight)
+    )(dec_hidden, gain_view, *weights)
     message = pl.pallas_call(
         query_last_kernel,
         grid=(last_steps,),
@@ -285,7 +328,7 @@
         in_specs=[
             pl.BlockSpec((dec_rows, depth), lambda i: (0, i + first_steps)),
             pl.BlockSpec((1, depth), lambda i: (0, i + first_steps)),
-            pl.BlockSpec((depth, query_width), lambda i: (i + first_steps, 0)),
+            *weight_blocks(first_steps),
             fixed((dec_rows, query_width)),
             fixed((dec_rows, 128)),
             fixed((1, HD)),
@@ -298,7 +341,7 @@
     )(
         dec_hidden,
         gain_view,
-        query_weight,
+        *weights,
         begun,
         inverse,
         query_gain.reshape(1, -1),

time: 122 us -> 122 us (level)
  transfers between devices with their start and end apart: 35 -> 35, of which waited for: 19 -> 19; matrix products, arithmetic and copies ran while one was open for 1% -> 1% of each run, Pallas kernels for 18% -> 17%
where the time goes in v5:
time: 122 us
  starting transfers between devices  59.1 us (48%)
  waiting for transfers between devices  33.6 us (28%)
  Pallas kernels  25 us (20%)
  local copies, waits for them, and re-layouts  3.11 us (3%)
    ppermute x34, starting transfers between devices, xor_permute(): return lax.ppermute(values, axes, [(i, i ^ step) for i in range(size)])  55.1 us
    ppermute x34, waiting for transfers between devices, xor_permute(): return lax.ppermute(values, axes, [(i, i ^ step) for i in range(size)])  30.9 us
    pallas_call x4, Pallas kernels, on_device(): pl.pallas_call(decode_kernel, out_shape=jax.ShapeDtypeStruct((dec_rows, 4...  8.12 us
    pallas_call x1, Pallas kernels, on_device(): pl.pallas_call(query_last_kernel, grid=(last_steps,), out_shape=jax.Shape...  6.7 us
    pallas_call x1, Pallas kernels, on_device(): pl.pallas_call(query_first_kernel, grid=(first_steps,), out_shape=(jax.Sh...  4.02 us
    ppermute x1, starting transfers between devices, image_permute(): return lax.ppermute(values, ('zh', 'y', 'zl'), pairs)  3.94 us
    ppermute x1, waiting for transfers between devices, image_permute(): return lax.ppermute(values, ('zh', 'y', 'zl'), pairs)  2.66 us
  transfers between devices with their start and end apart: 35, of which 19 were waited for; matrix products, arithmetic and copies ran while one was open for 1% of the time, Pallas kernels for 17%

profile of v5, /device:TPU:32, one launch (start us, length us, event | category | flops | bytes accessed | tf_op | source)
XLA Modules:
  0.0 121.7 jit_solution(12451047656551069698)
XLA Ops:
  0.0 3.9 %collective-permute-start.1 = (bf16[32,1280]{1,0:T(8,128)(2,1)}, bf16[32,1280]{1,0:T(8,128)(2,1)S(1)}, u32[]{:S(2)}, u32[]{:S(2)}) collective-permute-start(bf16[32,1280]{1,0:T(8,128)(2,1)} %param.12), channel_id=1, source_target_pairs={{0,0},{4,64},{8,128},{12,192},{16,16},{20,80},{24,144},{28,208},{6... | collective-permute-start | bytes 245768 | tf_op jit(solution)/shard_map/ppermute | solution.py:42
  4.0 2.7 %collective-permute-done.1 = bf16[32,1280]{1,0:T(8,128)(2,1)S(1)} collective-permute-done((bf16[32,1280]{1,0:T(8,128)(2,1)}, bf16[32,1280]{1,0:T(8,128)(2,1)S(1)}, u32[]{:S(2)}, u32[]{:S(2)}) %collective-permute-start.1) | collective-permute-done | bytes 81952 | tf_op jit(solution)/shard_map/ppermute | solution.py:42
  6.7 8.1 %collective-permute-start.8 = (bf16[56,1280]{1,0:T(8,128)(2,1)S(1)}, bf16[56,1280]{1,0:T(8,128)(2,1)S(1)}, u32[]{:S(2)}, u32[]{:S(2)}) collective-permute-start(bf16[56,1280]{1,0:T(8,128)(2,1)S(1)} %fusion.1.refs_0_), channel_id=1, source_target_pairs={{0,28},{4,24},{8,20},{12,16},{16,12},{20,8},{24,4},{28,0},{1,29},{... | collective-permute-start | bytes 430088 | tf_op jit(solution)/shard_map/ppermute | solution.py:32
  17.0 3.2 %collective-permute-start.5 = (bf16[56,1280]{1,0:T(8,128)(2,1)S(1)}, bf16[56,1280]{1,0:T(8,128)(2,1)S(1)}, u32[]{:S(2)}, u32[]{:S(2)}) collective-permute-start(bf16[56,1280]{1,0:T(8,128)(2,1)S(1)} %fusion.1.refs_0_), channel_id=1, source_target_pairs={{0,16},{4,20},{8,24},{12,28},{16,0},{20,4},{24,8},{28,12},{1,17},{... | collective-permute-start | bytes 430088 | tf_op jit(solution)/shard_map/ppermute | solution.py:32
  22.3 4.0 %collective-permute-done.7.refs_6_ = bf16[56,1280]{1,0:T(8,128)(2,1)S(1)} collective-permute-done((bf16[56,1280]{1,0:T(8,128)(2,1)S(1)}, bf16[56,1280]{1,0:T(8,128)(2,1)S(1)}, u32[]{:S(2)}, u32[]{:S(2)}) %collective-permute-start.7) | collective-permute-done | bytes 143392 | tf_op jit(solution)/shard_map/ppermute | solution.py:32
  26.3 2.2 %collective-permute-start.2 = (bf16[56,1280]{1,0:T(8,128)(2,1)S(1)}, bf16[56,1280]{1,0:T(8,128)(2,1)S(1)}, u32[]{:S(2)}, u32[]{:S(2)}) collective-permute-start(bf16[56,1280]{1,0:T(8,128)(2,1)S(1)} %fusion.1.refs_0_), channel_id=1, source_target_pairs={{0,4},{4,0},{8,12},{12,8},{16,20},{20,16},{24,28},{28,24},{1,5},{5... | collective-permute-start | bytes 430088 | tf_op jit(solution)/shard_map/ppermute | solution.py:32
  35.8 2.8 %collective-permute-start.11 = (bf16[480,256]{1,0:T(8,128)(2,1)S(1)}, bf16[480,256]{1,0:T(8,128)(2,1)S(1)}, u32[]{:S(2)}, u32[]{:S(2)}) collective-permute-start(bf16[480,256]{1,0:T(8,128)(2,1)S(1)} %get-tuple-element.13.refs_0_), channel_id=1, source_target_pairs={{0,3},{1,2},{2,1},{3,0},{4,7},{5,6},{6,5},{7,4},{8,11},{9,10},{10,... | collective-permute-start | bytes 737288 | tf_op jit(solution)/shard_map/ppermute | solution.py:32
  40.0 9.2 %collective-permute-done.11.refs_3_ = bf16[480,256]{1,0:T(8,128)(2,1)S(1)} collective-permute-done((bf16[480,256]{1,0:T(8,128)(2,1)S(1)}, bf16[480,256]{1,0:T(8,128)(2,1)S(1)}, u32[]{:S(2)}, u32[]{:S(2)}) %collective-permute-start.11) | collective-permute-done | bytes 245792 | tf_op jit(solution)/shard_map/ppermute | solution.py:32
  51.4 2.4 %shard_map.121.refs_0_ = bf16[160,256]{1,0:T(8,128)(2,1)S(1)} custom-call(bf16[2,256,80]{2,1,0:T(8,128)(2,1)S(1)} %get-tuple-element.12.q_ref, bf16[480,256]{1,0:T(8,128)(2,1)S(1)} %get-tuple-element.13.refs_0_, bf16[480,256]{1,0:T(8,128)(2,1)S(1)} %collective-permute-done.9.refs_1_, bf16[480,256]{1,0:T(8,128)(2,1)S(1)} %collective-permute-done.10.refs_2_, ...), custom_call_target="tpu_custom_call" | custom-call | tf_op jit(solution)/shard_map/pallas_call | solution.py:376
  54.8 3.0 %collective-permute-start.21 = (bf16[160,256]{1,0:T(8,128)(2,1)S(1)}, bf16[160,256]{1,0:T(8,128)(2,1)S(1)}, u32[]{:S(2)}, u32[]{:S(2)}) collective-permute-start(bf16[160,256]{1,0:T(8,128)(2,1)S(1)} %shard_map.121.refs_0_), channel_id=1, source_target_pairs={{0,24},{4,28},{8,16},{12,20},{16,8},{20,12},{24,0},{28,4},{1,25},{... | collective-permute-start | bytes 245768 | tf_op jit(solution)/shard_map/ppermute | solution.py:32
  58.0 4.0 %shard_map.118 = (f32[128,512]{1,0:T(8,128)}, f32[128,128]{1,0:T(8,128)}) custom-call(bf16[128,8192]{1,0:T(8,128)(2,1)} %x_ref.3, f32[1,8192]{1,0:T(1,128)} %bitcast.12, bf16[8192,512]{1,0:T(8,128)(2,1)} %refs_3_.3, bf16[8192,512]{1,0:T(8,128)(2,1)} %refs_3_.3, bf16[8192,512]{1,0:T(8,128)(2,1)} %refs_3_.3, bf16[8192,512]{1,0:T(8,128)(2,1)} %refs_3_.3), custom_call_target="tpu_custom_call" | custom-call | tf_op jit(solution)/shard_map/pallas_call | solution.py:309
  62.0 6.7 %shard_map.119.query_ref = bf16[144,512]{1,0:T(8,128)(2,1)} custom-call(bf16[128,8192]{1,0:T(8,128)(2,1)} %x_ref.3, f32[1,8192]{1,0:T(1,128)} %bitcast.13, bf16[8192,512]{1,0:T(8,128)(2,1)} %refs_3_.3, bf16[8192,512]{1,0:T(8,128)(2,1)} %refs_3_.3, bf16[8192,512]{1,0:T(8,128)(2,1)} %refs_3_.3, bf16[8192,512]{1,0:T(8,128)(2,1)} %refs_3_.3, ...), custom_call_target="tpu_custom_call" | custom-call | tf_op jit(solution)/shard_map/pallas_call | solution.py:324
  68.7 5.0 %collective-permute-start.33 = (bf16[144,512]{1,0:T(8,128)(2,1)}, bf16[144,512]{1,0:T(8,128)(2,1)S(1)}, u32[]{:S(2)}, u32[]{:S(2)}) collective-permute-start(bf16[144,512]{1,0:T(8,128)(2,1)} %shard_map.119.query_ref), channel_id=1, source_target_pairs={{0,192},{64,128},{128,64},{192,0},{1,193},{65,129},{129,65},{193,1... | collective-permute-start | bytes 442376 | tf_op jit(solution)/shard_map/ppermute | solution.py:32
  75.0 2.6 %collective-permute-start.18 = (bf16[160,256]{1,0:T(8,128)(2,1)S(1)}, bf16[160,256]{1,0:T(8,128)(2,1)S(1)}, u32[]{:S(2)}, u32[]{:S(2)}) collective-permute-start(bf16[160,256]{1,0:T(8,128)(2,1)S(1)} %shard_map.121.refs_0_), channel_id=1, source_target_pairs={{0,12},{4,8},{8,4},{12,0},{16,28},{20,24},{24,20},{28,16},{1,13},{... | collective-permute-start | bytes 245768 | tf_op jit(solution)/shard_map/ppermute | solution.py:32
  83.7 2.8 %collective-permute-start.25 = (bf16[256,256]{1,0:T(8,128)(2,1)S(1)}, bf16[256,256]{1,0:T(8,128)(2,1)S(1)}, u32[]{:S(2)}, u32[]{:S(2)}) collective-permute-start(bf16[256,256]{1,0:T(8,128)(2,1)S(1)} %shard_map.123.refs_0_), channel_id=1, source_target_pairs={{0,3},{1,2},{2,1},{3,0},{4,7},{5,6},{6,5},{7,4},{8,11},{9,10},{10,... | collective-permute-start | bytes 393224 | tf_op jit(solution)/shard_map/ppermute | solution.py:32
  88.5 4.3 %collective-permute-start = (bf16[144,512]{1,0:T(8,128)(2,1)S(1)}, bf16[144,512]{1,0:T(8,128)(2,1)S(1)}, u32[]{:S(2)}, u32[]{:S(2)}) collective-permute-start(bf16[144,512]{1,0:T(8,128)(2,1)S(1)} %copy-done.3), channel_id=1, source_target_pairs={{0,128},{64,192},{128,0},{192,64},{1,129},{65,193},{129,1},{193,65... | collective-permute-start | bytes 442376 | tf_op jit(solution)/shard_map/ppermute | solution.py:32
  96.0 2.2 %shard_map.126 = bf16[128,512]{1,0:T(8,128)(2,1)S(1)} custom-call(s32[3]{0:T(128)S(1)} %pad_add_fusion.place_ref, bf16[144,512]{1,0:T(8,128)(2,1)S(1)} %collective-permute-done.33.query_ref, bf16[256,256]{1,0:T(8,128)(2,1)S(1)} %shard_map.123.refs_0_, bf16[256,256]{1,0:T(8,128)(2,1)S(1)} %collective-permute-done.23.refs_1_, ...), custom_call_target="tpu_custom_call" | custom-call | tf_op jit(solution)/shard_map/pallas_call | solution.py:403
  99.1 1.7 %collective-permute-done.31.query_ref = bf16[144,512]{1,0:T(8,128)(2,1)S(1)} collective-permute-done((bf16[144,512]{1,0:T(8,128)(2,1)S(1)}, bf16[144,512]{1,0:T(8,128)(2,1)S(1)}, u32[]{:S(2)}, u32[]{:S(2)}) %collective-permute-start.31) | collective-permute-done | bytes 147488 | tf_op jit(solution)/shard_map/ppermute | solution.py:32
  100.8 2.0 %shard_map.125 = bf16[128,512]{1,0:T(8,128)(2,1)S(1)} custom-call(s32[3]{0:T(128)S(1)} %pad_add_fusion.place_ref, bf16[144,512]{1,0:T(8,128)(2,1)S(1)} %collective-permute-done.31.query_ref, bf16[256,256]{1,0:T(8,128)(2,1)S(1)} %shard_map.123.refs_0_, bf16[256,256]{1,0:T(8,128)(2,1)S(1)} %collective-permute-done.23.refs_1_, ...), custom_call_target="tpu_custom_call" | custom-call | tf_op jit(solution)/shard_map/pallas_call | solution.py:403
  102.8 3.5 %collective-permute-start.32 = (bf16[128,512]{1,0:T(8,128)(2,1)S(1)}, bf16[128,512]{1,0:T(8,128)(2,1)S(1)}, u32[]{:S(2)}, u32[]{:S(2)}) collective-permute-start(bf16[128,512]{1,0:T(8,128)(2,1)S(1)} %shard_map.125), channel_id=1, source_target_pairs={{0,64},{64,0},{128,192},{192,128},{1,65},{65,1},{129,193},{193,129... | collective-permute-start | bytes 393224 | tf_op jit(solution)/shard_map/ppermute | solution.py:32
  106.3 2.0 %shard_map.124 = bf16[128,512]{1,0:T(8,128)(2,1)S(1)} custom-call(s32[3]{0:T(128)S(1)} %pad_add_fusion.place_ref, bf16[144,512]{1,0:T(8,128)(2,1)S(1)} %collective-permute-done.query_ref, bf16[256,256]{1,0:T(8,128)(2,1)S(1)} %shard_map.123.refs_0_, bf16[256,256]{1,0:T(8,128)(2,1)S(1)} %collective-permute-done.23.refs_1_, ...), custom_call_target="tpu_custom_call" | custom-call | tf_op jit(solution)/shard_map/pallas_call | solution.py:403
  108.2 4.7 %collective-permute-start.30 = (bf16[128,512]{1,0:T(8,128)(2,1)S(1)}, bf16[128,512]{1,0:T(8,128)(2,1)S(1)}, u32[]{:S(2)}, u32[]{:S(2)}) collective-permute-start(bf16[128,512]{1,0:T(8,128)(2,1)S(1)} %shard_map.124), channel_id=1, source_target_pairs={{0,128},{64,192},{128,0},{192,64},{1,129},{65,193},{129,1},{193,65... | collective-permute-start | bytes 393224 | tf_op jit(solution)/shard_map/ppermute | solution.py:32
  113.0 2.0 %shard_map.127 = bf16[128,512]{1,0:T(8,128)(2,1)S(1)} custom-call(s32[3]{0:T(128)S(1)} %pad_add_fusion.place_ref, bf16[144,512]{1,0:T(8,128)(2,1)S(1)} %copy-done.3, bf16[256,256]{1,0:T(8,128)(2,1)S(1)} %shard_map.123.refs_0_, bf16[256,256]{1,0:T(8,128)(2,1)S(1)} %collective-permute-done.23.refs_1_, bf16[256,256]{1,0:T(8,128)(2,1)S(1)} %collective-permute-done.24.refs_2_, ...), custom_call_target="tpu_custom_call" | custom-call | tf_op jit(solution)/shard_map/pallas_call | solution.py:403
  115.0 6.0 %collective-permute-done.30 = bf16[128,512]{1,0:T(8,128)(2,1)S(1)} collective-permute-done((bf16[128,512]{1,0:T(8,128)(2,1)S(1)}, bf16[128,512]{1,0:T(8,128)(2,1)S(1)}, u32[]{:S(2)}, u32[]{:S(2)}) %collective-permute-start.30) | collective-permute-done | bytes 131104 | tf_op jit(solution)/shard_map/ppermute | solution.py:32
  (71 shorter events, 30.5 us)
Async XLA Ops:
  6.7 14.1 %collective-permute-start.8 = (bf16[56,1280]{1,0:T(8,128)(2,1)S(1)}, bf16[56,1280]{1,0:T(8,128)(2,1)S(1)}, u32[]{:S(2)}, u32[]{:S(2)}) collective-permute-start(bf16[56,1280]{1,0:T(8,128)(2,1)S(1)} %fusion.1.refs_0_), channel_id=1, source_target_pairs={{0,28},{4,24},{8,20},{12,16},{16,12},{20,8},{24,4},{28,0},{1,29},{... | collective-permute-start | bytes 430088 | tf_op jit(solution)/shard_map/ppermute | solution.py:32
  14.8 11.5 %collective-permute-start.7 = (bf16[56,1280]{1,0:T(8,128)(2,1)S(1)}, bf16[56,1280]{1,0:T(8,128)(2,1)S(1)}, u32[]{:S(2)}, u32[]{:S(2)}) collective-permute-start(bf16[56,1280]{1,0:T(8,128)(2,1)S(1)} %fusion.1.refs_0_), channel_id=1, source_target_pairs={{0,24},{4,28},{8,16},{12,20},{16,8},{20,12},{24,0},{28,4},{1,25},{... | collective-permute-start | bytes 430088 | tf_op jit(solution)/shard_map/ppermute | solution.py:32
  15.8 13.3 %collective-permute-start.6 = (bf16[56,1280]{1,0:T(8,128)(2,1)S(1)}, bf16[56,1280]{1,0:T(8,128)(2,1)S(1)}, u32[]{:S(2)}, u32[]{:S(2)}) collective-permute-start(bf16[56,1280]{1,0:T(8,128)(2,1)S(1)} %fusion.1.refs_0_), channel_id=1, source_target_pairs={{0,20},{4,16},{8,28},{12,24},{16,4},{20,0},{24,12},{28,8},{1,21},{... | collective-permute-start | bytes 430088 | tf_op jit(solution)/shard_map/ppermute | solution.py:32
  17.0 12.5 %collective-permute-start.5 = (bf16[56,1280]{1,0:T(8,128)(2,1)S(1)}, bf16[56,1280]{1,0:T(8,128)(2,1)S(1)}, u32[]{:S(2)}, u32[]{:S(2)}) collective-permute-start(bf16[56,1280]{1,0:T(8,128)(2,1)S(1)} %fusion.1.refs_0_), channel_id=1, source_target_pairs={{0,16},{4,20},{8,24},{12,28},{16,0},{20,4},{24,8},{28,12},{1,17},{... | collective-permute-start | bytes 430088 | tf_op jit(solution)/shard_map/ppermute | solution.py:32
  20.2 9.3 %collective-permute-start.4 = (bf16[56,1280]{1,0:T(8,128)(2,1)S(1)}, bf16[56,1280]{1,0:T(8,128)(2,1)S(1)}, u32[]{:S(2)}, u32[]{:S(2)}) collective-permute-start(bf16[56,1280]{1,0:T(8,128)(2,1)S(1)} %fusion.1.refs_0_), channel_id=1, source_target_pairs={{0,12},{4,8},{8,4},{12,0},{16,28},{20,24},{24,20},{28,16},{1,13},{... | collective-permute-start | bytes 430088 | tf_op jit(solution)/shard_map/ppermute | solution.py:32
  20.7 10.4 %collective-permute-start.3 = (bf16[56,1280]{1,0:T(8,128)(2,1)S(1)}, bf16[56,1280]{1,0:T(8,128)(2,1)S(1)}, u32[]{:S(2)}, u32[]{:S(2)}) collective-permute-start(bf16[56,1280]{1,0:T(8,128)(2,1)S(1)} %fusion.1.refs_0_), channel_id=1, source_target_pairs={{0,8},{4,12},{8,0},{12,4},{16,24},{20,28},{24,16},{28,20},{1,9},{5... | collective-permute-start | bytes 430088 | tf_op jit(solution)/shard_map/ppermute | solution.py:32
  35.8 13.3 %collective-permute-start.11 = (bf16[480,256]{1,0:T(8,128)(2,1)S(1)}, bf16[480,256]{1,0:T(8,128)(2,1)S(1)}, u32[]{:S(2)}, u32[]{:S(2)}) collective-permute-start(bf16[480,256]{1,0:T(8,128)(2,1)S(1)} %get-tuple-element.13.refs_0_), channel_id=1, source_target_pairs={{0,3},{1,2},{2,1},{3,0},{4,7},{5,6},{6,5},{7,4},{8,11},{9,10},{10,... | collective-permute-start | bytes 737288 | tf_op jit(solution)/shard_map/ppermute | solution.py:32
  38.7 10.5 %collective-permute-start.10 = (bf16[480,256]{1,0:T(8,128)(2,1)S(1)}, bf16[480,256]{1,0:T(8,128)(2,1)S(1)}, u32[]{:S(2)}, u32[]{:S(2)}) collective-permute-start(bf16[480,256]{1,0:T(8,128)(2,1)S(1)} %get-tuple-element.13.refs_0_), channel_id=1, source_target_pairs={{0,2},{1,3},{2,0},{3,1},{4,6},{5,7},{6,4},{7,5},{8,10},{9,11},{10,... | collective-permute-start | bytes 737288 | tf_op jit(solution)/shard_map/ppermute | solution.py:32
  39.5 10.3 %collective-permute-start.9 = (bf16[480,256]{1,0:T(8,128)(2,1)S(1)}, bf16[480,256]{1,0:T(8,128)(2,1)S(1)}, u32[]{:S(2)}, u32[]{:S(2)}) collective-permute-start(bf16[480,256]{1,0:T(8,128)(2,1)S(1)} %get-tuple-element.13.refs_0_), channel_id=1, source_target_pairs={{0,1},{1,0},{2,3},{3,2},{4,5},{5,4},{6,7},{7,6},{8,9},{9,8},{10,11... | collective-permute-start | bytes 737288 | tf_op jit(solution)/shard_map/ppermute | solution.py:32
  40.0 9.8 %collective-permute-start.12 = (bf16[480,256]{1,0:T(8,128)(2,1)S(1)}, bf16[480,256]{1,0:T(8,128)(2,1)S(1)}, u32[]{:S(2)}, u32[]{:S(2)}) collective-permute-start(bf16[480,256]{1,0:T(8,128)(2,1)S(1)} %get-tuple-element.13.refs_0_), channel_id=1, source_target_pairs={{0,32},{32,0},{1,33},{33,1},{2,34},{34,2},{3,35},{35,3},{4,36},{36... | collective-permute-start | bytes 737288 | tf_op jit(solution)/shard_map/ppermute | solution.py:32
  53.8 21.2 %collective-permute-start.22 = (bf16[160,256]{1,0:T(8,128)(2,1)S(1)}, bf16[160,256]{1,0:T(8,128)(2,1)S(1)}, u32[]{:S(2)}, u32[]{:S(2)}) collective-permute-start(bf16[160,256]{1,0:T(8,128)(2,1)S(1)} %shard_map.121.refs_0_), channel_id=1, source_target_pairs={{0,28},{4,24},{8,20},{12,16},{16,12},{20,8},{24,4},{28,0},{1,29},{... | collective-permute-start | bytes 245768 | tf_op jit(solution)/shard_map/ppermute | solution.py:32
  54.8 22.7 %collective-permute-start.21 = (bf16[160,256]{1,0:T(8,128)(2,1)S(1)}, bf16[160,256]{1,0:T(8,128)(2,1)S(1)}, u32[]{:S(2)}, u32[]{:S(2)}) collective-permute-start(bf16[160,256]{1,0:T(8,128)(2,1)S(1)} %shard_map.121.refs_0_), channel_id=1, source_target_pairs={{0,24},{4,28},{8,16},{12,20},{16,8},{20,12},{24,0},{28,4},{1,25},{... | collective-permute-start | bytes 245768 | tf_op jit(solution)/shard_map/ppermute | solution.py:32
  57.8 20.4 %collective-permute-start.20 = (bf16[160,256]{1,0:T(8,128)(2,1)S(1)}, bf16[160,256]{1,0:T(8,128)(2,1)S(1)}, u32[]{:S(2)}, u32[]{:S(2)}) collective-permute-start(bf16[160,256]{1,0:T(8,128)(2,1)S(1)} %shard_map.121.refs_0_), channel_id=1, source_target_pairs={{0,20},{4,16},{8,28},{12,24},{16,4},{20,0},{24,12},{28,8},{1,21},{... | collective-permute-start | bytes 245768 | tf_op jit(solution)/shard_map/ppermute | solution.py:32
  68.7 19.2 %collective-permute-start.33 = (bf16[144,512]{1,0:T(8,128)(2,1)}, bf16[144,512]{1,0:T(8,128)(2,1)S(1)}, u32[]{:S(2)}, u32[]{:S(2)}) collective-permute-start(bf16[144,512]{1,0:T(8,128)(2,1)} %shard_map.119.query_ref), channel_id=1, source_target_pairs={{0,192},{64,128},{128,64},{192,0},{1,193},{65,129},{129,65},{193,1... | collective-permute-start | bytes 442376 | tf_op jit(solution)/shard_map/ppermute | solution.py:32
  73.7 7.5 %collective-permute-start.19 = (bf16[160,256]{1,0:T(8,128)(2,1)S(1)}, bf16[160,256]{1,0:T(8,128)(2,1)S(1)}, u32[]{:S(2)}, u32[]{:S(2)}) collective-permute-start(bf16[160,256]{1,0:T(8,128)(2,1)S(1)} %shard_map.121.refs_0_), channel_id=1, source_target_pairs={{0,16},{4,20},{8,24},{12,28},{16,0},{20,4},{24,8},{28,12},{1,17},{... | collective-permute-start | bytes 245768 | tf_op jit(solution)/shard_map/ppermute | solution.py:32
  75.0 6.9 %collective-permute-start.18 = (bf16[160,256]{1,0:T(8,128)(2,1)S(1)}, bf16[160,256]{1,0:T(8,128)(2,1)S(1)}, u32[]{:S(2)}, u32[]{:S(2)}) collective-permute-start(bf16[160,256]{1,0:T(8,128)(2,1)S(1)} %shard_map.121.refs_0_), channel_id=1, source_target_pairs={{0,12},{4,8},{8,4},{12,0},{16,28},{20,24},{24,20},{28,16},{1,13},{... | collective-permute-start | bytes 245768 | tf_op jit(solution)/shard_map/ppermute | solution.py:32
  83.7 9.1 %collective-permute-start.25 = (bf16[256,256]{1,0:T(8,128)(2,1)S(1)}, bf16[256,256]{1,0:T(8,128)(2,1)S(1)}, u32[]{:S(2)}, u32[]{:S(2)}) collective-permute-start(bf16[256,256]{1,0:T(8,128)(2,1)S(1)} %shard_map.123.refs_0_), channel_id=1, source_target_pairs={{0,3},{1,2},{2,1},{3,0},{4,7},{5,6},{6,5},{7,4},{8,11},{9,10},{10,... | collective-permute-start | bytes 393224 | tf_op jit(solution)/shard_map/ppermute | solution.py:32
  86.6 7.9 %collective-permute-start.24 = (bf16[256,256]{1,0:T(8,128)(2,1)S(1)}, bf16[256,256]{1,0:T(8,128)(2,1)S(1)}, u32[]{:S(2)}, u32[]{:S(2)}) collective-permute-start(bf16[256,256]{1,0:T(8,128)(2,1)S(1)} %shard_map.123.refs_0_), channel_id=1, source_target_pairs={{0,2},{1,3},{2,0},{3,1},{4,6},{5,7},{6,4},{7,5},{8,10},{9,11},{10,... | collective-permute-start | bytes 393224 | tf_op jit(solution)/shard_map/ppermute | solution.py:32
  87.3 7.2 %collective-permute-start.23 = (bf16[256,256]{1,0:T(8,128)(2,1)S(1)}, bf16[256,256]{1,0:T(8,128)(2,1)S(1)}, u32[]{:S(2)}, u32[]{:S(2)}) collective-permute-start(bf16[256,256]{1,0:T(8,128)(2,1)S(1)} %shard_map.123.refs_0_), channel_id=1, source_target_pairs={{0,1},{1,0},{2,3},{3,2},{4,5},{5,4},{6,7},{7,6},{8,9},{9,8},{10,11... | collective-permute-start | bytes 393224 | tf_op jit(solution)/shard_map/ppermute | solution.py:32
  87.9 12.9 %collective-permute-start.31 = (bf16[144,512]{1,0:T(8,128)(2,1)S(1)}, bf16[144,512]{1,0:T(8,128)(2,1)S(1)}, u32[]{:S(2)}, u32[]{:S(2)}) collective-permute-start(bf16[144,512]{1,0:T(8,128)(2,1)S(1)} %copy-done.3), channel_id=1, source_target_pairs={{0,64},{64,0},{128,192},{192,128},{1,65},{65,1},{129,193},{193,129... | collective-permute-start | bytes 442376 | tf_op jit(solution)/shard_map/ppermute | solution.py:32
  88.5 17.8 %collective-permute-start = (bf16[144,512]{1,0:T(8,128)(2,1)S(1)}, bf16[144,512]{1,0:T(8,128)(2,1)S(1)}, u32[]{:S(2)}, u32[]{:S(2)}) collective-permute-start(bf16[144,512]{1,0:T(8,128)(2,1)S(1)} %copy-done.3), channel_id=1, source_target_pairs={{0,128},{64,192},{128,0},{192,64},{1,129},{65,193},{129,1},{193,65... | collective-permute-start | bytes 442376 | tf_op jit(solution)/shard_map/ppermute | solution.py:32
  98.2 16.7 %collective-permute-start.34 = (bf16[128,512]{1,0:T(8,128)(2,1)S(1)}, bf16[128,512]{1,0:T(8,128)(2,1)S(1)}, u32[]{:S(2)}, u32[]{:S(2)}) collective-permute-start(bf16[128,512]{1,0:T(8,128)(2,1)S(1)} %shard_map.126), channel_id=1, source_target_pairs={{0,192},{64,128},{128,64},{192,0},{1,193},{65,129},{129,65},{193,1... | collective-permute-start | bytes 393224 | tf_op jit(solution)/shard_map/ppermute | solution.py:32
  102.8 12.2 %collective-permute-start.32 = (bf16[128,512]{1,0:T(8,128)(2,1)S(1)}, bf16[128,512]{1,0:T(8,128)(2,1)S(1)}, u32[]{:S(2)}, u32[]{:S(2)}) collective-permute-start(bf16[128,512]{1,0:T(8,128)(2,1)S(1)} %shard_map.125), channel_id=1, source_target_pairs={{0,64},{64,0},{128,192},{192,128},{1,65},{65,1},{129,193},{193,129... | collective-permute-start | bytes 393224 | tf_op jit(solution)/shard_map/ppermute | solution.py:32
  108.2 12.7 %collective-permute-start.30 = (bf16[128,512]{1,0:T(8,128)(2,1)S(1)}, bf16[128,512]{1,0:T(8,128)(2,1)S(1)}, u32[]{:S(2)}, u32[]{:S(2)}) collective-permute-start(bf16[128,512]{1,0:T(8,128)(2,1)S(1)} %shard_map.124), channel_id=1, source_target_pairs={{0,128},{64,192},{128,0},{192,64},{1,129},{65,193},{129,1},{193,65... | collective-permute-start | bytes 393224 | tf_op jit(solution)/shard_map/ppermute | solution.py:32
  (16 other events, 66.8 us)

commit v6 on v5

--- a/solution.py
+++ b/solution.py
@@ -1,3 +1,4 @@
+import functools
 import math
 
 import jax
@@ -140,48 +141,48 @@
     out_ref[:, HD:] = proj[:, HD:].astype(BF16)
 
 
-def query_part(x_ref, gain_ref, weights, total, inverse, step):
+def query_part(x_ref, gain_ref, weights, total, square):
     depth = weights[0].shape[0]
-    out = total[...]
+    out, squares = total[...], square[...]
     for k, weight_ref in enumerate(weights):
-        low = (step * STREAMS + k) * depth
-        columns = pl.ds(pl.multiple_of(low, depth), depth)
-        normed = x_ref[:, columns].astype(F32) * inverse[:, 0:1] * gain_ref[:, columns]
-        out = out + jnp.dot(normed.astype(BF16), weight_ref[...], preferred_element_type=F32)
-    total[...] = out
+        columns = slice(k * depth, (k + 1) * depth)
+        x = x_ref[:, columns].astype(F32)
+        for low in range(0, depth, 128):
+            part = x[:, low : low + 128]
+            squares = squares + part * part
+        scaled = (x * gain_ref[:, columns]).astype(BF16)
+        out = out + jnp.dot(scaled, weight_ref[...], preferred_element_type=F32)
+    total[...], square[...] = out, squares
 
 
 def query_first_kernel(x_ref, gain_ref, *refs):
-    weights, (total, inverse) = refs[:STREAMS], refs[STREAMS:]
+    weights, (total, square) = refs[:STREAMS], refs[STREAMS:]
 
     @pl.when(pl.program_id(0) == 0)
     def _():
-        square = jnp.zeros((x_ref.shape[0], 128), F32)
-        for low in range(0, x_ref.shape[1], 128):
-            part = x_ref[:, low : low + 128].astype(F32)
-            square = square + part * part
-        mean = jnp.sum(square, axis=-1, keepdims=True) / x_ref.shape[1]
-        inverse[...] = jnp.broadcast_to(lax.rsqrt(mean + EPSILON), inverse.shape)
         total[...] = jnp.zeros_like(total)
-
-    query_part(x_ref, gain_ref, weights, total, inverse, pl.program_id(0))
-
-
-def query_last_kernel(x_ref, gain_ref, *refs):
+        square[...] = jnp.zeros_like(square)
+
+    query_part(x_ref, gain_ref, weights, total, square)
+
+
+def query_last_kernel(width, x_ref, gain_ref, *refs):
     weights, refs = refs[:STREAMS], refs[STREAMS:]
-    begun, inverse, head_gain_ref, image_ref, count_ref, out_ref, total = refs
+    begun, squares, head_gain_ref, image_ref, count_ref, out_ref, total, square = refs
     rows = x_ref.shape[0]
 
     @pl.when(pl.program_id(0) == 0)
     def _():
         total[...] = begun[...]
-
-    query_part(x_ref, gain_ref, weights, total, inverse, 0)
+        square[...] = squares[...]
+
+    query_part(x_ref, gain_ref, weights, total, square)
 
     @pl.when(pl.program_id(0) == pl.num_programs(0) - 1)
     def _():
+        inverse = lax.rsqrt(jnp.sum(square[...], axis=-1, keepdims=True) / width + EPSILON)
         for head in range(4):
-            q = total[:, head * HD : (head + 1) * HD]
+            q = total[:, head * HD : (head + 1) * HD] * inverse
             mean = jnp.mean(q * q, axis=-1, keepdims=True)
             q = q * lax.rsqrt(mean + EPSILON) * head_gain_ref[...] / math.sqrt(HD)
             out_ref[:rows, head * HD : (head + 1) * HD] = q.astype(BF16)
@@ -293,7 +294,7 @@
     own = image_permute(patches)
 
     dec_rows = dec_hidden.shape[0]
-    depth, first_steps, last_steps = 1024, 2, 6
+    depth, first_steps, last_steps = 1024, 4, 4
     dec_width, query_width = query_weight.shape
     fixed = lambda shape: pl.BlockSpec(shape, lambda i: (0, 0))
     gain_view = dec_gain.reshape(1, -1)
@@ -306,7 +307,7 @@
             for k in range(STREAMS)
         ]
 
-    begun, inverse = pl.pallas_call(
+    begun, squares = pl.pallas_call(
         query_first_kernel,
         grid=(first_steps,),
         out_shape=(
@@ -314,15 +315,15 @@
             jax.ShapeDtypeStruct((dec_rows, 128), F32),
         ),
         in_specs=[
-            fixed((dec_rows, dec_width)),
-            fixed((1, dec_width)),
+            pl.BlockSpec((dec_rows, depth), lambda i: (0, i)),
+            pl.BlockSpec((1, depth), lambda i: (0, i)),
         ]
         + weight_blocks(0),
         out_specs=(fixed((dec_rows, query_width)), fixed((dec_rows, 128))),
         compiler_params=limits(56),
     )(dec_hidden, gain_view, *weights)
     message = pl.pallas_call(
-        query_last_kernel,
+        functools.partial(query_last_kernel, dec_width),
         grid=(last_steps,),
         out_shape=jax.ShapeDtypeStruct((dec_rows + 16, query_width), BF16),
         in_specs=[
@@ -336,14 +337,14 @@
             fixed((1, dec_rows)),
         ],
         out_specs=fixed((dec_rows + 16, query_width)),
-        scratch_shapes=[pltpu.VMEM((dec_rows, query_width), F32)],
+        scratch_shapes=[pltpu.VMEM((dec_rows, query_width), F32), pltpu.VMEM((dec_rows, 128), F32)],
         compiler_params=limits(56),
     )(
         dec_hidden,
         gain_view,
         *weights,
         begun,
-        inverse,
+        squares,
         query_gain.reshape(1, -1),
         image_of_row.reshape(1, -1),
         valid_count.reshape(1, -1),
@@ -371,7 +372,9 @@
         compiler_params=limits(16),
     )(me, *pieces, gain_row, enc_qkv.transpose(0, 2, 1), cross_kv)
     kv_pieces = gather_xc(kv)
-    every_query = [message] + [xor_permute(message, "zh", ZH, k) for k in range(1, ZH)]
+    every_query = [message]
+    for k in range(1, ZH):
+        every_query.append(xor_permute(message, "zh", ZH, k))
 
     attended = pl.pallas_call(
         encoder_kernel,

time: 122 us -> 121 us (level)
  Pallas kernels: 25 us -> 23.6 us
    pallas_call x1, Pallas kernels: 6.7 us -> 4.91 us  [on_device(): pl.pallas_call(functools.partial(query_last_kernel, dec_width), grid=(las...]
  transfers between devices with their start and end apart: 35 -> 35, of which waited for: 19 -> 19; matrix products, arithmetic and copies ran while one was open for 1% -> 1% of each run, Pallas kernels for 17% -> 16%
where the time goes in v6:
time: 121 us; the launch traced here: 120 us
  starting transfers between devices  59.1 us (49%)
  waiting for transfers between devices  33.5 us (28%)
  Pallas kernels  23.6 us (20%)
  local copies, waits for them, and re-layouts  3.11 us (3%)
    ppermute x34, starting transfers between devices, xor_permute(): return lax.ppermute(values, axes, [(i, i ^ step) for i in range(size)])  55.1 us
    ppermute x34, waiting for transfers between devices, xor_permute(): return lax.ppermute(values, axes, [(i, i ^ step) for i in range(size)])  30.9 us
    pallas_call x4, Pallas kernels, on_device(): pl.pallas_call(decode_kernel, out_shape=jax.ShapeDtypeStruct((dec_rows, 4...  8.12 us
    pallas_call x1, Pallas kernels, on_device(): pl.pallas_call(functools.partial(query_last_kernel, dec_width), grid=(las...  4.91 us
    pallas_call x1, Pallas kernels, on_device(): pl.pallas_call(query_first_kernel, grid=(first_steps,), out_shape=(jax.Sh...  4.45 us
    ppermute x1, starting transfers between devices, image_permute(): return lax.ppermute(values, ('zh', 'y', 'zl'), pairs)  3.94 us
    ppermute x1, waiting for transfers between devices, image_permute(): return lax.ppermute(values, ('zh', 'y', 'zl'), pairs)  2.66 us
  transfers between devices with their start and end apart: 35, of which 19 were waited for; matrix products, arithmetic and copies ran while one was open for 1% of the time, Pallas kernels for 16%

profile of v6, /device:TPU:32, one launch (start us, length us, event | category | flops | bytes accessed | tf_op | source)
XLA Modules:
  0.0 120.3 jit_solution(12403818887433603216)
XLA Ops:
  0.0 3.9 %collective-permute-start.1 = (bf16[32,1280]{1,0:T(8,128)(2,1)}, bf16[32,1280]{1,0:T(8,128)(2,1)S(1)}, u32[]{:S(2)}, u32[]{:S(2)}) collective-permute-start(bf16[32,1280]{1,0:T(8,128)(2,1)} %param.12), channel_id=1, source_target_pairs={{0,0},{4,64},{8,128},{12,192},{16,16},{20,80},{24,144},{28,208},{6... | collective-permute-start | bytes 245768 | tf_op jit(solution)/shard_map/ppermute | solution.py:43
  4.0 2.7 %collective-permute-done.1 = bf16[32,1280]{1,0:T(8,128)(2,1)S(1)} collective-permute-done((bf16[32,1280]{1,0:T(8,128)(2,1)}, bf16[32,1280]{1,0:T(8,128)(2,1)S(1)}, u32[]{:S(2)}, u32[]{:S(2)}) %collective-permute-start.1) | collective-permute-done | bytes 81952 | tf_op jit(solution)/shard_map/ppermute | solution.py:43
  6.7 8.1 %collective-permute-start.8 = (bf16[56,1280]{1,0:T(8,128)(2,1)S(1)}, bf16[56,1280]{1,0:T(8,128)(2,1)S(1)}, u32[]{:S(2)}, u32[]{:S(2)}) collective-permute-start(bf16[56,1280]{1,0:T(8,128)(2,1)S(1)} %fusion.1.refs_0_), channel_id=1, source_target_pairs={{0,28},{4,24},{8,20},{12,16},{16,12},{20,8},{24,4},{28,0},{1,29},{... | collective-permute-start | bytes 430088 | tf_op jit(solution)/shard_map/ppermute | solution.py:33
  17.0 3.2 %collective-permute-start.5 = (bf16[56,1280]{1,0:T(8,128)(2,1)S(1)}, bf16[56,1280]{1,0:T(8,128)(2,1)S(1)}, u32[]{:S(2)}, u32[]{:S(2)}) collective-permute-start(bf16[56,1280]{1,0:T(8,128)(2,1)S(1)} %fusion.1.refs_0_), channel_id=1, source_target_pairs={{0,16},{4,20},{8,24},{12,28},{16,0},{20,4},{24,8},{28,12},{1,17},{... | collective-permute-start | bytes 430088 | tf_op jit(solution)/shard_map/ppermute | solution.py:33
  22.3 4.0 %collective-permute-done.7.refs_6_ = bf16[56,1280]{1,0:T(8,128)(2,1)S(1)} collective-permute-done((bf16[56,1280]{1,0:T(8,128)(2,1)S(1)}, bf16[56,1280]{1,0:T(8,128)(2,1)S(1)}, u32[]{:S(2)}, u32[]{:S(2)}) %collective-permute-start.7) | collective-permute-done | bytes 143392 | tf_op jit(solution)/shard_map/ppermute | solution.py:33
  26.3 2.2 %collective-permute-start.2 = (bf16[56,1280]{1,0:T(8,128)(2,1)S(1)}, bf16[56,1280]{1,0:T(8,128)(2,1)S(1)}, u32[]{:S(2)}, u32[]{:S(2)}) collective-permute-start(bf16[56,1280]{1,0:T(8,128)(2,1)S(1)} %fusion.1.refs_0_), channel_id=1, source_target_pairs={{0,4},{4,0},{8,12},{12,8},{16,20},{20,16},{24,28},{28,24},{1,5},{5... | collective-permute-start | bytes 430088 | tf_op jit(solution)/shard_map/ppermute | solution.py:33
  35.8 2.8 %collective-permute-start.11 = (bf16[480,256]{1,0:T(8,128)(2,1)S(1)}, bf16[480,256]{1,0:T(8,128)(2,1)S(1)}, u32[]{:S(2)}, u32[]{:S(2)}) collective-permute-start(bf16[480,256]{1,0:T(8,128)(2,1)S(1)} %get-tuple-element.13.refs_0_), channel_id=1, source_target_pairs={{0,3},{1,2},{2,1},{3,0},{4,7},{5,6},{6,5},{7,4},{8,11},{9,10},{10,... | collective-permute-start | bytes 737288 | tf_op jit(solution)/shard_map/ppermute | solution.py:33
  40.0 9.2 %collective-permute-done.11.refs_3_ = bf16[480,256]{1,0:T(8,128)(2,1)S(1)} collective-permute-done((bf16[480,256]{1,0:T(8,128)(2,1)S(1)}, bf16[480,256]{1,0:T(8,128)(2,1)S(1)}, u32[]{:S(2)}, u32[]{:S(2)}) %collective-permute-start.11) | collective-permute-done | bytes 245792 | tf_op jit(solution)/shard_map/ppermute | solution.py:33
  51.4 2.4 %shard_map.121.refs_0_ = bf16[160,256]{1,0:T(8,128)(2,1)S(1)} custom-call(bf16[2,256,80]{2,1,0:T(8,128)(2,1)S(1)} %get-tuple-element.12.q_ref, bf16[480,256]{1,0:T(8,128)(2,1)S(1)} %get-tuple-element.13.refs_0_, bf16[480,256]{1,0:T(8,128)(2,1)S(1)} %collective-permute-done.9.refs_1_, bf16[480,256]{1,0:T(8,128)(2,1)S(1)} %collective-permute-done.10.refs_2_, ...), custom_call_target="tpu_custom_call" | custom-call | tf_op jit(solution)/shard_map/pallas_call | solution.py:379
  54.8 3.0 %collective-permute-start.21 = (bf16[160,256]{1,0:T(8,128)(2,1)S(1)}, bf16[160,256]{1,0:T(8,128)(2,1)S(1)}, u32[]{:S(2)}, u32[]{:S(2)}) collective-permute-start(bf16[160,256]{1,0:T(8,128)(2,1)S(1)} %shard_map.121.refs_0_), channel_id=1, source_target_pairs={{0,24},{4,28},{8,16},{12,20},{16,8},{20,12},{24,0},{28,4},{1,25},{... | collective-permute-start | bytes 245768 | tf_op jit(solution)/shard_map/ppermute | solution.py:33
  58.0 4.5 %shard_map.118 = (f32[128,512]{1,0:T(8,128)}, f32[128,128]{1,0:T(8,128)}) custom-call(bf16[128,8192]{1,0:T(8,128)(2,1)} %x_ref.3, f32[1,8192]{1,0:T(1,128)} %bitcast.12, bf16[8192,512]{1,0:T(8,128)(2,1)} %refs_3_.3, bf16[8192,512]{1,0:T(8,128)(2,1)} %refs_3_.3, bf16[8192,512]{1,0:T(8,128)(2,1)} %refs_3_.3, bf16[8192,512]{1,0:T(8,128)(2,1)} %refs_3_.3), custom_call_target="tpu_custom_call" | custom-call | tf_op jit(solution)/shard_map/pallas_call | solution.py:310
  62.5 4.9 %shard_map.119.query_ref = bf16[144,512]{1,0:T(8,128)(2,1)} custom-call(bf16[128,8192]{1,0:T(8,128)(2,1)} %x_ref.3, f32[1,8192]{1,0:T(1,128)} %bitcast.13, bf16[8192,512]{1,0:T(8,128)(2,1)} %refs_3_.3, bf16[8192,512]{1,0:T(8,128)(2,1)} %refs_3_.3, bf16[8192,512]{1,0:T(8,128)(2,1)} %refs_3_.3, bf16[8192,512]{1,0:T(8,128)(2,1)} %refs_3_.3, ...), custom_call_target="tpu_custom_call" | custom-call | tf_op jit(solution)/shard_map/pallas_call | solution.py:325
  67.4 5.0 %collective-permute-start.33 = (bf16[144,512]{1,0:T(8,128)(2,1)}, bf16[144,512]{1,0:T(8,128)(2,1)S(1)}, u32[]{:S(2)}, u32[]{:S(2)}) collective-permute-start(bf16[144,512]{1,0:T(8,128)(2,1)} %shard_map.119.query_ref), channel_id=1, source_target_pairs={{0,192},{64,128},{128,64},{192,0},{1,193},{65,129},{129,65},{193,1... | collective-permute-start | bytes 442376 | tf_op jit(solution)/shard_map/ppermute | solution.py:33
  73.6 2.6 %collective-permute-start.18 = (bf16[160,256]{1,0:T(8,128)(2,1)S(1)}, bf16[160,256]{1,0:T(8,128)(2,1)S(1)}, u32[]{:S(2)}, u32[]{:S(2)}) collective-permute-start(bf16[160,256]{1,0:T(8,128)(2,1)S(1)} %shard_map.121.refs_0_), channel_id=1, source_target_pairs={{0,12},{4,8},{8,4},{12,0},{16,28},{20,24},{24,20},{28,16},{1,13},{... | collective-permute-start | bytes 245768 | tf_op jit(solution)/shard_map/ppermute | solution.py:33
  82.4 2.8 %collective-permute-start.25 = (bf16[256,256]{1,0:T(8,128)(2,1)S(1)}, bf16[256,256]{1,0:T(8,128)(2,1)S(1)}, u32[]{:S(2)}, u32[]{:S(2)}) collective-permute-start(bf16[256,256]{1,0:T(8,128)(2,1)S(1)} %shard_map.123.refs_0_), channel_id=1, source_target_pairs={{0,3},{1,2},{2,1},{3,0},{4,7},{5,6},{6,5},{7,4},{8,11},{9,10},{10,... | collective-permute-start | bytes 393224 | tf_op jit(solution)/shard_map/ppermute | solution.py:33
  87.1 4.3 %collective-permute-start = (bf16[144,512]{1,0:T(8,128)(2,1)S(1)}, bf16[144,512]{1,0:T(8,128)(2,1)S(1)}, u32[]{:S(2)}, u32[]{:S(2)}) collective-permute-start(bf16[144,512]{1,0:T(8,128)(2,1)S(1)} %copy-done.3), channel_id=1, source_target_pairs={{0,128},{64,192},{128,0},{192,64},{1,129},{65,193},{129,1},{193,65... | collective-permute-start | bytes 442376 | tf_op jit(solution)/shard_map/ppermute | solution.py:33
  94.6 2.2 %shard_map.126 = bf16[128,512]{1,0:T(8,128)(2,1)S(1)} custom-call(s32[3]{0:T(128)S(1)} %pad_add_fusion.place_ref, bf16[144,512]{1,0:T(8,128)(2,1)S(1)} %collective-permute-done.33.query_ref, bf16[256,256]{1,0:T(8,128)(2,1)S(1)} %shard_map.123.refs_0_, bf16[256,256]{1,0:T(8,128)(2,1)S(1)} %collective-permute-done.23.refs_1_, ...), custom_call_target="tpu_custom_call" | custom-call | tf_op jit(solution)/shard_map/pallas_call | solution.py:406
  97.7 1.7 %collective-permute-done.31.query_ref = bf16[144,512]{1,0:T(8,128)(2,1)S(1)} collective-permute-done((bf16[144,512]{1,0:T(8,128)(2,1)S(1)}, bf16[144,512]{1,0:T(8,128)(2,1)S(1)}, u32[]{:S(2)}, u32[]{:S(2)}) %collective-permute-start.31) | collective-permute-done | bytes 147488 | tf_op jit(solution)/shard_map/ppermute | solution.py:33
  99.5 2.0 %shard_map.125 = bf16[128,512]{1,0:T(8,128)(2,1)S(1)} custom-call(s32[3]{0:T(128)S(1)} %pad_add_fusion.place_ref, bf16[144,512]{1,0:T(8,128)(2,1)S(1)} %collective-permute-done.31.query_ref, bf16[256,256]{1,0:T(8,128)(2,1)S(1)} %shard_map.123.refs_0_, bf16[256,256]{1,0:T(8,128)(2,1)S(1)} %collective-permute-done.23.refs_1_, ...), custom_call_target="tpu_custom_call" | custom-call | tf_op jit(solution)/shard_map/pallas_call | solution.py:406
  101.4 3.5 %collective-permute-start.32 = (bf16[128,512]{1,0:T(8,128)(2,1)S(1)}, bf16[128,512]{1,0:T(8,128)(2,1)S(1)}, u32[]{:S(2)}, u32[]{:S(2)}) collective-permute-start(bf16[128,512]{1,0:T(8,128)(2,1)S(1)} %shard_map.125), channel_id=1, source_target_pairs={{0,64},{64,0},{128,192},{192,128},{1,65},{65,1},{129,193},{193,129... | collective-permute-start | bytes 393224 | tf_op jit(solution)/shard_map/ppermute | solution.py:33
  104.9 2.0 %shard_map.124 = bf16[128,512]{1,0:T(8,128)(2,1)S(1)} custom-call(s32[3]{0:T(128)S(1)} %pad_add_fusion.place_ref, bf16[144,512]{1,0:T(8,128)(2,1)S(1)} %collective-permute-done.query_ref, bf16[256,256]{1,0:T(8,128)(2,1)S(1)} %shard_map.123.refs_0_, bf16[256,256]{1,0:T(8,128)(2,1)S(1)} %collective-permute-done.23.refs_1_, ...), custom_call_target="tpu_custom_call" | custom-call | tf_op jit(solution)/shard_map/pallas_call | solution.py:406
  106.9 4.7 %collective-permute-start.30 = (bf16[128,512]{1,0:T(8,128)(2,1)S(1)}, bf16[128,512]{1,0:T(8,128)(2,1)S(1)}, u32[]{:S(2)}, u32[]{:S(2)}) collective-permute-start(bf16[128,512]{1,0:T(8,128)(2,1)S(1)} %shard_map.124), channel_id=1, source_target_pairs={{0,128},{64,192},{128,0},{192,64},{1,129},{65,193},{129,1},{193,65... | collective-permute-start | bytes 393224 | tf_op jit(solution)/shard_map/ppermute | solution.py:33
  111.6 2.0 %shard_map.127 = bf16[128,512]{1,0:T(8,128)(2,1)S(1)} custom-call(s32[3]{0:T(128)S(1)} %pad_add_fusion.place_ref, bf16[144,512]{1,0:T(8,128)(2,1)S(1)} %copy-done.3, bf16[256,256]{1,0:T(8,128)(2,1)S(1)} %shard_map.123.refs_0_, bf16[256,256]{1,0:T(8,128)(2,1)S(1)} %collective-permute-done.23.refs_1_, bf16[256,256]{1,0:T(8,128)(2,1)S(1)} %collective-permute-done.24.refs_2_, ...), custom_call_target="tpu_custom_call" | custom-call | tf_op jit(solution)/shard_map/pallas_call | solution.py:406
  113.6 6.0 %collective-permute-done.30 = bf16[128,512]{1,0:T(8,128)(2,1)S(1)} collective-permute-done((bf16[128,512]{1,0:T(8,128)(2,1)S(1)}, bf16[128,512]{1,0:T(8,128)(2,1)S(1)}, u32[]{:S(2)}, u32[]{:S(2)}) %collective-permute-start.30) | collective-permute-done | bytes 131104 | tf_op jit(solution)/shard_map/ppermute | solution.py:33
  (71 shorter events, 30.6 us)
Async XLA Ops:
  6.7 14.1 %collective-permute-start.8 = (bf16[56,1280]{1,0:T(8,128)(2,1)S(1)}, bf16[56,1280]{1,0:T(8,128)(2,1)S(1)}, u32[]{:S(2)}, u32[]{:S(2)}) collective-permute-start(bf16[56,1280]{1,0:T(8,128)(2,1)S(1)} %fusion.1.refs_0_), channel_id=1, source_target_pairs={{0,28},{4,24},{8,20},{12,16},{16,12},{20,8},{24,4},{28,0},{1,29},{... | collective-permute-start | bytes 430088 | tf_op jit(solution)/shard_map/ppermute | solution.py:33
  14.8 11.5 %collective-permute-start.7 = (bf16[56,1280]{1,0:T(8,128)(2,1)S(1)}, bf16[56,1280]{1,0:T(8,128)(2,1)S(1)}, u32[]{:S(2)}, u32[]{:S(2)}) collective-permute-start(bf16[56,1280]{1,0:T(8,128)(2,1)S(1)} %fusion.1.refs_0_), channel_id=1, source_target_pairs={{0,24},{4,28},{8,16},{12,20},{16,8},{20,12},{24,0},{28,4},{1,25},{... | collective-permute-start | bytes 430088 | tf_op jit(solution)/shard_map/ppermute | solution.py:33
  15.8 13.3 %collective-permute-start.6 = (bf16[56,1280]{1,0:T(8,128)(2,1)S(1)}, bf16[56,1280]{1,0:T(8,128)(2,1)S(1)}, u32[]{:S(2)}, u32[]{:S(2)}) collective-permute-start(bf16[56,1280]{1,0:T(8,128)(2,1)S(1)} %fusion.1.refs_0_), channel_id=1, source_target_pairs={{0,20},{4,16},{8,28},{12,24},{16,4},{20,0},{24,12},{28,8},{1,21},{... | collective-permute-start | bytes 430088 | tf_op jit(solution)/shard_map/ppermute | solution.py:33
  17.0 12.5 %collective-permute-start.5 = (bf16[56,1280]{1,0:T(8,128)(2,1)S(1)}, bf16[56,1280]{1,0:T(8,128)(2,1)S(1)}, u32[]{:S(2)}, u32[]{:S(2)}) collective-permute-start(bf16[56,1280]{1,0:T(8,128)(2,1)S(1)} %fusion.1.refs_0_), channel_id=1, source_target_pairs={{0,16},{4,20},{8,24},{12,28},{16,0},{20,4},{24,8},{28,12},{1,17},{... | collective-permute-start | bytes 430088 | tf_op jit(solution)/shard_map/ppermute | solution.py:33
  20.2 9.3 %collective-permute-start.4 = (bf16[56,1280]{1,0:T(8,128)(2,1)S(1)}, bf16[56,1280]{1,0:T(8,128)(2,1)S(1)}, u32[]{:S(2)}, u32[]{:S(2)}) collective-permute-start(bf16[56,1280]{1,0:T(8,128)(2,1)S(1)} %fusion.1.refs_0_), channel_id=1, source_target_pairs={{0,12},{4,8},{8,4},{12,0},{16,28},{20,24},{24,20},{28,16},{1,13},{... | collective-permute-start | bytes 430088 | tf_op jit(solution)/shard_map/ppermute | solution.py:33
  20.7 10.4 %collective-permute-start.3 = (bf16[56,1280]{1,0:T(8,128)(2,1)S(1)}, bf16[56,1280]{1,0:T(8,128)(2,1)S(1)}, u32[]{:S(2)}, u32[]{:S(2)}) collective-permute-start(bf16[56,1280]{1,0:T(8,128)(2,1)S(1)} %fusion.1.refs_0_), channel_id=1, source_target_pairs={{0,8},{4,12},{8,0},{12,4},{16,24},{20,28},{24,16},{28,20},{1,9},{5... | collective-permute-start | bytes 430088 | tf_op jit(solution)/shard_map/ppermute | solution.py:33
  35.8 13.3 %collective-permute-start.11 = (bf16[480,256]{1,0:T(8,128)(2,1)S(1)}, bf16[480,256]{1,0:T(8,128)(2,1)S(1)}, u32[]{:S(2)}, u32[]{:S(2)}) collective-permute-start(bf16[480,256]{1,0:T(8,128)(2,1)S(1)} %get-tuple-element.13.refs_0_), channel_id=1, source_target_pairs={{0,3},{1,2},{2,1},{3,0},{4,7},{5,6},{6,5},{7,4},{8,11},{9,10},{10,... | collective-permute-start | bytes 737288 | tf_op jit(solution)/shard_map/ppermute | solution.py:33
  38.7 10.5 %collective-permute-start.10 = (bf16[480,256]{1,0:T(8,128)(2,1)S(1)}, bf16[480,256]{1,0:T(8,128)(2,1)S(1)}, u32[]{:S(2)}, u32[]{:S(2)}) collective-permute-start(bf16[480,256]{1,0:T(8,128)(2,1)S(1)} %get-tuple-element.13.refs_0_), channel_id=1, source_target_pairs={{0,2},{1,3},{2,0},{3,1},{4,6},{5,7},{6,4},{7,5},{8,10},{9,11},{10,... | collective-permute-start | bytes 737288 | tf_op jit(solution)/shard_map/ppermute | solution.py:33
  39.5 10.3 %collective-permute-start.9 = (bf16[480,256]{1,0:T(8,128)(2,1)S(1)}, bf16[480,256]{1,0:T(8,128)(2,1)S(1)}, u32[]{:S(2)}, u32[]{:S(2)}) collective-permute-start(bf16[480,256]{1,0:T(8,128)(2,1)S(1)} %get-tuple-element.13.refs_0_), channel_id=1, source_target_pairs={{0,1},{1,0},{2,3},{3,2},{4,5},{5,4},{6,7},{7,6},{8,9},{9,8},{10,11... | collective-permute-start | bytes 737288 | tf_op jit(solution)/shard_map/ppermute | solution.py:33
  40.0 9.8 %collective-permute-start.12 = (bf16[480,256]{1,0:T(8,128)(2,1)S(1)}, bf16[480,256]{1,0:T(8,128)(2,1)S(1)}, u32[]{:S(2)}, u32[]{:S(2)}) collective-permute-start(bf16[480,256]{1,0:T(8,128)(2,1)S(1)} %get-tuple-element.13.refs_0_), channel_id=1, source_target_pairs={{0,32},{32,0},{1,33},{33,1},{2,34},{34,2},{3,35},{35,3},{4,36},{36... | collective-permute-start | bytes 737288 | tf_op jit(solution)/shard_map/ppermute | solution.py:33
  53.8 19.8 %collective-permute-start.22 = (bf16[160,256]{1,0:T(8,128)(2,1)S(1)}, bf16[160,256]{1,0:T(8,128)(2,1)S(1)}, u32[]{:S(2)}, u32[]{:S(2)}) collective-permute-start(bf16[160,256]{1,0:T(8,128)(2,1)S(1)} %shard_map.121.refs_0_), channel_id=1, source_target_pairs={{0,28},{4,24},{8,20},{12,16},{16,12},{20,8},{24,4},{28,0},{1,29},{... | collective-permute-start | bytes 245768 | tf_op jit(solution)/shard_map/ppermute | solution.py:33
  54.8 21.4 %collective-permute-start.21 = (bf16[160,256]{1,0:T(8,128)(2,1)S(1)}, bf16[160,256]{1,0:T(8,128)(2,1)S(1)}, u32[]{:S(2)}, u32[]{:S(2)}) collective-permute-start(bf16[160,256]{1,0:T(8,128)(2,1)S(1)} %shard_map.121.refs_0_), channel_id=1, source_target_pairs={{0,24},{4,28},{8,16},{12,20},{16,8},{20,12},{24,0},{28,4},{1,25},{... | collective-permute-start | bytes 245768 | tf_op jit(solution)/shard_map/ppermute | solution.py:33
  57.8 19.0 %collective-permute-start.20 = (bf16[160,256]{1,0:T(8,128)(2,1)S(1)}, bf16[160,256]{1,0:T(8,128)(2,1)S(1)}, u32[]{:S(2)}, u32[]{:S(2)}) collective-permute-start(bf16[160,256]{1,0:T(8,128)(2,1)S(1)} %shard_map.121.refs_0_), channel_id=1, source_target_pairs={{0,20},{4,16},{8,28},{12,24},{16,4},{20,0},{24,12},{28,8},{1,21},{... | collective-permute-start | bytes 245768 | tf_op jit(solution)/shard_map/ppermute | solution.py:33
  67.4 19.2 %collective-permute-start.33 = (bf16[144,512]{1,0:T(8,128)(2,1)}, bf16[144,512]{1,0:T(8,128)(2,1)S(1)}, u32[]{:S(2)}, u32[]{:S(2)}) collective-permute-start(bf16[144,512]{1,0:T(8,128)(2,1)} %shard_map.119.query_ref), channel_id=1, source_target_pairs={{0,192},{64,128},{128,64},{192,0},{1,193},{65,129},{129,65},{193,1... | collective-permute-start | bytes 442376 | tf_op jit(solution)/shard_map/ppermute | solution.py:33
  72.4 7.5 %collective-permute-start.19 = (bf16[160,256]{1,0:T(8,128)(2,1)S(1)}, bf16[160,256]{1,0:T(8,128)(2,1)S(1)}, u32[]{:S(2)}, u32[]{:S(2)}) collective-permute-start(bf16[160,256]{1,0:T(8,128)(2,1)S(1)} %shard_map.121.refs_0_), channel_id=1, source_target_pairs={{0,16},{4,20},{8,24},{12,28},{16,0},{20,4},{24,8},{28,12},{1,17},{... | collective-permute-start | bytes 245768 | tf_op jit(solution)/shard_map/ppermute | solution.py:33
  73.6 6.9 %collective-permute-start.18 = (bf16[160,256]{1,0:T(8,128)(2,1)S(1)}, bf16[160,256]{1,0:T(8,128)(2,1)S(1)}, u32[]{:S(2)}, u32[]{:S(2)}) collective-permute-start(bf16[160,256]{1,0:T(8,128)(2,1)S(1)} %shard_map.121.refs_0_), channel_id=1, source_target_pairs={{0,12},{4,8},{8,4},{12,0},{16,28},{20,24},{24,20},{28,16},{1,13},{... | collective-permute-start | bytes 245768 | tf_op jit(solution)/shard_map/ppermute | solution.py:33
  82.4 9.1 %collective-permute-start.25 = (bf16[256,256]{1,0:T(8,128)(2,1)S(1)}, bf16[256,256]{1,0:T(8,128)(2,1)S(1)}, u32[]{:S(2)}, u32[]{:S(2)}) collective-permute-start(bf16[256,256]{1,0:T(8,128)(2,1)S(1)} %shard_map.123.refs_0_), channel_id=1, source_target_pairs={{0,3},{1,2},{2,1},{3,0},{4,7},{5,6},{6,5},{7,4},{8,11},{9,10},{10,... | collective-permute-start | bytes 393224 | tf_op jit(solution)/shard_map/ppermute | solution.py:33
  85.2 7.9 %collective-permute-start.24 = (bf16[256,256]{1,0:T(8,128)(2,1)S(1)}, bf16[256,256]{1,0:T(8,128)(2,1)S(1)}, u32[]{:S(2)}, u32[]{:S(2)}) collective-permute-start(bf16[256,256]{1,0:T(8,128)(2,1)S(1)} %shard_map.123.refs_0_), channel_id=1, source_target_pairs={{0,2},{1,3},{2,0},{3,1},{4,6},{5,7},{6,4},{7,5},{8,10},{9,11},{10,... | collective-permute-start | bytes 393224 | tf_op jit(solution)/shard_map/ppermute | solution.py:33
  85.9 7.2 %collective-permute-start.23 = (bf16[256,256]{1,0:T(8,128)(2,1)S(1)}, bf16[256,256]{1,0:T(8,128)(2,1)S(1)}, u32[]{:S(2)}, u32[]{:S(2)}) collective-permute-start(bf16[256,256]{1,0:T(8,128)(2,1)S(1)} %shard_map.123.refs_0_), channel_id=1, source_target_pairs={{0,1},{1,0},{2,3},{3,2},{4,5},{5,4},{6,7},{7,6},{8,9},{9,8},{10,11... | collective-permute-start | bytes 393224 | tf_op jit(solution)/shard_map/ppermute | solution.py:33
  86.6 12.9 %collective-permute-start.31 = (bf16[144,512]{1,0:T(8,128)(2,1)S(1)}, bf16[144,512]{1,0:T(8,128)(2,1)S(1)}, u32[]{:S(2)}, u32[]{:S(2)}) collective-permute-start(bf16[144,512]{1,0:T(8,128)(2,1)S(1)} %copy-done.3), channel_id=1, source_target_pairs={{0,64},{64,0},{128,192},{192,128},{1,65},{65,1},{129,193},{193,129... | collective-permute-start | bytes 442376 | tf_op jit(solution)/shard_map/ppermute | solution.py:33
  87.1 17.8 %collective-permute-start = (bf16[144,512]{1,0:T(8,128)(2,1)S(1)}, bf16[144,512]{1,0:T(8,128)(2,1)S(1)}, u32[]{:S(2)}, u32[]{:S(2)}) collective-permute-start(bf16[144,512]{1,0:T(8,128)(2,1)S(1)} %copy-done.3), channel_id=1, source_target_pairs={{0,128},{64,192},{128,0},{192,64},{1,129},{65,193},{129,1},{193,65... | collective-permute-start | bytes 442376 | tf_op jit(solution)/shard_map/ppermute | solution.py:33
  96.8 16.7 %collective-permute-start.34 = (bf16[128,512]{1,0:T(8,128)(2,1)S(1)}, bf16[128,512]{1,0:T(8,128)(2,1)S(1)}, u32[]{:S(2)}, u32[]{:S(2)}) collective-permute-start(bf16[128,512]{1,0:T(8,128)(2,1)S(1)} %shard_map.126), channel_id=1, source_target_pairs={{0,192},{64,128},{128,64},{192,0},{1,193},{65,129},{129,65},{193,1... | collective-permute-start | bytes 393224 | tf_op jit(solution)/shard_map/ppermute | solution.py:33
  101.4 12.2 %collective-permute-start.32 = (bf16[128,512]{1,0:T(8,128)(2,1)S(1)}, bf16[128,512]{1,0:T(8,128)(2,1)S(1)}, u32[]{:S(2)}, u32[]{:S(2)}) collective-permute-start(bf16[128,512]{1,0:T(8,128)(2,1)S(1)} %shard_map.125), channel_id=1, source_target_pairs={{0,64},{64,0},{128,192},{192,128},{1,65},{65,1},{129,193},{193,129... | collective-permute-start | bytes 393224 | tf_op jit(solution)/shard_map/ppermute | solution.py:33
  106.9 12.7 %collective-permute-start.30 = (bf16[128,512]{1,0:T(8,128)(2,1)S(1)}, bf16[128,512]{1,0:T(8,128)(2,1)S(1)}, u32[]{:S(2)}, u32[]{:S(2)}) collective-permute-start(bf16[128,512]{1,0:T(8,128)(2,1)S(1)} %shard_map.124), channel_id=1, source_target_pairs={{0,128},{64,192},{128,0},{192,64},{1,129},{65,193},{129,1},{193,65... | collective-permute-start | bytes 393224 | tf_op jit(solution)/shard_map/ppermute | solution.py:33
  (16 other events, 66.8 us)

commit v7 on v6

--- a/solution.py
+++ b/solution.py
@@ -45,7 +45,7 @@
 
 def qkv_kernel(me_ref, *refs):
     pieces, refs = refs[:TENSOR], refs[TENSOR:]
-    gain_ref, weight_ref, cross_ref, q_ref, kv_ref, base_ref, normed, raw, out_rows = refs
+    gain_ref, weight_ref, cross_ref, kv_ref, normed, raw, out_rows = refs
     me = me_ref[0]
     rows = raw.shape[0] // TENSOR
     for step in range(TENSOR):
@@ -67,17 +67,19 @@
     for part in range(2):
         out = lax.dot_general(weight_ref[1 + part], x, NT, preferred_element_type=F32)
         kv_ref[part * width : (part + 1) * width, :] = out.astype(BF16)
-    q = lax.dot_general(x, weight_ref[0], NT, preferred_element_type=F32)
-    for head in range(2):
-        q_ref[head] = q[:, head * EHD : (head + 1) * EHD].astype(BF16)
-    cross = cross_ref[...]
-    fold = jnp.dot(out_rows[...], cross, preferred_element_type=F32)
+    fold = jnp.dot(out_rows[...], cross_ref[...], preferred_element_type=F32)
     row = lax.broadcasted_iota(jnp.int32, (TENSOR * SHARE, TENSOR * SLOT), 0)
     column = lax.broadcasted_iota(jnp.int32, (TENSOR * SHARE, TENSOR * SLOT), 1)
     chosen = (column == row + ((row * 3277) >> 16) * (SLOT - SHARE)).astype(F32).astype(BF16)
     fold = jnp.dot(chosen, fold.astype(BF16), preferred_element_type=F32)
     kv_ref[4 * EHD :, :] = fold.astype(BF16)
-    base_ref[...] = jnp.dot(raw[...], cross, preferred_element_type=F32)
+
+
+def local_kernel(normed_ref, raw_ref, weight_ref, cross_ref, q_ref, base_ref):
+    q = lax.dot_general(normed_ref[...], weight_ref[0], NT, preferred_element_type=F32)
+    for head in range(2):
+        q_ref[head] = q[:, head * EHD : (head + 1) * EHD].astype(BF16)
+    base_ref[...] = jnp.dot(raw_ref[...], cross_ref[...], preferred_element_type=F32)
 
 
 def encoder_kernel(q_ref, *refs):
@@ -355,23 +357,31 @@
     share = jnp.pad(share, ((0, 24 - SHARE), (0, 0)))
     gain_row = enc_gain.reshape(1, -1)
     pieces = gather_tensor(jnp.concatenate([own, share], axis=0))
-    q, kv, base = pl.pallas_call(
+    qkv_weight = enc_qkv.transpose(0, 2, 1)
+    row_shape = jax.ShapeDtypeStruct((rows, width), BF16)
+    kv, normed, raw = pl.pallas_call(
         qkv_kernel,
         out_shape=(
-            jax.ShapeDtypeStruct((2, rows, EHD), BF16),
             jax.ShapeDtypeStruct((4 * EHD + TENSOR * SHARE, rows), BF16),
-            jax.ShapeDtypeStruct((rows, 2 * HD), F32),
+            row_shape,
+            row_shape,
         ),
         in_specs=[smem()] + vmem(TENSOR + 3),
         out_specs=tuple(vmem(3)),
-        scratch_shapes=[
-            pltpu.VMEM((rows, width), BF16),
-            pltpu.VMEM((rows, width), BF16),
-            pltpu.VMEM((TENSOR * SLOT, width), BF16),
-        ],
+        scratch_shapes=[pltpu.VMEM((TENSOR * SLOT, width), BF16)],
         compiler_params=limits(16),
-    )(me, *pieces, gain_row, enc_qkv.transpose(0, 2, 1), cross_kv)
+    )(me, *pieces, gain_row, qkv_weight, cross_kv)
     kv_pieces = gather_xc(kv)
+    q, base = pl.pallas_call(
+        local_kernel,
+        out_shape=(
+            jax.ShapeDtypeStruct((2, rows, EHD), BF16),
+            jax.ShapeDtypeStruct((rows, 2 * HD), F32),
+        ),
+        in_specs=vmem(4),
+        out_specs=tuple(vmem(2)),
+        compiler_params=limits(12),
+    )(normed, raw, qkv_weight, cross_kv)
     every_query = [message]
     for k in range(1, ZH):
         every_query.append(xor_permute(message, "zh", ZH, k))

time: 121 us -> 119 us (0.983)
  the two profiles are of different devices: /device:TPU:32 before, /device:TPU:1 now
where the time goes in v7:
time: 119 us; the launch traced here: 118 us
  starting transfers between devices  56.4 us (47%)
  waiting for transfers between devices  33.6 us (28%)
  Pallas kernels  24 us (20%)
  local copies, waits for them, and re-layouts  3.11 us (3%)
    ppermute x34, starting transfers between devices, xor_permute(): return lax.ppermute(values, axes, [(i, i ^ step) for i in range(size)])  54.8 us
    ppermute x34, waiting for transfers between devices, xor_permute(): return lax.ppermute(values, axes, [(i, i ^ step) for i in range(size)])  33.6 us
    pallas_call x4, Pallas kernels, on_device(): pl.pallas_call(decode_kernel, out_shape=jax.ShapeDtypeStruct((dec_rows, 4...  8.13 us
    pallas_call x1, Pallas kernels, on_device(): pl.pallas_call(functools.partial(query_last_kernel, dec_width), grid=(las...  4.91 us
    pallas_call x1, Pallas kernels, on_device(): pl.pallas_call(query_first_kernel, grid=(first_steps,), out_shape=(jax.Sh...  4.44 us
    unnamed x10, local copies, waits for them, and re-layouts  2.39 us
  transfers between devices with their start and end apart: 35, of which 12 were waited for; matrix products, arithmetic and copies ran while one was open for 1% of the time, Pallas kernels for 17%

profile of v7, /device:TPU:1, one launch (start us, length us, event | category | flops | bytes accessed | tf_op | source)
XLA Modules:
  0.0 118.1 jit_solution(17365467340498656690)
XLA Ops:
  1.7 13.4 %collective-permute-start.8 = (bf16[56,1280]{1,0:T(8,128)(2,1)S(1)}, bf16[56,1280]{1,0:T(8,128)(2,1)S(1)}, u32[]{:S(2)}, u32[]{:S(2)}) collective-permute-start(bf16[56,1280]{1,0:T(8,128)(2,1)S(1)} %fusion.1.refs_0_), channel_id=1, source_target_pairs={{0,28},{4,24},{8,20},{12,16},{16,12},{20,8},{24,4},{28,0},{1,29},{... | collective-permute-start | bytes 430088 | tf_op jit(solution)/shard_map/ppermute | solution.py:33
  16.1 2.9 %collective-permute-start.5 = (bf16[56,1280]{1,0:T(8,128)(2,1)S(1)}, bf16[56,1280]{1,0:T(8,128)(2,1)S(1)}, u32[]{:S(2)}, u32[]{:S(2)}) collective-permute-start(bf16[56,1280]{1,0:T(8,128)(2,1)S(1)} %fusion.1.refs_0_), channel_id=1, source_target_pairs={{0,16},{4,20},{8,24},{12,28},{16,0},{20,4},{24,8},{28,12},{1,17},{... | collective-permute-start | bytes 430088 | tf_op jit(solution)/shard_map/ppermute | solution.py:33
  20.6 8.2 %collective-permute-done.7.refs_6_ = bf16[56,1280]{1,0:T(8,128)(2,1)S(1)} collective-permute-done((bf16[56,1280]{1,0:T(8,128)(2,1)S(1)}, bf16[56,1280]{1,0:T(8,128)(2,1)S(1)}, u32[]{:S(2)}, u32[]{:S(2)}) %collective-permute-start.7) | collective-permute-done | bytes 143392 | tf_op jit(solution)/shard_map/ppermute | solution.py:33
  29.6 3.4 %collective-permute-done.3.refs_2_ = bf16[56,1280]{1,0:T(8,128)(2,1)S(1)} collective-permute-done((bf16[56,1280]{1,0:T(8,128)(2,1)S(1)}, bf16[56,1280]{1,0:T(8,128)(2,1)S(1)}, u32[]{:S(2)}, u32[]{:S(2)}) %collective-permute-start.3) | collective-permute-done | bytes 143392 | tf_op jit(solution)/shard_map/ppermute | solution.py:33
  36.8 2.6 %collective-permute-start.11 = (bf16[480,256]{1,0:T(8,128)(2,1)S(1)}, bf16[480,256]{1,0:T(8,128)(2,1)S(1)}, u32[]{:S(2)}, u32[]{:S(2)}) collective-permute-start(bf16[480,256]{1,0:T(8,128)(2,1)S(1)} %get-tuple-element.17.refs_0_), channel_id=1, source_target_pairs={{0,3},{1,2},{2,1},{3,0},{4,7},{5,6},{6,5},{7,4},{8,11},{9,10},{10,... | collective-permute-start | bytes 737288 | tf_op jit(solution)/shard_map/ppermute | solution.py:33
  40.2 2.7 %collective-permute-start.12 = (bf16[480,256]{1,0:T(8,128)(2,1)S(1)}, bf16[480,256]{1,0:T(8,128)(2,1)S(1)}, u32[]{:S(2)}, u32[]{:S(2)}) collective-permute-start(bf16[480,256]{1,0:T(8,128)(2,1)S(1)} %get-tuple-element.17.refs_0_), channel_id=1, source_target_pairs={{0,32},{32,0},{1,33},{33,1},{2,34},{34,2},{3,35},{35,3},{4,36},{36... | collective-permute-start | bytes 737288 | tf_op jit(solution)/shard_map/ppermute | solution.py:33
  42.9 6.9 %collective-permute-done.11.refs_3_ = bf16[480,256]{1,0:T(8,128)(2,1)S(1)} collective-permute-done((bf16[480,256]{1,0:T(8,128)(2,1)S(1)}, bf16[480,256]{1,0:T(8,128)(2,1)S(1)}, u32[]{:S(2)}, u32[]{:S(2)}) %collective-permute-start.11) | collective-permute-done | bytes 245792 | tf_op jit(solution)/shard_map/ppermute | solution.py:33
  53.5 2.4 %shard_map.122.refs_0_ = bf16[160,256]{1,0:T(8,128)(2,1)S(1)} custom-call(bf16[2,256,80]{2,1,0:T(8,128)(2,1)S(1)} %get-tuple-element.16.q_ref, bf16[480,256]{1,0:T(8,128)(2,1)S(1)} %get-tuple-element.17.refs_0_, bf16[480,256]{1,0:T(8,128)(2,1)S(1)} %collective-permute-done.9.refs_1_, bf16[480,256]{1,0:T(8,128)(2,1)S(1)} %collective-permute-done.10.refs_2_, ...), custom_call_target="tpu_custom_call" | custom-call | tf_op jit(solution)/shard_map/pallas_call | solution.py:389
  56.0 2.9 %collective-permute-start.21 = (bf16[160,256]{1,0:T(8,128)(2,1)S(1)}, bf16[160,256]{1,0:T(8,128)(2,1)S(1)}, u32[]{:S(2)}, u32[]{:S(2)}) collective-permute-start(bf16[160,256]{1,0:T(8,128)(2,1)S(1)} %shard_map.122.refs_0_), channel_id=1, source_target_pairs={{0,24},{4,28},{8,16},{12,20},{16,8},{20,12},{24,0},{28,4},{1,25},{... | collective-permute-start | bytes 245768 | tf_op jit(solution)/shard_map/ppermute | solution.py:33
  60.1 4.4 %shard_map.118 = (f32[128,512]{1,0:T(8,128)}, f32[128,128]{1,0:T(8,128)}) custom-call(bf16[128,8192]{1,0:T(8,128)(2,1)} %x_ref.3, f32[1,8192]{1,0:T(1,128)} %bitcast.13, bf16[8192,512]{1,0:T(8,128)(2,1)} %refs_3_.3, bf16[8192,512]{1,0:T(8,128)(2,1)} %refs_3_.3, bf16[8192,512]{1,0:T(8,128)(2,1)} %refs_3_.3, bf16[8192,512]{1,0:T(8,128)(2,1)} %refs_3_.3), custom_call_target="tpu_custom_call" | custom-call | tf_op jit(solution)/shard_map/pallas_call | solution.py:312
  64.6 4.9 %shard_map.119.query_ref = bf16[144,512]{1,0:T(8,128)(2,1)} custom-call(bf16[128,8192]{1,0:T(8,128)(2,1)} %x_ref.3, f32[1,8192]{1,0:T(1,128)} %bitcast.14, bf16[8192,512]{1,0:T(8,128)(2,1)} %refs_3_.3, bf16[8192,512]{1,0:T(8,128)(2,1)} %refs_3_.3, bf16[8192,512]{1,0:T(8,128)(2,1)} %refs_3_.3, bf16[8192,512]{1,0:T(8,128)(2,1)} %refs_3_.3, ...), custom_call_target="tpu_custom_call" | custom-call | tf_op jit(solution)/shard_map/pallas_call | solution.py:327
  69.5 4.7 %collective-permute-start = (bf16[144,512]{1,0:T(8,128)(2,1)}, bf16[144,512]{1,0:T(8,128)(2,1)S(1)}, u32[]{:S(2)}, u32[]{:S(2)}) collective-permute-start(bf16[144,512]{1,0:T(8,128)(2,1)} %shard_map.119.query_ref), channel_id=1, source_target_pairs={{0,128},{64,192},{128,0},{192,64},{1,129},{65,193},{129,1},{193,65... | collective-permute-start | bytes 442376 | tf_op jit(solution)/shard_map/ppermute | solution.py:33
  75.0 2.4 %collective-permute-start.18 = (bf16[160,256]{1,0:T(8,128)(2,1)S(1)}, bf16[160,256]{1,0:T(8,128)(2,1)S(1)}, u32[]{:S(2)}, u32[]{:S(2)}) collective-permute-start(bf16[160,256]{1,0:T(8,128)(2,1)S(1)} %shard_map.122.refs_0_), channel_id=1, source_target_pairs={{0,12},{4,8},{8,4},{12,0},{16,28},{20,24},{24,20},{28,16},{1,13},{... | collective-permute-start | bytes 245768 | tf_op jit(solution)/shard_map/ppermute | solution.py:33
  79.6 3.5 %collective-permute-done.18.refs_3_ = bf16[160,256]{1,0:T(8,128)(2,1)S(1)} collective-permute-done((bf16[160,256]{1,0:T(8,128)(2,1)S(1)}, bf16[160,256]{1,0:T(8,128)(2,1)S(1)}, u32[]{:S(2)}, u32[]{:S(2)}) %collective-permute-start.18) | collective-permute-done | bytes 81952 | tf_op jit(solution)/shard_map/ppermute | solution.py:33
  83.1 1.9 %collective-permute-done.16.refs_1_ = bf16[160,256]{1,0:T(8,128)(2,1)S(1)} collective-permute-done((bf16[160,256]{1,0:T(8,128)(2,1)S(1)}, bf16[160,256]{1,0:T(8,128)(2,1)S(1)}, u32[]{:S(2)}, u32[]{:S(2)}) %collective-permute-start.16) | collective-permute-done | bytes 81952 | tf_op jit(solution)/shard_map/ppermute | solution.py:33
  87.4 2.5 %collective-permute-start.25 = (bf16[256,256]{1,0:T(8,128)(2,1)S(1)}, bf16[256,256]{1,0:T(8,128)(2,1)S(1)}, u32[]{:S(2)}, u32[]{:S(2)}) collective-permute-start(bf16[256,256]{1,0:T(8,128)(2,1)S(1)} %shard_map.124.refs_0_), channel_id=1, source_target_pairs={{0,3},{1,2},{2,1},{3,0},{4,7},{5,6},{6,5},{7,4},{8,11},{9,10},{10,... | collective-permute-start | bytes 393224 | tf_op jit(solution)/shard_map/ppermute | solution.py:33
  91.6 3.8 %collective-permute-done.25.refs_3_ = bf16[256,256]{1,0:T(8,128)(2,1)S(1)} collective-permute-done((bf16[256,256]{1,0:T(8,128)(2,1)S(1)}, bf16[256,256]{1,0:T(8,128)(2,1)S(1)}, u32[]{:S(2)}, u32[]{:S(2)}) %collective-permute-start.25) | collective-permute-done | bytes 131104 | tf_op jit(solution)/shard_map/ppermute | solution.py:33
  99.5 2.2 %shard_map.125 = bf16[128,512]{1,0:T(8,128)(2,1)S(1)} custom-call(s32[3]{0:T(128)S(1)} %pad_add_fusion.place_ref, bf16[144,512]{1,0:T(8,128)(2,1)S(1)} %collective-permute-done.query_ref, bf16[256,256]{1,0:T(8,128)(2,1)S(1)} %shard_map.124.refs_0_, bf16[256,256]{1,0:T(8,128)(2,1)S(1)} %collective-permute-done.23.refs_1_, ...), custom_call_target="tpu_custom_call" | custom-call | tf_op jit(solution)/shard_map/pallas_call | solution.py:416
  101.8 2.0 %shard_map.126 = bf16[128,512]{1,0:T(8,128)(2,1)S(1)} custom-call(s32[3]{0:T(128)S(1)} %pad_add_fusion.place_ref, bf16[144,512]{1,0:T(8,128)(2,1)S(1)} %collective-permute-done.31.query_ref, bf16[256,256]{1,0:T(8,128)(2,1)S(1)} %shard_map.124.refs_0_, bf16[256,256]{1,0:T(8,128)(2,1)S(1)} %collective-permute-done.23.refs_1_, ...), custom_call_target="tpu_custom_call" | custom-call | tf_op jit(solution)/shard_map/pallas_call | solution.py:416
  103.8 2.9 %collective-permute-start.32 = (bf16[128,512]{1,0:T(8,128)(2,1)S(1)}, bf16[128,512]{1,0:T(8,128)(2,1)S(1)}, u32[]{:S(2)}, u32[]{:S(2)}) collective-permute-start(bf16[128,512]{1,0:T(8,128)(2,1)S(1)} %shard_map.126), channel_id=1, source_target_pairs={{0,64},{64,0},{128,192},{192,128},{1,65},{65,1},{129,193},{193,129... | collective-permute-start | bytes 393224 | tf_op jit(solution)/shard_map/ppermute | solution.py:33
  106.7 2.0 %shard_map.127 = bf16[128,512]{1,0:T(8,128)(2,1)S(1)} custom-call(s32[3]{0:T(128)S(1)} %pad_add_fusion.place_ref, bf16[144,512]{1,0:T(8,128)(2,1)S(1)} %collective-permute-done.33.query_ref, bf16[256,256]{1,0:T(8,128)(2,1)S(1)} %shard_map.124.refs_0_, bf16[256,256]{1,0:T(8,128)(2,1)S(1)} %collective-permute-done.23.refs_1_, ...), custom_call_target="tpu_custom_call" | custom-call | tf_op jit(solution)/shard_map/pallas_call | solution.py:416
  108.7 2.9 %collective-permute-start.34 = (bf16[128,512]{1,0:T(8,128)(2,1)S(1)}, bf16[128,512]{1,0:T(8,128)(2,1)S(1)}, u32[]{:S(2)}, u32[]{:S(2)}) collective-permute-start(bf16[128,512]{1,0:T(8,128)(2,1)S(1)} %shard_map.127), channel_id=1, source_target_pairs={{0,192},{64,128},{128,64},{192,0},{1,193},{65,129},{129,65},{193,1... | collective-permute-start | bytes 393224 | tf_op jit(solution)/shard_map/ppermute | solution.py:33
  111.6 2.0 %shard_map.128 = bf16[128,512]{1,0:T(8,128)(2,1)S(1)} custom-call(s32[3]{0:T(128)S(1)} %pad_add_fusion.place_ref, bf16[144,512]{1,0:T(8,128)(2,1)S(1)} %copy-done.3, bf16[256,256]{1,0:T(8,128)(2,1)S(1)} %shard_map.124.refs_0_, bf16[256,256]{1,0:T(8,128)(2,1)S(1)} %collective-permute-done.23.refs_1_, bf16[256,256]{1,0:T(8,128)(2,1)S(1)} %collective-permute-done.24.refs_2_, ...), custom_call_target="tpu_custom_call" | custom-call | tf_op jit(solution)/shard_map/pallas_call | solution.py:416
  113.6 3.8 %collective-permute-done.32 = bf16[128,512]{1,0:T(8,128)(2,1)S(1)} collective-permute-done((bf16[128,512]{1,0:T(8,128)(2,1)S(1)}, bf16[128,512]{1,0:T(8,128)(2,1)S(1)}, u32[]{:S(2)}, u32[]{:S(2)}) %collective-permute-start.32) | collective-permute-done | bytes 131104 | tf_op jit(solution)/shard_map/ppermute | solution.py:33
  (72 shorter events, 26.7 us)
Async XLA Ops:
  1.7 17.6 %collective-permute-start.8 = (bf16[56,1280]{1,0:T(8,128)(2,1)S(1)}, bf16[56,1280]{1,0:T(8,128)(2,1)S(1)}, u32[]{:S(2)}, u32[]{:S(2)}) collective-permute-start(bf16[56,1280]{1,0:T(8,128)(2,1)S(1)} %fusion.1.refs_0_), channel_id=1, source_target_pairs={{0,28},{4,24},{8,20},{12,16},{16,12},{20,8},{24,4},{28,0},{1,29},{... | collective-permute-start | bytes 430088 | tf_op jit(solution)/shard_map/ppermute | solution.py:33
  15.1 13.6 %collective-permute-start.7 = (bf16[56,1280]{1,0:T(8,128)(2,1)S(1)}, bf16[56,1280]{1,0:T(8,128)(2,1)S(1)}, u32[]{:S(2)}, u32[]{:S(2)}) collective-permute-start(bf16[56,1280]{1,0:T(8,128)(2,1)S(1)} %fusion.1.refs_0_), channel_id=1, source_target_pairs={{0,24},{4,28},{8,16},{12,20},{16,8},{20,12},{24,0},{28,4},{1,25},{... | collective-permute-start | bytes 430088 | tf_op jit(solution)/shard_map/ppermute | solution.py:33
  15.2 14.3 %collective-permute-start.6 = (bf16[56,1280]{1,0:T(8,128)(2,1)S(1)}, bf16[56,1280]{1,0:T(8,128)(2,1)S(1)}, u32[]{:S(2)}, u32[]{:S(2)}) collective-permute-start(bf16[56,1280]{1,0:T(8,128)(2,1)S(1)} %fusion.1.refs_0_), channel_id=1, source_target_pairs={{0,20},{4,16},{8,28},{12,24},{16,4},{20,0},{24,12},{28,8},{1,21},{... | collective-permute-start | bytes 430088 | tf_op jit(solution)/shard_map/ppermute | solution.py:33
  16.1 13.5 %collective-permute-start.5 = (bf16[56,1280]{1,0:T(8,128)(2,1)S(1)}, bf16[56,1280]{1,0:T(8,128)(2,1)S(1)}, u32[]{:S(2)}, u32[]{:S(2)}) collective-permute-start(bf16[56,1280]{1,0:T(8,128)(2,1)S(1)} %fusion.1.refs_0_), channel_id=1, source_target_pairs={{0,16},{4,20},{8,24},{12,28},{16,0},{20,4},{24,8},{28,12},{1,17},{... | collective-permute-start | bytes 430088 | tf_op jit(solution)/shard_map/ppermute | solution.py:33
  19.0 10.5 %collective-permute-start.4 = (bf16[56,1280]{1,0:T(8,128)(2,1)S(1)}, bf16[56,1280]{1,0:T(8,128)(2,1)S(1)}, u32[]{:S(2)}, u32[]{:S(2)}) collective-permute-start(bf16[56,1280]{1,0:T(8,128)(2,1)S(1)} %fusion.1.refs_0_), channel_id=1, source_target_pairs={{0,12},{4,8},{8,4},{12,0},{16,28},{20,24},{24,20},{28,16},{1,13},{... | collective-permute-start | bytes 430088 | tf_op jit(solution)/shard_map/ppermute | solution.py:33
  19.3 13.6 %collective-permute-start.3 = (bf16[56,1280]{1,0:T(8,128)(2,1)S(1)}, bf16[56,1280]{1,0:T(8,128)(2,1)S(1)}, u32[]{:S(2)}, u32[]{:S(2)}) collective-permute-start(bf16[56,1280]{1,0:T(8,128)(2,1)S(1)} %fusion.1.refs_0_), channel_id=1, source_target_pairs={{0,8},{4,12},{8,0},{12,4},{16,24},{20,28},{24,16},{28,20},{1,9},{5... | collective-permute-start | bytes 430088 | tf_op jit(solution)/shard_map/ppermute | solution.py:33
  36.8 13.0 %collective-permute-start.11 = (bf16[480,256]{1,0:T(8,128)(2,1)S(1)}, bf16[480,256]{1,0:T(8,128)(2,1)S(1)}, u32[]{:S(2)}, u32[]{:S(2)}) collective-permute-start(bf16[480,256]{1,0:T(8,128)(2,1)S(1)} %get-tuple-element.17.refs_0_), channel_id=1, source_target_pairs={{0,3},{1,2},{2,1},{3,0},{4,7},{5,6},{6,5},{7,4},{8,11},{9,10},{10,... | collective-permute-start | bytes 737288 | tf_op jit(solution)/shard_map/ppermute | solution.py:33
  39.4 12.2 %collective-permute-start.10 = (bf16[480,256]{1,0:T(8,128)(2,1)S(1)}, bf16[480,256]{1,0:T(8,128)(2,1)S(1)}, u32[]{:S(2)}, u32[]{:S(2)}) collective-permute-start(bf16[480,256]{1,0:T(8,128)(2,1)S(1)} %get-tuple-element.17.refs_0_), channel_id=1, source_target_pairs={{0,2},{1,3},{2,0},{3,1},{4,6},{5,7},{6,4},{7,5},{8,10},{9,11},{10,... | collective-permute-start | bytes 737288 | tf_op jit(solution)/shard_map/ppermute | solution.py:33
  39.9 12.0 %collective-permute-start.9 = (bf16[480,256]{1,0:T(8,128)(2,1)S(1)}, bf16[480,256]{1,0:T(8,128)(2,1)S(1)}, u32[]{:S(2)}, u32[]{:S(2)}) collective-permute-start(bf16[480,256]{1,0:T(8,128)(2,1)S(1)} %get-tuple-element.17.refs_0_), channel_id=1, source_target_pairs={{0,1},{1,0},{2,3},{3,2},{4,5},{5,4},{6,7},{7,6},{8,9},{9,8},{10,11... | collective-permute-start | bytes 737288 | tf_op jit(solution)/shard_map/ppermute | solution.py:33
  40.2 12.8 %collective-permute-start.12 = (bf16[480,256]{1,0:T(8,128)(2,1)S(1)}, bf16[480,256]{1,0:T(8,128)(2,1)S(1)}, u32[]{:S(2)}, u32[]{:S(2)}) collective-permute-start(bf16[480,256]{1,0:T(8,128)(2,1)S(1)} %get-tuple-element.17.refs_0_), channel_id=1, source_target_pairs={{0,32},{32,0},{1,33},{33,1},{2,34},{34,2},{3,35},{35,3},{4,36},{36... | collective-permute-start | bytes 737288 | tf_op jit(solution)/shard_map/ppermute | solution.py:33
  55.9 19.1 %collective-permute-start.22 = (bf16[160,256]{1,0:T(8,128)(2,1)S(1)}, bf16[160,256]{1,0:T(8,128)(2,1)S(1)}, u32[]{:S(2)}, u32[]{:S(2)}) collective-permute-start(bf16[160,256]{1,0:T(8,128)(2,1)S(1)} %shard_map.122.refs_0_), channel_id=1, source_target_pairs={{0,28},{4,24},{8,20},{12,16},{16,12},{20,8},{24,4},{28,0},{1,29},{... | collective-permute-start | bytes 245768 | tf_op jit(solution)/shard_map/ppermute | solution.py:33
  56.0 21.4 %collective-permute-start.21 = (bf16[160,256]{1,0:T(8,128)(2,1)S(1)}, bf16[160,256]{1,0:T(8,128)(2,1)S(1)}, u32[]{:S(2)}, u32[]{:S(2)}) collective-permute-start(bf16[160,256]{1,0:T(8,128)(2,1)S(1)} %shard_map.122.refs_0_), channel_id=1, source_target_pairs={{0,24},{4,28},{8,16},{12,20},{16,8},{20,12},{24,0},{28,4},{1,25},{... | collective-permute-start | bytes 245768 | tf_op jit(solution)/shard_map/ppermute | solution.py:33
  58.9 19.1 %collective-permute-start.20 = (bf16[160,256]{1,0:T(8,128)(2,1)S(1)}, bf16[160,256]{1,0:T(8,128)(2,1)S(1)}, u32[]{:S(2)}, u32[]{:S(2)}) collective-permute-start(bf16[160,256]{1,0:T(8,128)(2,1)S(1)} %shard_map.122.refs_0_), channel_id=1, source_target_pairs={{0,20},{4,16},{8,28},{12,24},{16,4},{20,0},{24,12},{28,8},{1,21},{... | collective-permute-start | bytes 245768 | tf_op jit(solution)/shard_map/ppermute | solution.py:33
  69.5 21.2 %collective-permute-start = (bf16[144,512]{1,0:T(8,128)(2,1)}, bf16[144,512]{1,0:T(8,128)(2,1)S(1)}, u32[]{:S(2)}, u32[]{:S(2)}) collective-permute-start(bf16[144,512]{1,0:T(8,128)(2,1)} %shard_map.119.query_ref), channel_id=1, source_target_pairs={{0,128},{64,192},{128,0},{192,64},{1,129},{65,193},{129,1},{193,65... | collective-permute-start | bytes 442376 | tf_op jit(solution)/shard_map/ppermute | solution.py:33
  75.0 8.1 %collective-permute-start.18 = (bf16[160,256]{1,0:T(8,128)(2,1)S(1)}, bf16[160,256]{1,0:T(8,128)(2,1)S(1)}, u32[]{:S(2)}, u32[]{:S(2)}) collective-permute-start(bf16[160,256]{1,0:T(8,128)(2,1)S(1)} %shard_map.122.refs_0_), channel_id=1, source_target_pairs={{0,12},{4,8},{8,4},{12,0},{16,28},{20,24},{24,20},{28,16},{1,13},{... | collective-permute-start | bytes 245768 | tf_op jit(solution)/shard_map/ppermute | solution.py:33
  77.9 7.1 %collective-permute-start.16 = (bf16[160,256]{1,0:T(8,128)(2,1)S(1)}, bf16[160,256]{1,0:T(8,128)(2,1)S(1)}, u32[]{:S(2)}, u32[]{:S(2)}) collective-permute-start(bf16[160,256]{1,0:T(8,128)(2,1)S(1)} %shard_map.122.refs_0_), channel_id=1, source_target_pairs={{0,4},{4,0},{8,12},{12,8},{16,20},{20,16},{24,28},{28,24},{1,5},{5... | collective-permute-start | bytes 245768 | tf_op jit(solution)/shard_map/ppermute | solution.py:33
  87.4 7.9 %collective-permute-start.25 = (bf16[256,256]{1,0:T(8,128)(2,1)S(1)}, bf16[256,256]{1,0:T(8,128)(2,1)S(1)}, u32[]{:S(2)}, u32[]{:S(2)}) collective-permute-start(bf16[256,256]{1,0:T(8,128)(2,1)S(1)} %shard_map.124.refs_0_), channel_id=1, source_target_pairs={{0,3},{1,2},{2,1},{3,0},{4,7},{5,6},{6,5},{7,4},{8,11},{9,10},{10,... | collective-permute-start | bytes 393224 | tf_op jit(solution)/shard_map/ppermute | solution.py:33
  89.9 6.5 %collective-permute-start.24 = (bf16[256,256]{1,0:T(8,128)(2,1)S(1)}, bf16[256,256]{1,0:T(8,128)(2,1)S(1)}, u32[]{:S(2)}, u32[]{:S(2)}) collective-permute-start(bf16[256,256]{1,0:T(8,128)(2,1)S(1)} %shard_map.124.refs_0_), channel_id=1, source_target_pairs={{0,2},{1,3},{2,0},{3,1},{4,6},{5,7},{6,4},{7,5},{8,10},{9,11},{10,... | collective-permute-start | bytes 393224 | tf_op jit(solution)/shard_map/ppermute | solution.py:33
  90.3 7.9 %collective-permute-start.23 = (bf16[256,256]{1,0:T(8,128)(2,1)S(1)}, bf16[256,256]{1,0:T(8,128)(2,1)S(1)}, u32[]{:S(2)}, u32[]{:S(2)}) collective-permute-start(bf16[256,256]{1,0:T(8,128)(2,1)S(1)} %shard_map.124.refs_0_), channel_id=1, source_target_pairs={{0,1},{1,0},{2,3},{3,2},{4,5},{5,4},{6,7},{7,6},{8,9},{9,8},{10,11... | collective-permute-start | bytes 393224 | tf_op jit(solution)/shard_map/ppermute | solution.py:33
  90.7 11.1 %collective-permute-start.31 = (bf16[144,512]{1,0:T(8,128)(2,1)S(1)}, bf16[144,512]{1,0:T(8,128)(2,1)S(1)}, u32[]{:S(2)}, u32[]{:S(2)}) collective-permute-start(bf16[144,512]{1,0:T(8,128)(2,1)S(1)} %copy-done.3), channel_id=1, source_target_pairs={{0,64},{64,0},{128,192},{192,128},{1,65},{65,1},{129,193},{193,129... | collective-permute-start | bytes 442376 | tf_op jit(solution)/shard_map/ppermute | solution.py:33
  90.7 16.0 %collective-permute-start.33 = (bf16[144,512]{1,0:T(8,128)(2,1)S(1)}, bf16[144,512]{1,0:T(8,128)(2,1)S(1)}, u32[]{:S(2)}, u32[]{:S(2)}) collective-permute-start(bf16[144,512]{1,0:T(8,128)(2,1)S(1)} %copy-done.3), channel_id=1, source_target_pairs={{0,192},{64,128},{128,64},{192,0},{1,193},{65,129},{129,65},{193,1... | collective-permute-start | bytes 442376 | tf_op jit(solution)/shard_map/ppermute | solution.py:33
  101.7 11.9 %collective-permute-start.30 = (bf16[128,512]{1,0:T(8,128)(2,1)S(1)}, bf16[128,512]{1,0:T(8,128)(2,1)S(1)}, u32[]{:S(2)}, u32[]{:S(2)}) collective-permute-start(bf16[128,512]{1,0:T(8,128)(2,1)S(1)} %shard_map.125), channel_id=1, source_target_pairs={{0,128},{64,192},{128,0},{192,64},{1,129},{65,193},{129,1},{193,65... | collective-permute-start | bytes 393224 | tf_op jit(solution)/shard_map/ppermute | solution.py:33
  103.8 13.6 %collective-permute-start.32 = (bf16[128,512]{1,0:T(8,128)(2,1)S(1)}, bf16[128,512]{1,0:T(8,128)(2,1)S(1)}, u32[]{:S(2)}, u32[]{:S(2)}) collective-permute-start(bf16[128,512]{1,0:T(8,128)(2,1)S(1)} %shard_map.126), channel_id=1, source_target_pairs={{0,64},{64,0},{128,192},{192,128},{1,65},{65,1},{129,193},{193,129... | collective-permute-start | bytes 393224 | tf_op jit(solution)/shard_map/ppermute | solution.py:33
  108.7 8.7 %collective-permute-start.34 = (bf16[128,512]{1,0:T(8,128)(2,1)S(1)}, bf16[128,512]{1,0:T(8,128)(2,1)S(1)}, u32[]{:S(2)}, u32[]{:S(2)}) collective-permute-start(bf16[128,512]{1,0:T(8,128)(2,1)S(1)} %shard_map.127), channel_id=1, source_target_pairs={{0,192},{64,128},{128,64},{192,0},{1,193},{65,129},{129,65},{193,1... | collective-permute-start | bytes 393224 | tf_op jit(solution)/shard_map/ppermute | solution.py:33
  (16 other events, 67.7 us)

commit v8 on v7

--- a/solution.py
+++ b/solution.py
@@ -45,7 +45,7 @@
 
 def qkv_kernel(me_ref, *refs):
     pieces, refs = refs[:TENSOR], refs[TENSOR:]
-    gain_ref, weight_ref, cross_ref, kv_ref, normed, raw, out_rows = refs
+    gain_ref, weight_ref, cross_ref, kv_ref, fold_ref, normed, raw, out_rows = refs
     me = me_ref[0]
     rows = raw.shape[0] // TENSOR
     for step in range(TENSOR):
@@ -72,7 +72,7 @@
     column = lax.broadcasted_iota(jnp.int32, (TENSOR * SHARE, TENSOR * SLOT), 1)
     chosen = (column == row + ((row * 3277) >> 16) * (SLOT - SHARE)).astype(F32).astype(BF16)
     fold = jnp.dot(chosen, fold.astype(BF16), preferred_element_type=F32)
-    kv_ref[4 * EHD :, :] = fold.astype(BF16)
+    fold_ref[...] = fold.astype(BF16)
 
 
 def local_kernel(normed_ref, raw_ref, weight_ref, cross_ref, q_ref, base_ref):
@@ -116,7 +116,7 @@
     for k in range(8):
         owner = jnp.bitwise_xor(c, k // 4) * 4 + jnp.bitwise_xor(x, k % 4)
         low = pl.multiple_of(owner * size, size)
-        stacked[pl.ds(low, size), :] = pieces[k][4 * EHD :, :]
+        stacked[pl.ds(low, size), :] = pieces[k][...]
     for t in range(TENSOR):
         row = lax.broadcasted_iota(jnp.int32, (size, 8 * size), 0)
         column = lax.broadcasted_iota(jnp.int32, (size, 8 * size), 1)
@@ -223,34 +223,29 @@
     member = mine.astype(F32)
     count = jnp.sum(member)
 
-    @pl.when(count <= few)
-    def _():
-        below = lax.broadcasted_iota(jnp.int32, (rows, rows), 0)
-        below = below < lax.broadcasted_iota(jnp.int32, (rows, rows), 1)
-        rank = jnp.dot(
-            jnp.broadcast_to(member, (8, rows)).astype(BF16),
-            below.astype(F32).astype(BF16),
-            preferred_element_type=F32,
-        )[0:1]
-        slot = lax.broadcasted_iota(jnp.int32, (few, rows), 0).astype(F32)
-        chosen = jnp.where(rank == slot, member, 0.0)
+    below = lax.broadcasted_iota(jnp.int32, (rows, rows), 0)
+    below = below < lax.broadcasted_iota(jnp.int32, (rows, rows), 1)
+    rank = jnp.dot(
+        jnp.broadcast_to(member, (8, rows)).astype(BF16),
+        below.astype(F32).astype(BF16),
+        preferred_element_type=F32,
+    )[0:1]
+    out_ref[...] = jnp.zeros_like(out_ref)
+
+    def half(step, carry):
+        slot = lax.broadcasted_iota(jnp.int32, (few, rows), 0) + step * few
+        chosen = jnp.where(rank == slot.astype(F32), member, 0.0)
         picked = chosen.astype(BF16)
         q = jnp.dot(picked, query_ref[:rows, :], preferred_element_type=F32).astype(BF16)
         q = jnp.concatenate([q[:, head * HD : (head + 1) * HD] for head in range(4)], axis=0)
         bound = jnp.sum(chosen * limit, axis=-1, keepdims=True)
         out = decode_rows(q, jnp.concatenate([bound] * 4, axis=0), first, slabs)
         out = jnp.concatenate([out[head * few : (head + 1) * few] for head in range(4)], axis=1)
-        back = chosen.T.astype(BF16)
-        out_ref[...] = jnp.dot(back, out, preferred_element_type=F32).astype(BF16)
-
-    @pl.when(count > few)
-    def _():
-        bound = jnp.broadcast_to(limit, (8, rows)).T[:, 0:1]
-        q = [query_ref[:rows, head * HD : (head + 1) * HD] for head in range(4)]
-        q = jnp.concatenate(q, axis=0)
-        out = decode_rows(q, jnp.concatenate([bound] * 4, axis=0), first, slabs)
-        for head in range(4):
-            out_ref[:, head * HD : (head + 1) * HD] = out[head * rows : (head + 1) * rows]
+        back = jnp.dot(chosen.T.astype(BF16), out, preferred_element_type=F32)
+        out_ref[...] = (out_ref[...].astype(F32) + back).astype(BF16)
+        return carry
+
+    lax.fori_loop(0, jnp.where(count > few, 2, 1), half, 0)
 
 
 def limits(mib):
@@ -359,19 +354,21 @@
     pieces = gather_tensor(jnp.concatenate([own, share], axis=0))
     qkv_weight = enc_qkv.transpose(0, 2, 1)
     row_shape = jax.ShapeDtypeStruct((rows, width), BF16)
-    kv, normed, raw = pl.pallas_call(
+    kv, share, normed, raw = pl.pallas_call(
         qkv_kernel,
         out_shape=(
-            jax.ShapeDtypeStruct((4 * EHD + TENSOR * SHARE, rows), BF16),
+            jax.ShapeDtypeStruct((4 * EHD, rows), BF16),
+            jax.ShapeDtypeStruct((TENSOR * SHARE, 2 * HD), BF16),
             row_shape,
             row_shape,
         ),
         in_specs=[smem()] + vmem(TENSOR + 3),
-        out_specs=tuple(vmem(3)),
+        out_specs=tuple(vmem(4)),
         scratch_shapes=[pltpu.VMEM((TENSOR * SLOT, width), BF16)],
         compiler_params=limits(16),
     )(me, *pieces, gain_row, qkv_weight, cross_kv)
     kv_pieces = gather_xc(kv)
+    shares = gather_xc(share)
     q, base = pl.pallas_call(
         local_kernel,
         out_shape=(
@@ -402,7 +399,7 @@
         out_specs=vmem(1)[0],
         scratch_shapes=[pltpu.VMEM((TENSOR * 2 * EHD, 2 * HD), BF16)],
         compiler_params=limits(16),
-    )(place, *kv_pieces)
+    )(place, *shares)
     slab = pl.pallas_call(
         cross_kernel,
         out_shape=jax.ShapeDtypeStruct((rows, 2 * HD), BF16),

time: 119 us -> 129 us (1.084)
  starting transfers between devices: 56.4 us -> 78.9 us
  waiting for transfers between devices: 33.6 us -> 21.2 us
    ppermute x34 -> x41, starting transfers between devices: 54.8 us -> 77.2 us  [xor_permute(): return lax.ppermute(values, axes, [(i, i ^ step) for i in range(size)])]
    ppermute x34 -> x41, waiting for transfers between devices: 33.6 us -> 21.2 us  [xor_permute(): return lax.ppermute(values, axes, [(i, i ^ step) for i in range(size)])]
  transfers between devices with their start and end apart: 35 -> 42, of which waited for: 12 -> 10; matrix products, arithmetic and copies ran while one was open for 1% -> 1% of each run, Pallas kernels for 17% -> 17%
where the time goes in v8:
time: 129 us; the launch traced here: 128 us
  starting transfers between devices  78.9 us (61%)
  Pallas kernels  23.5 us (18%)
  waiting for transfers between devices  21.2 us (16%)
  local copies, waits for them, and re-layouts  3.11 us (2%)
    ppermute x41, starting transfers between devices, xor_permute(): return lax.ppermute(values, axes, [(i, i ^ step) for i in range(size)])  77.2 us
    ppermute x41, waiting for transfers between devices, xor_permute(): return lax.ppermute(values, axes, [(i, i ^ step) for i in range(size)])  21.2 us
    pallas_call x4, Pallas kernels, on_device(): pl.pallas_call(decode_kernel, out_shape=jax.ShapeDtypeStruct((dec_rows, 4...  7.57 us
    pallas_call x1, Pallas kernels, on_device(): pl.pallas_call(functools.partial(query_last_kernel, dec_width), grid=(las...  4.91 us
    pallas_call x1, Pallas kernels, on_device(): pl.pallas_call(query_first_kernel, grid=(first_steps,), out_shape=(jax.Sh...  4.45 us
  transfers between devices with their start and end apart: 42, of which 10 were waited for; matrix products, arithmetic and copies ran while one was open for 1% of the time, Pallas kernels for 17%

profile of v8, /device:TPU:1, one launch (start us, length us, event | category | flops | bytes accessed | tf_op | source)
XLA Modules:
  0.0 127.6 jit_solution(9951635687715348972)
XLA Ops:
  1.7 6.5 %collective-permute-start.2 = (bf16[56,1280]{1,0:T(8,128)(2,1)S(1)}, bf16[56,1280]{1,0:T(8,128)(2,1)S(1)}, u32[]{:S(2)}, u32[]{:S(2)}) collective-permute-start(bf16[56,1280]{1,0:T(8,128)(2,1)S(1)} %fusion.1.refs_0_), channel_id=1, source_target_pairs={{0,4},{4,0},{8,12},{12,8},{16,20},{20,16},{24,28},{28,24},{1,5},{5... | collective-permute-start | bytes 430088 | tf_op jit(solution)/shard_map/ppermute | solution.py:33
  8.3 5.2 %collective-permute-start.3 = (bf16[56,1280]{1,0:T(8,128)(2,1)S(1)}, bf16[56,1280]{1,0:T(8,128)(2,1)S(1)}, u32[]{:S(2)}, u32[]{:S(2)}) collective-permute-start(bf16[56,1280]{1,0:T(8,128)(2,1)S(1)} %fusion.1.refs_0_), channel_id=1, source_target_pairs={{0,8},{4,12},{8,0},{12,4},{16,24},{20,28},{24,16},{28,20},{1,9},{5... | collective-permute-start | bytes 430088 | tf_op jit(solution)/shard_map/ppermute | solution.py:33
  14.6 2.9 %collective-permute-start.5 = (bf16[56,1280]{1,0:T(8,128)(2,1)S(1)}, bf16[56,1280]{1,0:T(8,128)(2,1)S(1)}, u32[]{:S(2)}, u32[]{:S(2)}) collective-permute-start(bf16[56,1280]{1,0:T(8,128)(2,1)S(1)} %fusion.1.refs_0_), channel_id=1, source_target_pairs={{0,16},{4,20},{8,24},{12,28},{16,0},{20,4},{24,8},{28,12},{1,17},{... | collective-permute-start | bytes 430088 | tf_op jit(solution)/shard_map/ppermute | solution.py:33
  17.6 3.2 %collective-permute-start.7 = (bf16[56,1280]{1,0:T(8,128)(2,1)S(1)}, bf16[56,1280]{1,0:T(8,128)(2,1)S(1)}, u32[]{:S(2)}, u32[]{:S(2)}) collective-permute-start(bf16[56,1280]{1,0:T(8,128)(2,1)S(1)} %fusion.1.refs_0_), channel_id=1, source_target_pairs={{0,24},{4,28},{8,16},{12,20},{16,8},{20,12},{24,0},{28,4},{1,25},{... | collective-permute-start | bytes 430088 | tf_op jit(solution)/shard_map/ppermute | solution.py:33
  23.3 3.2 %collective-permute-done.5.refs_4_ = bf16[56,1280]{1,0:T(8,128)(2,1)S(1)} collective-permute-done((bf16[56,1280]{1,0:T(8,128)(2,1)S(1)}, bf16[56,1280]{1,0:T(8,128)(2,1)S(1)}, u32[]{:S(2)}, u32[]{:S(2)}) %collective-permute-start.5) | collective-permute-done | bytes 143392 | tf_op jit(solution)/shard_map/ppermute | solution.py:33
  26.5 3.5 %collective-permute-done.7.refs_6_ = bf16[56,1280]{1,0:T(8,128)(2,1)S(1)} collective-permute-done((bf16[56,1280]{1,0:T(8,128)(2,1)S(1)}, bf16[56,1280]{1,0:T(8,128)(2,1)S(1)}, u32[]{:S(2)}, u32[]{:S(2)}) %collective-permute-start.7) | collective-permute-done | bytes 143392 | tf_op jit(solution)/shard_map/ppermute | solution.py:33
  35.0 2.4 %collective-permute-start.10 = (bf16[320,256]{1,0:T(8,128)(2,1)S(1)}, bf16[320,256]{1,0:T(8,128)(2,1)S(1)}, u32[]{:S(2)}, u32[]{:S(2)}) collective-permute-start(bf16[320,256]{1,0:T(8,128)(2,1)S(1)} %get-tuple-element.18.refs_0_), channel_id=1, source_target_pairs={{0,2},{1,3},{2,0},{3,1},{4,6},{5,7},{6,4},{7,5},{8,10},{9,11},{10,... | collective-permute-start | bytes 491528 | tf_op jit(solution)/shard_map/ppermute | solution.py:33
  37.7 3.7 %collective-permute-start.24 = (bf16[160,256]{1,0:T(8,128)(2,1)S(1)}, bf16[160,256]{1,0:T(8,128)(2,1)S(1)}, u32[]{:S(2)}, u32[]{:S(2)}) collective-permute-start(bf16[160,256]{1,0:T(8,128)(2,1)S(1)} %get-tuple-element.19.refs_0_), channel_id=1, source_target_pairs={{0,2},{1,3},{2,0},{3,1},{4,6},{5,7},{6,4},{7,5},{8,10},{9,11},{10,... | collective-permute-start | bytes 245768 | tf_op jit(solution)/shard_map/ppermute | solution.py:33
  41.5 5.6 %collective-permute-start.12 = (bf16[320,256]{1,0:T(8,128)(2,1)S(1)}, bf16[320,256]{1,0:T(8,128)(2,1)S(1)}, u32[]{:S(2)}, u32[]{:S(2)}) collective-permute-start(bf16[320,256]{1,0:T(8,128)(2,1)S(1)} %get-tuple-element.18.refs_0_), channel_id=1, source_target_pairs={{0,32},{32,0},{1,33},{33,1},{2,34},{34,2},{3,35},{35,3},{4,36},{36... | collective-permute-start | bytes 491528 | tf_op jit(solution)/shard_map/ppermute | solution.py:33
  48.4 2.5 %collective-permute-start.15 = (bf16[320,256]{1,0:T(8,128)(2,1)S(1)}, bf16[320,256]{1,0:T(8,128)(2,1)S(1)}, u32[]{:S(2)}, u32[]{:S(2)}) collective-permute-start(bf16[320,256]{1,0:T(8,128)(2,1)S(1)} %collective-permute-done.11.refs_3_), channel_id=1, source_target_pairs={{0,32},{32,0},{1,33},{33,1},{2,34},{34,2},{3,35},{35,3},{4,36},{36... | collective-permute-start | bytes 491528 | tf_op jit(solution)/shard_map/ppermute | solution.py:33
  50.9 5.2 %collective-permute-done.25.refs_3_ = bf16[160,256]{1,0:T(8,128)(2,1)S(1)} collective-permute-done((bf16[160,256]{1,0:T(8,128)(2,1)S(1)}, bf16[160,256]{1,0:T(8,128)(2,1)S(1)}, u32[]{:S(2)}, u32[]{:S(2)}) %collective-permute-start.25) | collective-permute-done | bytes 81952 | tf_op jit(solution)/shard_map/ppermute | solution.py:33
  58.4 2.4 %shard_map.122.refs_0_ = bf16[160,256]{1,0:T(8,128)(2,1)S(1)} custom-call(bf16[2,256,80]{2,1,0:T(8,128)(2,1)S(1)} %get-tuple-element.17.q_ref, bf16[320,256]{1,0:T(8,128)(2,1)S(1)} %get-tuple-element.18.refs_0_, bf16[320,256]{1,0:T(8,128)(2,1)S(1)} %collective-permute-done.9.refs_1_, bf16[320,256]{1,0:T(8,128)(2,1)S(1)} %collective-permute-done.10.refs_2_, ...), custom_call_target="tpu_custom_call" | custom-call | tf_op jit(solution)/shard_map/pallas_call | solution.py:386
  63.6 4.4 %shard_map.118 = (f32[128,512]{1,0:T(8,128)}, f32[128,128]{1,0:T(8,128)}) custom-call(bf16[128,8192]{1,0:T(8,128)(2,1)} %x_ref.3, f32[1,8192]{1,0:T(1,128)} %bitcast.13, bf16[8192,512]{1,0:T(8,128)(2,1)} %refs_3_.3, bf16[8192,512]{1,0:T(8,128)(2,1)} %refs_3_.3, bf16[8192,512]{1,0:T(8,128)(2,1)} %refs_3_.3, bf16[8192,512]{1,0:T(8,128)(2,1)} %refs_3_.3), custom_call_target="tpu_custom_call" | custom-call | tf_op jit(solution)/shard_map/pallas_call | solution.py:307
  68.0 4.9 %shard_map.119.query_ref = bf16[144,512]{1,0:T(8,128)(2,1)} custom-call(bf16[128,8192]{1,0:T(8,128)(2,1)} %x_ref.3, f32[1,8192]{1,0:T(1,128)} %bitcast.14, bf16[8192,512]{1,0:T(8,128)(2,1)} %refs_3_.3, bf16[8192,512]{1,0:T(8,128)(2,1)} %refs_3_.3, bf16[8192,512]{1,0:T(8,128)(2,1)} %refs_3_.3, bf16[8192,512]{1,0:T(8,128)(2,1)} %refs_3_.3, ...), custom_call_target="tpu_custom_call" | custom-call | tf_op jit(solution)/shard_map/pallas_call | solution.py:322
  73.0 4.5 %collective-permute-start.38 = (bf16[144,512]{1,0:T(8,128)(2,1)}, bf16[144,512]{1,0:T(8,128)(2,1)S(1)}, u32[]{:S(2)}, u32[]{:S(2)}) collective-permute-start(bf16[144,512]{1,0:T(8,128)(2,1)} %shard_map.119.query_ref), channel_id=1, source_target_pairs={{0,64},{64,0},{128,192},{192,128},{1,65},{65,1},{129,193},{193,129... | collective-permute-start | bytes 442376 | tf_op jit(solution)/shard_map/ppermute | solution.py:33
  80.3 2.1 %collective-permute-start.21 = (bf16[160,256]{1,0:T(8,128)(2,1)S(1)}, bf16[160,256]{1,0:T(8,128)(2,1)S(1)}, u32[]{:S(2)}, u32[]{:S(2)}) collective-permute-start(bf16[160,256]{1,0:T(8,128)(2,1)S(1)} %shard_map.122.refs_0_), channel_id=1, source_target_pairs={{0,24},{4,28},{8,16},{12,20},{16,8},{20,12},{24,0},{28,4},{1,25},{... | collective-permute-start | bytes 245768 | tf_op jit(solution)/shard_map/ppermute | solution.py:33
  90.9 2.3 %collective-permute-start.32 = (bf16[256,256]{1,0:T(8,128)(2,1)S(1)}, bf16[256,256]{1,0:T(8,128)(2,1)S(1)}, u32[]{:S(2)}, u32[]{:S(2)}) collective-permute-start(bf16[256,256]{1,0:T(8,128)(2,1)S(1)} %shard_map.124.refs_0_), channel_id=1, source_target_pairs={{0,3},{1,2},{2,1},{3,0},{4,7},{5,6},{6,5},{7,4},{8,11},{9,10},{10,... | collective-permute-start | bytes 393224 | tf_op jit(solution)/shard_map/ppermute | solution.py:33
  93.3 3.4 %collective-permute-start.33 = (bf16[256,256]{1,0:T(8,128)(2,1)S(1)}, bf16[256,256]{1,0:T(8,128)(2,1)S(1)}, u32[]{:S(2)}, u32[]{:S(2)}) collective-permute-start(bf16[256,256]{1,0:T(8,128)(2,1)S(1)} %shard_map.124.refs_0_), channel_id=1, source_target_pairs={{0,32},{32,0},{1,33},{33,1},{2,34},{34,2},{3,35},{35,3},{4,36},{36... | collective-permute-start | bytes 393224 | tf_op jit(solution)/shard_map/ppermute | solution.py:33
  96.7 3.8 %collective-permute-start = (bf16[144,512]{1,0:T(8,128)(2,1)S(1)}, bf16[144,512]{1,0:T(8,128)(2,1)S(1)}, u32[]{:S(2)}, u32[]{:S(2)}) collective-permute-start(bf16[144,512]{1,0:T(8,128)(2,1)S(1)} %copy-done.3), channel_id=1, source_target_pairs={{0,128},{64,192},{128,0},{192,64},{1,129},{65,193},{129,1},{193,65... | collective-permute-start | bytes 442376 | tf_op jit(solution)/shard_map/ppermute | solution.py:33
  102.6 1.9 %shard_map.126 = bf16[128,512]{1,0:T(8,128)(2,1)S(1)} custom-call(s32[3]{0:T(128)S(1)} %pad_add_fusion.place_ref, bf16[144,512]{1,0:T(8,128)(2,1)S(1)} %collective-permute-done.38.query_ref, bf16[256,256]{1,0:T(8,128)(2,1)S(1)} %shard_map.124.refs_0_, bf16[256,256]{1,0:T(8,128)(2,1)S(1)} %collective-permute-done.30.refs_1_, ...), custom_call_target="tpu_custom_call" | custom-call | tf_op jit(solution)/shard_map/pallas_call | solution.py:413
  104.5 2.0 %collective-permute-start.39 = (bf16[128,512]{1,0:T(8,128)(2,1)S(1)}, bf16[128,512]{1,0:T(8,128)(2,1)S(1)}, u32[]{:S(2)}, u32[]{:S(2)}) collective-permute-start(bf16[128,512]{1,0:T(8,128)(2,1)S(1)} %shard_map.126), channel_id=1, source_target_pairs={{0,64},{64,0},{128,192},{192,128},{1,65},{65,1},{129,193},{193,129... | collective-permute-start | bytes 393224 | tf_op jit(solution)/shard_map/ppermute | solution.py:33
  108.5 5.3 %collective-permute-start.37 = (bf16[128,512]{1,0:T(8,128)(2,1)S(1)}, bf16[128,512]{1,0:T(8,128)(2,1)S(1)}, u32[]{:S(2)}, u32[]{:S(2)}) collective-permute-start(bf16[128,512]{1,0:T(8,128)(2,1)S(1)} %shard_map.125), channel_id=1, source_target_pairs={{0,128},{64,192},{128,0},{192,64},{1,129},{65,193},{129,1},{193,65... | collective-permute-start | bytes 393224 | tf_op jit(solution)/shard_map/ppermute | solution.py:33
  115.6 4.2 %collective-permute-start.41 = (bf16[128,512]{1,0:T(8,128)(2,1)S(1)}, bf16[128,512]{1,0:T(8,128)(2,1)S(1)}, u32[]{:S(2)}, u32[]{:S(2)}) collective-permute-start(bf16[128,512]{1,0:T(8,128)(2,1)S(1)} %shard_map.127), channel_id=1, source_target_pairs={{0,192},{64,128},{128,64},{192,0},{1,193},{65,129},{129,65},{193,1... | collective-permute-start | bytes 393224 | tf_op jit(solution)/shard_map/ppermute | solution.py:33
  121.8 5.1 %collective-permute-done.41 = bf16[128,512]{1,0:T(8,128)(2,1)S(1)} collective-permute-done((bf16[128,512]{1,0:T(8,128)(2,1)S(1)}, bf16[128,512]{1,0:T(8,128)(2,1)S(1)}, u32[]{:S(2)}, u32[]{:S(2)}) %collective-permute-start.41) | collective-permute-done | bytes 131104 | tf_op jit(solution)/shard_map/ppermute | solution.py:33
  (86 shorter events, 36.9 us)
Async XLA Ops:
  1.7 15.8 %collective-permute-start.2 = (bf16[56,1280]{1,0:T(8,128)(2,1)S(1)}, bf16[56,1280]{1,0:T(8,128)(2,1)S(1)}, u32[]{:S(2)}, u32[]{:S(2)}) collective-permute-start(bf16[56,1280]{1,0:T(8,128)(2,1)S(1)} %fusion.1.refs_0_), channel_id=1, source_target_pairs={{0,4},{4,0},{8,12},{12,8},{16,20},{20,16},{24,28},{28,24},{1,5},{5... | collective-permute-start | bytes 430088 | tf_op jit(solution)/shard_map/ppermute | solution.py:33
  8.3 12.5 %collective-permute-start.3 = (bf16[56,1280]{1,0:T(8,128)(2,1)S(1)}, bf16[56,1280]{1,0:T(8,128)(2,1)S(1)}, u32[]{:S(2)}, u32[]{:S(2)}) collective-permute-start(bf16[56,1280]{1,0:T(8,128)(2,1)S(1)} %fusion.1.refs_0_), channel_id=1, source_target_pairs={{0,8},{4,12},{8,0},{12,4},{16,24},{20,28},{24,16},{28,20},{1,9},{5... | collective-permute-start | bytes 430088 | tf_op jit(solution)/shard_map/ppermute | solution.py:33
  14.6 11.9 %collective-permute-start.5 = (bf16[56,1280]{1,0:T(8,128)(2,1)S(1)}, bf16[56,1280]{1,0:T(8,128)(2,1)S(1)}, u32[]{:S(2)}, u32[]{:S(2)}) collective-permute-start(bf16[56,1280]{1,0:T(8,128)(2,1)S(1)} %fusion.1.refs_0_), channel_id=1, source_target_pairs={{0,16},{4,20},{8,24},{12,28},{16,0},{20,4},{24,8},{28,12},{1,17},{... | collective-permute-start | bytes 430088 | tf_op jit(solution)/shard_map/ppermute | solution.py:33
  17.6 12.4 %collective-permute-start.7 = (bf16[56,1280]{1,0:T(8,128)(2,1)S(1)}, bf16[56,1280]{1,0:T(8,128)(2,1)S(1)}, u32[]{:S(2)}, u32[]{:S(2)}) collective-permute-start(bf16[56,1280]{1,0:T(8,128)(2,1)S(1)} %fusion.1.refs_0_), channel_id=1, source_target_pairs={{0,24},{4,28},{8,16},{12,20},{16,8},{20,12},{24,0},{28,4},{1,25},{... | collective-permute-start | bytes 430088 | tf_op jit(solution)/shard_map/ppermute | solution.py:33
  33.7 13.4 %collective-permute-start.9 = (bf16[320,256]{1,0:T(8,128)(2,1)S(1)}, bf16[320,256]{1,0:T(8,128)(2,1)S(1)}, u32[]{:S(2)}, u32[]{:S(2)}) collective-permute-start(bf16[320,256]{1,0:T(8,128)(2,1)S(1)} %get-tuple-element.18.refs_0_), channel_id=1, source_target_pairs={{0,1},{1,0},{2,3},{3,2},{4,5},{5,4},{6,7},{7,6},{8,9},{9,8},{10,11... | collective-permute-start | bytes 491528 | tf_op jit(solution)/shard_map/ppermute | solution.py:33
  35.0 12.1 %collective-permute-start.10 = (bf16[320,256]{1,0:T(8,128)(2,1)S(1)}, bf16[320,256]{1,0:T(8,128)(2,1)S(1)}, u32[]{:S(2)}, u32[]{:S(2)}) collective-permute-start(bf16[320,256]{1,0:T(8,128)(2,1)S(1)} %get-tuple-element.18.refs_0_), channel_id=1, source_target_pairs={{0,2},{1,3},{2,0},{3,1},{4,6},{5,7},{6,4},{7,5},{8,10},{9,11},{10,... | collective-permute-start | bytes 491528 | tf_op jit(solution)/shard_map/ppermute | solution.py:33
  37.5 10.9 %collective-permute-start.11 = (bf16[320,256]{1,0:T(8,128)(2,1)S(1)}, bf16[320,256]{1,0:T(8,128)(2,1)S(1)}, u32[]{:S(2)}, u32[]{:S(2)}) collective-permute-start(bf16[320,256]{1,0:T(8,128)(2,1)S(1)} %get-tuple-element.18.refs_0_), channel_id=1, source_target_pairs={{0,3},{1,2},{2,1},{3,0},{4,7},{5,6},{6,5},{7,4},{8,11},{9,10},{10,... | collective-permute-start | bytes 491528 | tf_op jit(solution)/shard_map/ppermute | solution.py:33
  37.7 13.2 %collective-permute-start.24 = (bf16[160,256]{1,0:T(8,128)(2,1)S(1)}, bf16[160,256]{1,0:T(8,128)(2,1)S(1)}, u32[]{:S(2)}, u32[]{:S(2)}) collective-permute-start(bf16[160,256]{1,0:T(8,128)(2,1)S(1)} %get-tuple-element.19.refs_0_), channel_id=1, source_target_pairs={{0,2},{1,3},{2,0},{3,1},{4,6},{5,7},{6,4},{7,5},{8,10},{9,11},{10,... | collective-permute-start | bytes 245768 | tf_op jit(solution)/shard_map/ppermute | solution.py:33
  41.5 15.5 %collective-permute-start.12 = (bf16[320,256]{1,0:T(8,128)(2,1)S(1)}, bf16[320,256]{1,0:T(8,128)(2,1)S(1)}, u32[]{:S(2)}, u32[]{:S(2)}) collective-permute-start(bf16[320,256]{1,0:T(8,128)(2,1)S(1)} %get-tuple-element.18.refs_0_), channel_id=1, source_target_pairs={{0,32},{32,0},{1,33},{33,1},{2,34},{34,2},{3,35},{35,3},{4,36},{36... | collective-permute-start | bytes 491528 | tf_op jit(solution)/shard_map/ppermute | solution.py:33
  47.1 10.4 %collective-permute-start.13 = (bf16[320,256]{1,0:T(8,128)(2,1)S(1)}, bf16[320,256]{1,0:T(8,128)(2,1)S(1)}, u32[]{:S(2)}, u32[]{:S(2)}) collective-permute-start(bf16[320,256]{1,0:T(8,128)(2,1)S(1)} %collective-permute-done.9.refs_1_), channel_id=1, source_target_pairs={{0,32},{32,0},{1,33},{33,1},{2,34},{34,2},{3,35},{35,3},{4,36},{36... | collective-permute-start | bytes 491528 | tf_op jit(solution)/shard_map/ppermute | solution.py:33
  47.1 11.2 %collective-permute-start.14 = (bf16[320,256]{1,0:T(8,128)(2,1)S(1)}, bf16[320,256]{1,0:T(8,128)(2,1)S(1)}, u32[]{:S(2)}, u32[]{:S(2)}) collective-permute-start(bf16[320,256]{1,0:T(8,128)(2,1)S(1)} %collective-permute-done.10.refs_2_), channel_id=1, source_target_pairs={{0,32},{32,0},{1,33},{33,1},{2,34},{34,2},{3,35},{35,3},{4,36},{36... | collective-permute-start | bytes 491528 | tf_op jit(solution)/shard_map/ppermute | solution.py:33
  57.6 15.4 %collective-permute-start.28 = (bf16[160,256]{1,0:T(8,128)(2,1)S(1)}, bf16[160,256]{1,0:T(8,128)(2,1)S(1)}, u32[]{:S(2)}, u32[]{:S(2)}) collective-permute-start(bf16[160,256]{1,0:T(8,128)(2,1)S(1)} %collective-permute-done.24.refs_2_), channel_id=1, source_target_pairs={{0,32},{32,0},{1,33},{33,1},{2,34},{34,2},{3,35},{35,3},{4,36},{36... | collective-permute-start | bytes 245768 | tf_op jit(solution)/shard_map/ppermute | solution.py:33
  58.3 19.1 %collective-permute-start.29 = (bf16[160,256]{1,0:T(8,128)(2,1)S(1)}, bf16[160,256]{1,0:T(8,128)(2,1)S(1)}, u32[]{:S(2)}, u32[]{:S(2)}) collective-permute-start(bf16[160,256]{1,0:T(8,128)(2,1)S(1)} %collective-permute-done.25.refs_3_), channel_id=1, source_target_pairs={{0,32},{32,0},{1,33},{33,1},{2,34},{34,2},{3,35},{35,3},{4,36},{36... | collective-permute-start | bytes 245768 | tf_op jit(solution)/shard_map/ppermute | solution.py:33
  60.8 18.1 %collective-permute-start.16 = (bf16[160,256]{1,0:T(8,128)(2,1)S(1)}, bf16[160,256]{1,0:T(8,128)(2,1)S(1)}, u32[]{:S(2)}, u32[]{:S(2)}) collective-permute-start(bf16[160,256]{1,0:T(8,128)(2,1)S(1)} %shard_map.122.refs_0_), channel_id=1, source_target_pairs={{0,4},{4,0},{8,12},{12,8},{16,20},{20,16},{24,28},{28,24},{1,5},{5... | collective-permute-start | bytes 245768 | tf_op jit(solution)/shard_map/ppermute | solution.py:33
  62.3 18.0 %collective-permute-start.17 = (bf16[160,256]{1,0:T(8,128)(2,1)S(1)}, bf16[160,256]{1,0:T(8,128)(2,1)S(1)}, u32[]{:S(2)}, u32[]{:S(2)}) collective-permute-start(bf16[160,256]{1,0:T(8,128)(2,1)S(1)} %shard_map.122.refs_0_), channel_id=1, source_target_pairs={{0,8},{4,12},{8,0},{12,4},{16,24},{20,28},{24,16},{28,20},{1,9},{5... | collective-permute-start | bytes 245768 | tf_op jit(solution)/shard_map/ppermute | solution.py:33
  62.5 19.9 %collective-permute-start.18 = (bf16[160,256]{1,0:T(8,128)(2,1)S(1)}, bf16[160,256]{1,0:T(8,128)(2,1)S(1)}, u32[]{:S(2)}, u32[]{:S(2)}) collective-permute-start(bf16[160,256]{1,0:T(8,128)(2,1)S(1)} %shard_map.122.refs_0_), channel_id=1, source_target_pairs={{0,12},{4,8},{8,4},{12,0},{16,28},{20,24},{24,20},{28,16},{1,13},{... | collective-permute-start | bytes 245768 | tf_op jit(solution)/shard_map/ppermute | solution.py:33
  73.0 23.7 %collective-permute-start.38 = (bf16[144,512]{1,0:T(8,128)(2,1)}, bf16[144,512]{1,0:T(8,128)(2,1)S(1)}, u32[]{:S(2)}, u32[]{:S(2)}) collective-permute-start(bf16[144,512]{1,0:T(8,128)(2,1)} %shard_map.119.query_ref), channel_id=1, source_target_pairs={{0,64},{64,0},{128,192},{192,128},{1,65},{65,1},{129,193},{193,129... | collective-permute-start | bytes 442376 | tf_op jit(solution)/shard_map/ppermute | solution.py:33
  89.3 11.2 %collective-permute-start.30 = (bf16[256,256]{1,0:T(8,128)(2,1)S(1)}, bf16[256,256]{1,0:T(8,128)(2,1)S(1)}, u32[]{:S(2)}, u32[]{:S(2)}) collective-permute-start(bf16[256,256]{1,0:T(8,128)(2,1)S(1)} %shard_map.124.refs_0_), channel_id=1, source_target_pairs={{0,1},{1,0},{2,3},{3,2},{4,5},{5,4},{6,7},{7,6},{8,9},{9,8},{10,11... | collective-permute-start | bytes 393224 | tf_op jit(solution)/shard_map/ppermute | solution.py:33
  89.4 11.3 %collective-permute-start.31 = (bf16[256,256]{1,0:T(8,128)(2,1)S(1)}, bf16[256,256]{1,0:T(8,128)(2,1)S(1)}, u32[]{:S(2)}, u32[]{:S(2)}) collective-permute-start(bf16[256,256]{1,0:T(8,128)(2,1)S(1)} %shard_map.124.refs_0_), channel_id=1, source_target_pairs={{0,2},{1,3},{2,0},{3,1},{4,6},{5,7},{6,4},{7,5},{8,10},{9,11},{10,... | collective-permute-start | bytes 393224 | tf_op jit(solution)/shard_map/ppermute | solution.py:33
  90.9 10.1 %collective-permute-start.32 = (bf16[256,256]{1,0:T(8,128)(2,1)S(1)}, bf16[256,256]{1,0:T(8,128)(2,1)S(1)}, u32[]{:S(2)}, u32[]{:S(2)}) collective-permute-start(bf16[256,256]{1,0:T(8,128)(2,1)S(1)} %shard_map.124.refs_0_), channel_id=1, source_target_pairs={{0,3},{1,2},{2,1},{3,0},{4,7},{5,6},{6,5},{7,4},{8,11},{9,10},{10,... | collective-permute-start | bytes 393224 | tf_op jit(solution)/shard_map/ppermute | solution.py:33
  100.5 13.2 %collective-permute-start.40 = (bf16[144,512]{1,0:T(8,128)(2,1)S(1)}, bf16[144,512]{1,0:T(8,128)(2,1)S(1)}, u32[]{:S(2)}, u32[]{:S(2)}) collective-permute-start(bf16[144,512]{1,0:T(8,128)(2,1)S(1)} %copy-done.3), channel_id=1, source_target_pairs={{0,192},{64,128},{128,64},{192,0},{1,193},{65,129},{129,65},{193,1... | collective-permute-start | bytes 442376 | tf_op jit(solution)/shard_map/ppermute | solution.py:33
  104.5 17.2 %collective-permute-start.39 = (bf16[128,512]{1,0:T(8,128)(2,1)S(1)}, bf16[128,512]{1,0:T(8,128)(2,1)S(1)}, u32[]{:S(2)}, u32[]{:S(2)}) collective-permute-start(bf16[128,512]{1,0:T(8,128)(2,1)S(1)} %shard_map.126), channel_id=1, source_target_pairs={{0,64},{64,0},{128,192},{192,128},{1,65},{65,1},{129,193},{193,129... | collective-permute-start | bytes 393224 | tf_op jit(solution)/shard_map/ppermute | solution.py:33
  108.5 13.3 %collective-permute-start.37 = (bf16[128,512]{1,0:T(8,128)(2,1)S(1)}, bf16[128,512]{1,0:T(8,128)(2,1)S(1)}, u32[]{:S(2)}, u32[]{:S(2)}) collective-permute-start(bf16[128,512]{1,0:T(8,128)(2,1)S(1)} %shard_map.125), channel_id=1, source_target_pairs={{0,128},{64,192},{128,0},{192,64},{1,129},{65,193},{129,1},{193,65... | collective-permute-start | bytes 393224 | tf_op jit(solution)/shard_map/ppermute | solution.py:33
  115.6 11.3 %collective-permute-start.41 = (bf16[128,512]{1,0:T(8,128)(2,1)S(1)}, bf16[128,512]{1,0:T(8,128)(2,1)S(1)}, u32[]{:S(2)}, u32[]{:S(2)}) collective-permute-start(bf16[128,512]{1,0:T(8,128)(2,1)S(1)} %shard_map.127), channel_id=1, source_target_pairs={{0,192},{64,128},{128,64},{192,0},{1,193},{65,129},{129,65},{193,1... | collective-permute-start | bytes 393224 | tf_op jit(solution)/shard_map/ppermute | solution.py:33
  (23 other events, 160.7 us)

commit v9 on v6

--- a/solution.py
+++ b/solution.py
@@ -221,34 +221,29 @@
     member = mine.astype(F32)
     count = jnp.sum(member)
 
-    @pl.when(count <= few)
-    def _():
-        below = lax.broadcasted_iota(jnp.int32, (rows, rows), 0)
-        below = below < lax.broadcasted_iota(jnp.int32, (rows, rows), 1)
-        rank = jnp.dot(
-            jnp.broadcast_to(member, (8, rows)).astype(BF16),
-            below.astype(F32).astype(BF16),
-            preferred_element_type=F32,
-        )[0:1]
-        slot = lax.broadcasted_iota(jnp.int32, (few, rows), 0).astype(F32)
-        chosen = jnp.where(rank == slot, member, 0.0)
+    below = lax.broadcasted_iota(jnp.int32, (rows, rows), 0)
+    below = below < lax.broadcasted_iota(jnp.int32, (rows, rows), 1)
+    rank = jnp.dot(
+        jnp.broadcast_to(member, (8, rows)).astype(BF16),
+        below.astype(F32).astype(BF16),
+        preferred_element_type=F32,
+    )[0:1]
+    out_ref[...] = jnp.zeros_like(out_ref)
+
+    def half(step, carry):
+        slot = lax.broadcasted_iota(jnp.int32, (few, rows), 0) + step * few
+        chosen = jnp.where(rank == slot.astype(F32), member, 0.0)
         picked = chosen.astype(BF16)
         q = jnp.dot(picked, query_ref[:rows, :], preferred_element_type=F32).astype(BF16)
         q = jnp.concatenate([q[:, head * HD : (head + 1) * HD] for head in range(4)], axis=0)
         bound = jnp.sum(chosen * limit, axis=-1, keepdims=True)
         out = decode_rows(q, jnp.concatenate([bound] * 4, axis=0), first, slabs)
         out = jnp.concatenate([out[head * few : (head + 1) * few] for head in range(4)], axis=1)
-        back = chosen.T.astype(BF16)
-        out_ref[...] = jnp.dot(back, out, preferred_element_type=F32).astype(BF16)
-
-    @pl.when(count > few)
-    def _():
-        bound = jnp.broadcast_to(limit, (8, rows)).T[:, 0:1]
-        q = [query_ref[:rows, head * HD : (head + 1) * HD] for head in range(4)]
-        q = jnp.concatenate(q, axis=0)
-        out = decode_rows(q, jnp.concatenate([bound] * 4, axis=0), first, slabs)
-        for head in range(4):
-            out_ref[:, head * HD : (head + 1) * HD] = out[head * rows : (head + 1) * rows]
+        back = jnp.dot(chosen.T.astype(BF16), out, preferred_element_type=F32)
+        out_ref[...] = (out_ref[...].astype(F32) + back).astype(BF16)
+        return carry
+
+    lax.fori_loop(0, jnp.where(count > few, 2, 1), half, 0)
 
 
 def limits(mib):

time: 121 us -> 120 us (level)
  transfers between devices with their start and end apart: 35 -> 35, of which waited for: 19 -> 20; matrix products, arithmetic and copies ran while one was open for 1% -> 1% of each run, Pallas kernels for 16% -> 16%
where the time goes in v9:
time: 120 us
  starting transfers between devices  59.3 us (49%)
  waiting for transfers between devices  33.6 us (28%)
  Pallas kernels  23 us (19%)
  local copies, waits for them, and re-layouts  3.11 us (3%)
    ppermute x34, starting transfers between devices, xor_permute(): return lax.ppermute(values, axes, [(i, i ^ step) for i in range(size)])  55.4 us
    ppermute x34, waiting for transfers between devices, xor_permute(): return lax.ppermute(values, axes, [(i, i ^ step) for i in range(size)])  31 us
    pallas_call x4, Pallas kernels, on_device(): pl.pallas_call(decode_kernel, out_shape=jax.ShapeDtypeStruct((dec_rows, 4...  7.51 us
    pallas_call x1, Pallas kernels, on_device(): pl.pallas_call(functools.partial(query_last_kernel, dec_width), grid=(las...  4.91 us
    pallas_call x1, Pallas kernels, on_device(): pl.pallas_call(query_first_kernel, grid=(first_steps,), out_shape=(jax.Sh...  4.45 us
    ppermute x1, starting transfers between devices, image_permute(): return lax.ppermute(values, ('zh', 'y', 'zl'), pairs)  3.94 us
    ppermute x1, waiting for transfers between devices, image_permute(): return lax.ppermute(values, ('zh', 'y', 'zl'), pairs)  2.66 us
  transfers between devices with their start and end apart: 35, of which 20 were waited for; matrix products, arithmetic and copies ran while one was open for 1% of the time, Pallas kernels for 16%

profile of v9, /device:TPU:32, one launch (start us, length us, event | category | flops | bytes accessed | tf_op | source)
XLA Modules:
  0.0 120.0 jit_solution(9131327331161353311)
XLA Ops:
  0.0 3.9 %collective-permute-start.1 = (bf16[32,1280]{1,0:T(8,128)(2,1)}, bf16[32,1280]{1,0:T(8,128)(2,1)S(1)}, u32[]{:S(2)}, u32[]{:S(2)}) collective-permute-start(bf16[32,1280]{1,0:T(8,128)(2,1)} %param.12), channel_id=1, source_target_pairs={{0,0},{4,64},{8,128},{12,192},{16,16},{20,80},{24,144},{28,208},{6... | collective-permute-start | bytes 245768 | tf_op jit(solution)/shard_map/ppermute | solution.py:43
  4.0 2.7 %collective-permute-done.1 = bf16[32,1280]{1,0:T(8,128)(2,1)S(1)} collective-permute-done((bf16[32,1280]{1,0:T(8,128)(2,1)}, bf16[32,1280]{1,0:T(8,128)(2,1)S(1)}, u32[]{:S(2)}, u32[]{:S(2)}) %collective-permute-start.1) | collective-permute-done | bytes 81952 | tf_op jit(solution)/shard_map/ppermute | solution.py:43
  6.7 8.1 %collective-permute-start.8 = (bf16[56,1280]{1,0:T(8,128)(2,1)S(1)}, bf16[56,1280]{1,0:T(8,128)(2,1)S(1)}, u32[]{:S(2)}, u32[]{:S(2)}) collective-permute-start(bf16[56,1280]{1,0:T(8,128)(2,1)S(1)} %fusion.1.refs_0_), channel_id=1, source_target_pairs={{0,28},{4,24},{8,20},{12,16},{16,12},{20,8},{24,4},{28,0},{1,29},{... | collective-permute-start | bytes 430088 | tf_op jit(solution)/shard_map/ppermute | solution.py:33
  17.0 3.2 %collective-permute-start.5 = (bf16[56,1280]{1,0:T(8,128)(2,1)S(1)}, bf16[56,1280]{1,0:T(8,128)(2,1)S(1)}, u32[]{:S(2)}, u32[]{:S(2)}) collective-permute-start(bf16[56,1280]{1,0:T(8,128)(2,1)S(1)} %fusion.1.refs_0_), channel_id=1, source_target_pairs={{0,16},{4,20},{8,24},{12,28},{16,0},{20,4},{24,8},{28,12},{1,17},{... | collective-permute-start | bytes 430088 | tf_op jit(solution)/shard_map/ppermute | solution.py:33
  22.3 4.0 %collective-permute-done.7.refs_6_ = bf16[56,1280]{1,0:T(8,128)(2,1)S(1)} collective-permute-done((bf16[56,1280]{1,0:T(8,128)(2,1)S(1)}, bf16[56,1280]{1,0:T(8,128)(2,1)S(1)}, u32[]{:S(2)}, u32[]{:S(2)}) %collective-permute-start.7) | collective-permute-done | bytes 143392 | tf_op jit(solution)/shard_map/ppermute | solution.py:33
  26.3 2.2 %collective-permute-start.2 = (bf16[56,1280]{1,0:T(8,128)(2,1)S(1)}, bf16[56,1280]{1,0:T(8,128)(2,1)S(1)}, u32[]{:S(2)}, u32[]{:S(2)}) collective-permute-start(bf16[56,1280]{1,0:T(8,128)(2,1)S(1)} %fusion.1.refs_0_), channel_id=1, source_target_pairs={{0,4},{4,0},{8,12},{12,8},{16,20},{20,16},{24,28},{28,24},{1,5},{5... | collective-permute-start | bytes 430088 | tf_op jit(solution)/shard_map/ppermute | solution.py:33
  35.8 2.8 %collective-permute-start.11 = (bf16[480,256]{1,0:T(8,128)(2,1)S(1)}, bf16[480,256]{1,0:T(8,128)(2,1)S(1)}, u32[]{:S(2)}, u32[]{:S(2)}) collective-permute-start(bf16[480,256]{1,0:T(8,128)(2,1)S(1)} %get-tuple-element.13.refs_0_), channel_id=1, source_target_pairs={{0,3},{1,2},{2,1},{3,0},{4,7},{5,6},{6,5},{7,4},{8,11},{9,10},{10,... | collective-permute-start | bytes 737288 | tf_op jit(solution)/shard_map/ppermute | solution.py:33
  40.0 9.2 %collective-permute-done.11.refs_3_ = bf16[480,256]{1,0:T(8,128)(2,1)S(1)} collective-permute-done((bf16[480,256]{1,0:T(8,128)(2,1)S(1)}, bf16[480,256]{1,0:T(8,128)(2,1)S(1)}, u32[]{:S(2)}, u32[]{:S(2)}) %collective-permute-start.11) | collective-permute-done | bytes 245792 | tf_op jit(solution)/shard_map/ppermute | solution.py:33
  51.4 2.4 %shard_map.121.refs_0_ = bf16[160,256]{1,0:T(8,128)(2,1)S(1)} custom-call(bf16[2,256,80]{2,1,0:T(8,128)(2,1)S(1)} %get-tuple-element.12.q_ref, bf16[480,256]{1,0:T(8,128)(2,1)S(1)} %get-tuple-element.13.refs_0_, bf16[480,256]{1,0:T(8,128)(2,1)S(1)} %collective-permute-done.9.refs_1_, bf16[480,256]{1,0:T(8,128)(2,1)S(1)} %collective-permute-done.10.refs_2_, ...), custom_call_target="tpu_custom_call" | custom-call | tf_op jit(solution)/shard_map/pallas_call | solution.py:374
  54.8 3.0 %collective-permute-start.21 = (bf16[160,256]{1,0:T(8,128)(2,1)S(1)}, bf16[160,256]{1,0:T(8,128)(2,1)S(1)}, u32[]{:S(2)}, u32[]{:S(2)}) collective-permute-start(bf16[160,256]{1,0:T(8,128)(2,1)S(1)} %shard_map.121.refs_0_), channel_id=1, source_target_pairs={{0,24},{4,28},{8,16},{12,20},{16,8},{20,12},{24,0},{28,4},{1,25},{... | collective-permute-start | bytes 245768 | tf_op jit(solution)/shard_map/ppermute | solution.py:33
  58.0 4.5 %shard_map.118 = (f32[128,512]{1,0:T(8,128)}, f32[128,128]{1,0:T(8,128)}) custom-call(bf16[128,8192]{1,0:T(8,128)(2,1)} %x_ref.3, f32[1,8192]{1,0:T(1,128)} %bitcast.12, bf16[8192,512]{1,0:T(8,128)(2,1)} %refs_3_.3, bf16[8192,512]{1,0:T(8,128)(2,1)} %refs_3_.3, bf16[8192,512]{1,0:T(8,128)(2,1)} %refs_3_.3, bf16[8192,512]{1,0:T(8,128)(2,1)} %refs_3_.3), custom_call_target="tpu_custom_call" | custom-call | tf_op jit(solution)/shard_map/pallas_call | solution.py:305
  62.5 4.9 %shard_map.119.query_ref = bf16[144,512]{1,0:T(8,128)(2,1)} custom-call(bf16[128,8192]{1,0:T(8,128)(2,1)} %x_ref.3, f32[1,8192]{1,0:T(1,128)} %bitcast.13, bf16[8192,512]{1,0:T(8,128)(2,1)} %refs_3_.3, bf16[8192,512]{1,0:T(8,128)(2,1)} %refs_3_.3, bf16[8192,512]{1,0:T(8,128)(2,1)} %refs_3_.3, bf16[8192,512]{1,0:T(8,128)(2,1)} %refs_3_.3, ...), custom_call_target="tpu_custom_call" | custom-call | tf_op jit(solution)/shard_map/pallas_call | solution.py:320
  67.4 5.0 %collective-permute-start.33 = (bf16[144,512]{1,0:T(8,128)(2,1)}, bf16[144,512]{1,0:T(8,128)(2,1)S(1)}, u32[]{:S(2)}, u32[]{:S(2)}) collective-permute-start(bf16[144,512]{1,0:T(8,128)(2,1)} %shard_map.119.query_ref), channel_id=1, source_target_pairs={{0,192},{64,128},{128,64},{192,0},{1,193},{65,129},{129,65},{193,1... | collective-permute-start | bytes 442376 | tf_op jit(solution)/shard_map/ppermute | solution.py:33
  73.6 2.6 %collective-permute-start.18 = (bf16[160,256]{1,0:T(8,128)(2,1)S(1)}, bf16[160,256]{1,0:T(8,128)(2,1)S(1)}, u32[]{:S(2)}, u32[]{:S(2)}) collective-permute-start(bf16[160,256]{1,0:T(8,128)(2,1)S(1)} %shard_map.121.refs_0_), channel_id=1, source_target_pairs={{0,12},{4,8},{8,4},{12,0},{16,28},{20,24},{24,20},{28,16},{1,13},{... | collective-permute-start | bytes 245768 | tf_op jit(solution)/shard_map/ppermute | solution.py:33
  82.4 2.8 %collective-permute-start.25 = (bf16[256,256]{1,0:T(8,128)(2,1)S(1)}, bf16[256,256]{1,0:T(8,128)(2,1)S(1)}, u32[]{:S(2)}, u32[]{:S(2)}) collective-permute-start(bf16[256,256]{1,0:T(8,128)(2,1)S(1)} %shard_map.123.refs_0_), channel_id=1, source_target_pairs={{0,3},{1,2},{2,1},{3,0},{4,7},{5,6},{6,5},{7,4},{8,11},{9,10},{10,... | collective-permute-start | bytes 393224 | tf_op jit(solution)/shard_map/ppermute | solution.py:33
  87.1 4.3 %collective-permute-start = (bf16[144,512]{1,0:T(8,128)(2,1)S(1)}, bf16[144,512]{1,0:T(8,128)(2,1)S(1)}, u32[]{:S(2)}, u32[]{:S(2)}) collective-permute-start(bf16[144,512]{1,0:T(8,128)(2,1)S(1)} %copy-done.3), channel_id=1, source_target_pairs={{0,128},{64,192},{128,0},{192,64},{1,129},{65,193},{129,1},{193,65... | collective-permute-start | bytes 442376 | tf_op jit(solution)/shard_map/ppermute | solution.py:33
  94.6 1.9 %shard_map.126 = bf16[128,512]{1,0:T(8,128)(2,1)S(1)} custom-call(s32[3]{0:T(128)S(1)} %pad_add_fusion.place_ref, bf16[144,512]{1,0:T(8,128)(2,1)S(1)} %collective-permute-done.33.query_ref, bf16[256,256]{1,0:T(8,128)(2,1)S(1)} %shard_map.123.refs_0_, bf16[256,256]{1,0:T(8,128)(2,1)S(1)} %collective-permute-done.23.refs_1_, ...), custom_call_target="tpu_custom_call" | custom-call | tf_op jit(solution)/shard_map/pallas_call | solution.py:401
  97.6 1.8 %collective-permute-done.31.query_ref = bf16[144,512]{1,0:T(8,128)(2,1)S(1)} collective-permute-done((bf16[144,512]{1,0:T(8,128)(2,1)S(1)}, bf16[144,512]{1,0:T(8,128)(2,1)S(1)}, u32[]{:S(2)}, u32[]{:S(2)}) %collective-permute-start.31) | collective-permute-done | bytes 147488 | tf_op jit(solution)/shard_map/ppermute | solution.py:33
  99.5 1.9 %shard_map.125 = bf16[128,512]{1,0:T(8,128)(2,1)S(1)} custom-call(s32[3]{0:T(128)S(1)} %pad_add_fusion.place_ref, bf16[144,512]{1,0:T(8,128)(2,1)S(1)} %collective-permute-done.31.query_ref, bf16[256,256]{1,0:T(8,128)(2,1)S(1)} %shard_map.123.refs_0_, bf16[256,256]{1,0:T(8,128)(2,1)S(1)} %collective-permute-done.23.refs_1_, ...), custom_call_target="tpu_custom_call" | custom-call | tf_op jit(solution)/shard_map/pallas_call | solution.py:401
  101.3 3.5 %collective-permute-start.32 = (bf16[128,512]{1,0:T(8,128)(2,1)S(1)}, bf16[128,512]{1,0:T(8,128)(2,1)S(1)}, u32[]{:S(2)}, u32[]{:S(2)}) collective-permute-start(bf16[128,512]{1,0:T(8,128)(2,1)S(1)} %shard_map.125), channel_id=1, source_target_pairs={{0,64},{64,0},{128,192},{192,128},{1,65},{65,1},{129,193},{193,129... | collective-permute-start | bytes 393224 | tf_op jit(solution)/shard_map/ppermute | solution.py:33
  104.8 1.9 %shard_map.124 = bf16[128,512]{1,0:T(8,128)(2,1)S(1)} custom-call(s32[3]{0:T(128)S(1)} %pad_add_fusion.place_ref, bf16[144,512]{1,0:T(8,128)(2,1)S(1)} %collective-permute-done.query_ref, bf16[256,256]{1,0:T(8,128)(2,1)S(1)} %shard_map.123.refs_0_, bf16[256,256]{1,0:T(8,128)(2,1)S(1)} %collective-permute-done.23.refs_1_, ...), custom_call_target="tpu_custom_call" | custom-call | tf_op jit(solution)/shard_map/pallas_call | solution.py:401
  106.7 4.7 %collective-permute-start.30 = (bf16[128,512]{1,0:T(8,128)(2,1)S(1)}, bf16[128,512]{1,0:T(8,128)(2,1)S(1)}, u32[]{:S(2)}, u32[]{:S(2)}) collective-permute-start(bf16[128,512]{1,0:T(8,128)(2,1)S(1)} %shard_map.124), channel_id=1, source_target_pairs={{0,128},{64,192},{128,0},{192,64},{1,129},{65,193},{129,1},{193,65... | collective-permute-start | bytes 393224 | tf_op jit(solution)/shard_map/ppermute | solution.py:33
  111.4 1.9 %shard_map.127 = bf16[128,512]{1,0:T(8,128)(2,1)S(1)} custom-call(s32[3]{0:T(128)S(1)} %pad_add_fusion.place_ref, bf16[144,512]{1,0:T(8,128)(2,1)S(1)} %copy-done.3, bf16[256,256]{1,0:T(8,128)(2,1)S(1)} %shard_map.123.refs_0_, bf16[256,256]{1,0:T(8,128)(2,1)S(1)} %collective-permute-done.23.refs_1_, bf16[256,256]{1,0:T(8,128)(2,1)S(1)} %collective-permute-done.24.refs_2_, ...), custom_call_target="tpu_custom_call" | custom-call | tf_op jit(solution)/shard_map/pallas_call | solution.py:401
  113.5 5.8 %collective-permute-done.30 = bf16[128,512]{1,0:T(8,128)(2,1)S(1)} collective-permute-done((bf16[128,512]{1,0:T(8,128)(2,1)S(1)}, bf16[128,512]{1,0:T(8,128)(2,1)S(1)}, u32[]{:S(2)}, u32[]{:S(2)}) %collective-permute-start.30) | collective-permute-done | bytes 131104 | tf_op jit(solution)/shard_map/ppermute | solution.py:33
  (71 shorter events, 31.0 us)
Async XLA Ops:
  6.7 14.1 %collective-permute-start.8 = (bf16[56,1280]{1,0:T(8,128)(2,1)S(1)}, bf16[56,1280]{1,0:T(8,128)(2,1)S(1)}, u32[]{:S(2)}, u32[]{:S(2)}) collective-permute-start(bf16[56,1280]{1,0:T(8,128)(2,1)S(1)} %fusion.1.refs_0_), channel_id=1, source_target_pairs={{0,28},{4,24},{8,20},{12,16},{16,12},{20,8},{24,4},{28,0},{1,29},{... | collective-permute-start | bytes 430088 | tf_op jit(solution)/shard_map/ppermute | solution.py:33
  14.8 11.5 %collective-permute-start.7 = (bf16[56,1280]{1,0:T(8,128)(2,1)S(1)}, bf16[56,1280]{1,0:T(8,128)(2,1)S(1)}, u32[]{:S(2)}, u32[]{:S(2)}) collective-permute-start(bf16[56,1280]{1,0:T(8,128)(2,1)S(1)} %fusion.1.refs_0_), channel_id=1, source_target_pairs={{0,24},{4,28},{8,16},{12,20},{16,8},{20,12},{24,0},{28,4},{1,25},{... | collective-permute-start | bytes 430088 | tf_op jit(solution)/shard_map/ppermute | solution.py:33
  15.8 13.3 %collective-permute-start.6 = (bf16[56,1280]{1,0:T(8,128)(2,1)S(1)}, bf16[56,1280]{1,0:T(8,128)(2,1)S(1)}, u32[]{:S(2)}, u32[]{:S(2)}) collective-permute-start(bf16[56,1280]{1,0:T(8,128)(2,1)S(1)} %fusion.1.refs_0_), channel_id=1, source_target_pairs={{0,20},{4,16},{8,28},{12,24},{16,4},{20,0},{24,12},{28,8},{1,21},{... | collective-permute-start | bytes 430088 | tf_op jit(solution)/shard_map/ppermute | solution.py:33
  17.0 12.5 %collective-permute-start.5 = (bf16[56,1280]{1,0:T(8,128)(2,1)S(1)}, bf16[56,1280]{1,0:T(8,128)(2,1)S(1)}, u32[]{:S(2)}, u32[]{:S(2)}) collective-permute-start(bf16[56,1280]{1,0:T(8,128)(2,1)S(1)} %fusion.1.refs_0_), channel_id=1, source_target_pairs={{0,16},{4,20},{8,24},{12,28},{16,0},{20,4},{24,8},{28,12},{1,17},{... | collective-permute-start | bytes 430088 | tf_op jit(solution)/shard_map/ppermute | solution.py:33
  20.2 9.3 %collective-permute-start.4 = (bf16[56,1280]{1,0:T(8,128)(2,1)S(1)}, bf16[56,1280]{1,0:T(8,128)(2,1)S(1)}, u32[]{:S(2)}, u32[]{:S(2)}) collective-permute-start(bf16[56,1280]{1,0:T(8,128)(2,1)S(1)} %fusion.1.refs_0_), channel_id=1, source_target_pairs={{0,12},{4,8},{8,4},{12,0},{16,28},{20,24},{24,20},{28,16},{1,13},{... | collective-permute-start | bytes 430088 | tf_op jit(solution)/shard_map/ppermute | solution.py:33
  20.7 10.4 %collective-permute-start.3 = (bf16[56,1280]{1,0:T(8,128)(2,1)S(1)}, bf16[56,1280]{1,0:T(8,128)(2,1)S(1)}, u32[]{:S(2)}, u32[]{:S(2)}) collective-permute-start(bf16[56,1280]{1,0:T(8,128)(2,1)S(1)} %fusion.1.refs_0_), channel_id=1, source_target_pairs={{0,8},{4,12},{8,0},{12,4},{16,24},{20,28},{24,16},{28,20},{1,9},{5... | collective-permute-start | bytes 430088 | tf_op jit(solution)/shard_map/ppermute | solution.py:33
  35.8 13.3 %collective-permute-start.11 = (bf16[480,256]{1,0:T(8,128)(2,1)S(1)}, bf16[480,256]{1,0:T(8,128)(2,1)S(1)}, u32[]{:S(2)}, u32[]{:S(2)}) collective-permute-start(bf16[480,256]{1,0:T(8,128)(2,1)S(1)} %get-tuple-element.13.refs_0_), channel_id=1, source_target_pairs={{0,3},{1,2},{2,1},{3,0},{4,7},{5,6},{6,5},{7,4},{8,11},{9,10},{10,... | collective-permute-start | bytes 737288 | tf_op jit(solution)/shard_map/ppermute | solution.py:33
  38.7 10.5 %collective-permute-start.10 = (bf16[480,256]{1,0:T(8,128)(2,1)S(1)}, bf16[480,256]{1,0:T(8,128)(2,1)S(1)}, u32[]{:S(2)}, u32[]{:S(2)}) collective-permute-start(bf16[480,256]{1,0:T(8,128)(2,1)S(1)} %get-tuple-element.13.refs_0_), channel_id=1, source_target_pairs={{0,2},{1,3},{2,0},{3,1},{4,6},{5,7},{6,4},{7,5},{8,10},{9,11},{10,... | collective-permute-start | bytes 737288 | tf_op jit(solution)/shard_map/ppermute | solution.py:33
  39.5 10.3 %collective-permute-start.9 = (bf16[480,256]{1,0:T(8,128)(2,1)S(1)}, bf16[480,256]{1,0:T(8,128)(2,1)S(1)}, u32[]{:S(2)}, u32[]{:S(2)}) collective-permute-start(bf16[480,256]{1,0:T(8,128)(2,1)S(1)} %get-tuple-element.13.refs_0_), channel_id=1, source_target_pairs={{0,1},{1,0},{2,3},{3,2},{4,5},{5,4},{6,7},{7,6},{8,9},{9,8},{10,11... | collective-permute-start | bytes 737288 | tf_op jit(solution)/shard_map/ppermute | solution.py:33
  40.0 9.8 %collective-permute-start.12 = (bf16[480,256]{1,0:T(8,128)(2,1)S(1)}, bf16[480,256]{1,0:T(8,128)(2,1)S(1)}, u32[]{:S(2)}, u32[]{:S(2)}) collective-permute-start(bf16[480,256]{1,0:T(8,128)(2,1)S(1)} %get-tuple-element.13.refs_0_), channel_id=1, source_target_pairs={{0,32},{32,0},{1,33},{33,1},{2,34},{34,2},{3,35},{35,3},{4,36},{36... | collective-permute-start | bytes 737288 | tf_op jit(solution)/shard_map/ppermute | solution.py:33
  53.8 19.8 %collective-permute-start.22 = (bf16[160,256]{1,0:T(8,128)(2,1)S(1)}, bf16[160,256]{1,0:T(8,128)(2,1)S(1)}, u32[]{:S(2)}, u32[]{:S(2)}) collective-permute-start(bf16[160,256]{1,0:T(8,128)(2,1)S(1)} %shard_map.121.refs_0_), channel_id=1, source_target_pairs={{0,28},{4,24},{8,20},{12,16},{16,12},{20,8},{24,4},{28,0},{1,29},{... | collective-permute-start | bytes 245768 | tf_op jit(solution)/shard_map/ppermute | solution.py:33
  54.8 21.4 %collective-permute-start.21 = (bf16[160,256]{1,0:T(8,128)(2,1)S(1)}, bf16[160,256]{1,0:T(8,128)(2,1)S(1)}, u32[]{:S(2)}, u32[]{:S(2)}) collective-permute-start(bf16[160,256]{1,0:T(8,128)(2,1)S(1)} %shard_map.121.refs_0_), channel_id=1, source_target_pairs={{0,24},{4,28},{8,16},{12,20},{16,8},{20,12},{24,0},{28,4},{1,25},{... | collective-permute-start | bytes 245768 | tf_op jit(solution)/shard_map/ppermute | solution.py:33
  57.8 19.0 %collective-permute-start.20 = (bf16[160,256]{1,0:T(8,128)(2,1)S(1)}, bf16[160,256]{1,0:T(8,128)(2,1)S(1)}, u32[]{:S(2)}, u32[]{:S(2)}) collective-permute-start(bf16[160,256]{1,0:T(8,128)(2,1)S(1)} %shard_map.121.refs_0_), channel_id=1, source_target_pairs={{0,20},{4,16},{8,28},{12,24},{16,4},{20,0},{24,12},{28,8},{1,21},{... | collective-permute-start | bytes 245768 | tf_op jit(solution)/shard_map/ppermute | solution.py:33
  67.4 19.2 %collective-permute-start.33 = (bf16[144,512]{1,0:T(8,128)(2,1)}, bf16[144,512]{1,0:T(8,128)(2,1)S(1)}, u32[]{:S(2)}, u32[]{:S(2)}) collective-permute-start(bf16[144,512]{1,0:T(8,128)(2,1)} %shard_map.119.query_ref), channel_id=1, source_target_pairs={{0,192},{64,128},{128,64},{192,0},{1,193},{65,129},{129,65},{193,1... | collective-permute-start | bytes 442376 | tf_op jit(solution)/shard_map/ppermute | solution.py:33
  72.4 7.5 %collective-permute-start.19 = (bf16[160,256]{1,0:T(8,128)(2,1)S(1)}, bf16[160,256]{1,0:T(8,128)(2,1)S(1)}, u32[]{:S(2)}, u32[]{:S(2)}) collective-permute-start(bf16[160,256]{1,0:T(8,128)(2,1)S(1)} %shard_map.121.refs_0_), channel_id=1, source_target_pairs={{0,16},{4,20},{8,24},{12,28},{16,0},{20,4},{24,8},{28,12},{1,17},{... | collective-permute-start | bytes 245768 | tf_op jit(solution)/shard_map/ppermute | solution.py:33
  73.6 6.9 %collective-permute-start.18 = (bf16[160,256]{1,0:T(8,128)(2,1)S(1)}, bf16[160,256]{1,0:T(8,128)(2,1)S(1)}, u32[]{:S(2)}, u32[]{:S(2)}) collective-permute-start(bf16[160,256]{1,0:T(8,128)(2,1)S(1)} %shard_map.121.refs_0_), channel_id=1, source_target_pairs={{0,12},{4,8},{8,4},{12,0},{16,28},{20,24},{24,20},{28,16},{1,13},{... | collective-permute-start | bytes 245768 | tf_op jit(solution)/shard_map/ppermute | solution.py:33
  82.4 9.1 %collective-permute-start.25 = (bf16[256,256]{1,0:T(8,128)(2,1)S(1)}, bf16[256,256]{1,0:T(8,128)(2,1)S(1)}, u32[]{:S(2)}, u32[]{:S(2)}) collective-permute-start(bf16[256,256]{1,0:T(8,128)(2,1)S(1)} %shard_map.123.refs_0_), channel_id=1, source_target_pairs={{0,3},{1,2},{2,1},{3,0},{4,7},{5,6},{6,5},{7,4},{8,11},{9,10},{10,... | collective-permute-start | bytes 393224 | tf_op jit(solution)/shard_map/ppermute | solution.py:33
  85.2 7.9 %collective-permute-start.24 = (bf16[256,256]{1,0:T(8,128)(2,1)S(1)}, bf16[256,256]{1,0:T(8,128)(2,1)S(1)}, u32[]{:S(2)}, u32[]{:S(2)}) collective-permute-start(bf16[256,256]{1,0:T(8,128)(2,1)S(1)} %shard_map.123.refs_0_), channel_id=1, source_target_pairs={{0,2},{1,3},{2,0},{3,1},{4,6},{5,7},{6,4},{7,5},{8,10},{9,11},{10,... | collective-permute-start | bytes 393224 | tf_op jit(solution)/shard_map/ppermute | solution.py:33
  85.9 7.2 %collective-permute-start.23 = (bf16[256,256]{1,0:T(8,128)(2,1)S(1)}, bf16[256,256]{1,0:T(8,128)(2,1)S(1)}, u32[]{:S(2)}, u32[]{:S(2)}) collective-permute-start(bf16[256,256]{1,0:T(8,128)(2,1)S(1)} %shard_map.123.refs_0_), channel_id=1, source_target_pairs={{0,1},{1,0},{2,3},{3,2},{4,5},{5,4},{6,7},{7,6},{8,9},{9,8},{10,11... | collective-permute-start | bytes 393224 | tf_op jit(solution)/shard_map/ppermute | solution.py:33
  86.6 12.9 %collective-permute-start.31 = (bf16[144,512]{1,0:T(8,128)(2,1)S(1)}, bf16[144,512]{1,0:T(8,128)(2,1)S(1)}, u32[]{:S(2)}, u32[]{:S(2)}) collective-permute-start(bf16[144,512]{1,0:T(8,128)(2,1)S(1)} %copy-done.3), channel_id=1, source_target_pairs={{0,64},{64,0},{128,192},{192,128},{1,65},{65,1},{129,193},{193,129... | collective-permute-start | bytes 442376 | tf_op jit(solution)/shard_map/ppermute | solution.py:33
  87.1 17.7 %collective-permute-start = (bf16[144,512]{1,0:T(8,128)(2,1)S(1)}, bf16[144,512]{1,0:T(8,128)(2,1)S(1)}, u32[]{:S(2)}, u32[]{:S(2)}) collective-permute-start(bf16[144,512]{1,0:T(8,128)(2,1)S(1)} %copy-done.3), channel_id=1, source_target_pairs={{0,128},{64,192},{128,0},{192,64},{1,129},{65,193},{129,1},{193,65... | collective-permute-start | bytes 442376 | tf_op jit(solution)/shard_map/ppermute | solution.py:33
  96.5 16.8 %collective-permute-start.34 = (bf16[128,512]{1,0:T(8,128)(2,1)S(1)}, bf16[128,512]{1,0:T(8,128)(2,1)S(1)}, u32[]{:S(2)}, u32[]{:S(2)}) collective-permute-start(bf16[128,512]{1,0:T(8,128)(2,1)S(1)} %shard_map.126), channel_id=1, source_target_pairs={{0,192},{64,128},{128,64},{192,0},{1,193},{65,129},{129,65},{193,1... | collective-permute-start | bytes 393224 | tf_op jit(solution)/shard_map/ppermute | solution.py:33
  101.3 12.2 %collective-permute-start.32 = (bf16[128,512]{1,0:T(8,128)(2,1)S(1)}, bf16[128,512]{1,0:T(8,128)(2,1)S(1)}, u32[]{:S(2)}, u32[]{:S(2)}) collective-permute-start(bf16[128,512]{1,0:T(8,128)(2,1)S(1)} %shard_map.125), channel_id=1, source_target_pairs={{0,64},{64,0},{128,192},{192,128},{1,65},{65,1},{129,193},{193,129... | collective-permute-start | bytes 393224 | tf_op jit(solution)/shard_map/ppermute | solution.py:33
  106.7 12.6 %collective-permute-start.30 = (bf16[128,512]{1,0:T(8,128)(2,1)S(1)}, bf16[128,512]{1,0:T(8,128)(2,1)S(1)}, u32[]{:S(2)}, u32[]{:S(2)}) collective-permute-start(bf16[128,512]{1,0:T(8,128)(2,1)S(1)} %shard_map.124), channel_id=1, source_target_pairs={{0,128},{64,192},{128,0},{192,64},{1,129},{65,193},{129,1},{193,65... | collective-permute-start | bytes 393224 | tf_op jit(solution)/shard_map/ppermute | solution.py:33
  (16 other events, 66.8 us)
